TPU v7x, 32 devices: a whole 2x2x4 slice. The times are simulated.
32 devices in a mesh: seq: 8 (over z, core), tp: 4 (over y, x).
Axes of the slice: x: 2, y: 2, z: 4, core: 2. Of those that a mesh axis runs over, the one named last changes fastest.
Arguments:
- qkv: bfloat16 [3, 4, 128, 3072], P(None, None, ('seq', 'tp')), may hold values from -6 to 6
- positions: int32 [3, 4, 128], P(None, None, ('seq', 'tp')), may hold values from 0 to 31, as said below
- w_proj: bfloat16 [3072, 64], replicated, may hold values from -0.21875 to 0.21875
- latents: bfloat16 [4, 128, 64], P(None, 'seq'), may hold values from -6 to 6
- embed_w: bfloat16 [64, 2048], replicated, may hold values from -0.75 to 0.75
- up_w: bfloat16 [2048, 8192], P(None, 'tp'), may hold values from -0.125 to 0.125
- down_w: bfloat16 [8192, 2048], P('tp'), may hold values from -0.0625 to 0.0625
- head_w: bfloat16 [2048, 1000], P(('seq', 'tp')), may hold values from -3 to 3
- labels: int32 [4], replicated, may hold values from 0 to 999
- timesteps: int32 [4], replicated, may hold values from 0 to 999
Outputs:
- guided: bfloat16 [4, 128, 64], P(None, ('seq', 'tp'))
Inputs may be any that keep to these rules, and one draw needn't show every extreme that they name: For each video the tokens are the cells of a stack of frames of 32 x 32 cells, each cell once, in shuffled order; positions[0] is the frame, positions[1] the row, positions[2] the column.
All inputs are finite; a program needn't handle non-finite values.
Results may differ from a plain program's by a relative error of at most 0.0095.
Values may be sent and summed in bfloat16 or wider, within the bound.
No kernel may reach another device: no remote copies, remote signals or barrier semaphores. Data moves between devices by JAX's collectives and lax.ppermute only.
A program may use at most 64 MiB of HBM per device.

v0:
```python
import jax
import jax.numpy as jnp
from jax import lax
from jax.sharding import PartitionSpec as P

HEADS = 24
HEAD_DIM = 128


GUIDANCE = 0.1


def rope_angles(positions, head_dim):
    frame_width = head_dim // 8
    plane_width = (head_dim - frame_width) // 2
    pieces = []
    for axis, width in zip(range(3), (frame_width, plane_width, plane_width)):
        freqs = 10000.0 ** (-jnp.arange(0, width, 2, dtype=jnp.float32) / width)
        pieces.append(positions[axis][..., None] * freqs)
    return jnp.concatenate(pieces, axis=-1)


def rotate(values, angles):
    half = values.shape[-1] // 2
    floats = values.astype(jnp.float32)
    first = floats[..., :half]
    second = floats[..., half:]
    cosine = jnp.cos(angles)[:, :, None, :]
    sine = jnp.sin(angles)[:, :, None, :]
    turned = jnp.concatenate(
        [first * cosine - second * sine, first * sine + second * cosine], axis=-1
    )
    return turned.astype(jnp.bfloat16)


def gelu_slope(values):
    cdf = 0.5 * (1.0 + jax.scipy.special.erf(values * 0.7071067811865476))
    pdf = jnp.exp(-0.5 * values * values) * 0.3989422804014327
    return cdf + values * pdf


def pairs_first(array):
    samples, tokens = (array.shape[0], array.shape[1])
    return array.transpose(0, 2, 1, 3).reshape(samples * HEADS, tokens, HEAD_DIM)


def per_device(qkv, positions, w_proj, latents, embed_w, up_w, down_w, head_w, labels, timesteps):
    samples, tok_dev = (qkv.shape[1], qkv.shape[2])
    angles = rope_angles(positions.astype(jnp.float32), HEAD_DIM)
    shaped = (samples, tok_dev, HEADS, HEAD_DIM)
    queries = rotate(qkv[0].reshape(shaped), angles)
    keys_tok = rotate(qkv[1].reshape(shaped), angles)
    values_tok = qkv[2].reshape(shaped)
    moved = lax.all_to_all(
        jnp.stack([pairs_first(queries), pairs_first(keys_tok), pairs_first(values_tok)]),
        "seq",
        split_axis=1,
        concat_axis=2,
        tiled=True,
    )
    query_pairs = moved[0]
    pair_count, query_count = (query_pairs.shape[0], query_pairs.shape[1])
    running = jnp.full((pair_count, query_count), -jnp.inf, jnp.float32)
    total = jnp.zeros((pair_count, query_count), jnp.float32)
    accum = jnp.zeros((pair_count, query_count, HEAD_DIM), jnp.float32)
    key_piece = lax.all_gather(moved[1], "tp", axis=1, tiled=True)
    value_piece = lax.all_gather(moved[2], "tp", axis=1, tiled=True)
    scores = jnp.einsum(
        "iqd,ikd->iqk", query_pairs, key_piece, preferred_element_type=jnp.float32
    ) * HEAD_DIM ** (-0.5)
    newest = jnp.max(scores, axis=-1)
    factor = jnp.exp(running - newest)
    weights = jnp.exp(scores - newest[..., None])
    total = total * factor + jnp.sum(weights, axis=-1)
    accum = accum * factor[..., None] + jnp.einsum(
        "iqk,ikd->iqd",
        weights.astype(jnp.bfloat16),
        value_piece,
        preferred_element_type=jnp.float32,
    )
    running, total, accum = (newest, total, accum)
    attended = (accum / total[..., None]).astype(jnp.bfloat16)
    returned = lax.all_to_all(attended, "seq", split_axis=1, concat_axis=0, tiled=True)
    returned = returned.reshape(samples, HEADS, tok_dev, HEAD_DIM).transpose(0, 2, 1, 3)
    returned = returned.reshape(samples, tok_dev, HEADS * HEAD_DIM)
    eps = jnp.dot(returned, w_proj, preferred_element_type=jnp.float32)
    seq_len = latents.shape[1] * lax.axis_size("seq")
    tp_index = lax.axis_index("tp")
    emb = jnp.dot(latents, embed_w, preferred_element_type=jnp.float32).astype(jnp.bfloat16)
    hidden = jnp.dot(emb, up_w, preferred_element_type=jnp.float32)
    act = jax.nn.gelu(hidden, approximate=False).astype(jnp.bfloat16)
    branch = jnp.dot(act, down_w, preferred_element_type=jnp.float32)
    own_emb = lax.dynamic_slice_in_dim(emb, tp_index * tok_dev, tok_dev, 1).astype(jnp.float32)
    partial_pool = jnp.sum(branch, axis=1) + jnp.sum(own_emb, axis=1)
    head_rows = head_w.shape[0]
    flat_index = lax.axis_index("seq") * lax.axis_size("tp") + tp_index
    pooled = lax.psum(partial_pool, ("seq", "tp")) / seq_len
    pooled_share = lax.dynamic_slice_in_dim(pooled, flat_index * head_rows, head_rows, 1)
    head_float = head_w.astype(jnp.float32)
    logit_terms = jnp.dot(pooled_share, head_float, precision=lax.Precision.HIGHEST)
    logits = lax.psum(logit_terms, ("seq", "tp"))
    probs = jax.nn.softmax(logits, axis=-1)
    onehot = (labels[:, None] == jnp.arange(logits.shape[1], dtype=jnp.int32)[None, :]).astype(
        jnp.float32
    )
    grad_share = jnp.dot(onehot - probs, head_float.T, precision=lax.Precision.HIGHEST)
    dpool = lax.all_gather(grad_share, ("seq", "tp"), axis=1, tiled=True)
    dact = jnp.dot(dpool, down_w.astype(jnp.float32).T, precision=lax.Precision.HIGHEST)
    dh1 = (gelu_slope(hidden) * dact[:, None, :]).astype(jnp.bfloat16)
    demb = jnp.einsum("btf,cf->btc", dh1, up_w, preferred_element_type=jnp.float32)
    embed_float = embed_w.astype(jnp.float32)
    dx_terms = jnp.einsum("btc,lc->btl", demb, embed_float, precision=lax.Precision.HIGHEST)
    dx_mine = lax.psum_scatter(
        dx_terms.astype(jnp.bfloat16), "tp", scatter_dimension=1, tiled=True
    ).astype(jnp.float32)
    dx_pool = jnp.dot(dpool, embed_float.T, precision=lax.Precision.HIGHEST)
    dx_total = dx_mine + dx_pool[:, None, :]
    phase = (timesteps.astype(jnp.float32) / 1000.0 + 0.008) / 1.008 * (jnp.pi / 2)
    abar = jnp.cos(phase) ** 2
    scale = GUIDANCE * jnp.sqrt(1.0 - abar)
    return (eps - scale[:, None, None] * dx_total).astype(jnp.bfloat16)


def solution(mesh):
    placed = (
        P(None, None, ("seq", "tp"), None),
        P(None, None, ("seq", "tp")),
        P(),
        P(None, "seq", None),
        P(),
        P(None, "tp"),
        P("tp", None),
        P(("seq", "tp"), None),
        P(),
        P(),
    )
    return jax.shard_map(
        per_device,
        mesh=mesh,
        in_specs=placed,
        out_specs=P(None, ("seq", "tp"), None),
        check_vma=False,
    )
```

profile of v0, /device:TPU:0, one launch (start us, length us, event | category | flops | bytes accessed | tf_op | source)
XLA Modules:
  0.0 233.0 jit_solution(14291918177690481106)
XLA Ops:
  0.0 1.1 slice_convert_fusion.1
  1.4 0.7 convert_element_type.55
  3.2 0.9 copy.29
  4.1 6.4 %all-to-all-start = ((bf16[3,96,4,128]{3,2,0,1:T(4,128)(2,1)}), bf16[3,96,4,128]{3,2,0,1:T(4,128)(2,1)S(1)}, u32[]{:S(2)}, u32[]{:S(2)}) async-start(bf16[3,96,4,128]{3,2,0,1:T(4,128)(2,1)} %copy.29), calls=%async_computation | async-start | bytes 589824 | tf_op jit(solution)/shard_map/all_to_all | solution.py:54
  10.4 1.2 convolution_convert_fusion
  11.6 5.1 %fusion.72 = (u8[16,2048]{1,0:T(8,128)(4,1)S(1)}, u8[16,2048]{1,0:T(8,128)(4,1)S(1)}, f32[4,16,2048]{2,1,0:T(8,128)S(1)}) fusion(bf16[4,16,2048]{2,1,0:T(8,128)(2,1)S(1)} %convolution_convert_fusion, bf16[2048,2048]{1,0:T(8,128)(2,1)} %param.15), kind=kOutput, calls=%fused_computation.95 | convolution fusion | flops 538509312 | bytes 9240576 | tf_op jit(solution)/shard_map/dot_general | solution.py:90
  16.8 6.0 %fusion.6 = f32[4,2048]{1,0:T(4,128)S(1)} fusion(bf16[2048,2048]{1,0:T(8,128)(2,1)} %param.16, f32[4,16,2048]{2,1,0:T(8,128)S(1)} %get-tuple-element.34, u8[16,2048]{1,0:T(8,128)(4,1)S(1)} %get-tuple-element.6, u8[16,2048]{1,0:T(8,128)(4,1)S(1)} %get-tuple-element.5), kind=kOutput, calls=%fused_computation.7 | convolution fusion | flops 546168832 | bytes 9011200 | tf_op jit(solution)/shard_map/dot_general | solution.py:92
  22.8 40.9 %psum.14 = f32[4,2048]{1,0:T(4,128)S(1)} all-reduce(f32[4,2048]{1,0:T(4,128)S(1)} %add.59), channel_id=1, replica_groups=mesh['seq'=8,'tp'=4] {'seq','tp'}, use_global_device_ids=true, to_apply=%region_4.0 | all-reduce | flops 8192 | bytes 65536 | tf_op jit(solution)/shard_map/psum | solution.py:97
  64.0 40.0 %psum.15 = f32[4,1000]{1,0:T(4,128)S(1)} all-reduce(f32[4,1000]{1,0:T(4,128)S(1)} %fusion.82), channel_id=1, replica_groups=mesh['seq'=8,'tp'=4] {'seq','tp'}, use_global_device_ids=true, to_apply=%region_5.0 | all-reduce | flops 4000 | bytes 32000 | tf_op jit(solution)/shard_map/psum | solution.py:101
  104.6 66.3 %all-gather = f32[32,64,4]{1,2,0:T(4,128)S(1)} all-gather(f32[1,64,4]{1,2,0:T(4,128)S(1)} %convolution_bitcast_fusion), channel_id=1, replica_groups=mesh['seq'=8,'tp'=4] {'seq','tp'}, dimensions={0}, use_global_device_ids=true | all-gather | bytes 33792 | tf_op jit(solution)/shard_map/all_gather | solution.py:107
  171.0 8.9 %fusion.129 = f32[4,2048]{1,0:T(4,128)S(1)} fusion(f32[2048,4]{0,1:T(4,128)S(1)} %reshape.88, bf16[2048,2048]{1,0:T(8,128)(2,1)} %param.16), kind=kOutput, calls=%fused_computation.170 | convolution fusion | flops 201326592 | bytes 8454144 | tf_op jit(solution)/shard_map/dot_general | solution.py:108
  179.9 6.1 %fusion.2 = f32[4,16,2048]{2,1,0:T(8,128)S(1)} fusion(bf16[2048,2048]{1,0:T(8,128)(2,1)} %param.15, f32[4,16,2048]{2,1,0:T(8,128)S(1)} %get-tuple-element.34, f32[4,2048]{1,0:T(4,128)S(1)} %fusion.129), kind=kOutput, calls=%fused_computation.2 | convolution fusion | flops 538181632 | bytes 9469952 | tf_op jit(solution)/shard_map/btf,cf->btc/dot_general | solution.py:110
  186.0 0.6 dynamic-slice
  187.3 0.4 convolution_convert_fusion.1
  187.7 13.9 %all-reduce = bf16[4,16,64]{2,1,0:T(8,128)(2,1)S(1)} all-reduce(bf16[4,16,64]{2,1,0:T(8,128)(2,1)S(1)} %convolution_convert_fusion.1), channel_id=2, replica_groups=mesh['seq'=8,'tp'=4] {'tp'}, use_global_device_ids=true, to_apply=%region_8.0.clone | all-reduce | flops 4096 | bytes 16384
  201.5 0.3 fusion.130
  202.1 8.9 %all_gather.10 = bf16[12,128,128]{2,1,0:T(8,128)(2,1)S(1)} all-gather(bf16[12,32,128]{2,1,0:T(8,128)(2,1)S(1)} %bitcast.77), channel_id=1, replica_groups=mesh['seq'=8,'tp'=4] {'tp'}, dimensions={1}, use_global_device_ids=true | all-gather | bytes 491520 | tf_op jit(solution)/shard_map/all_gather | solution.py:67
  211.1 9.3 %all_gather.9 = bf16[12,128,128]{2,1,0:T(8,128)(2,1)S(1)} all-gather(bf16[12,32,128]{2,1,0:T(8,128)(2,1)S(1)} %bitcast.78), channel_id=1, replica_groups=mesh['seq'=8,'tp'=4] {'tp'}, dimensions={1}, use_global_device_ids=true | all-gather | bytes 491520 | tf_op jit(solution)/shard_map/all_gather | solution.py:66
  220.4 0.4 fusion.128
  221.1 0.3 fusion.10
  221.4 0.7 copy.34
  222.1 3.4 %all-to-all-start.1 = ((bf16[12,32,128]{2,0,1:T(8,128)(2,1)}), bf16[12,32,128]{2,0,1:T(8,128)(2,1)S(1)}, u32[]{:S(2)}, u32[]{:S(2)}) async-start(bf16[12,32,128]{2,0,1:T(8,128)(2,1)} %copy.34), calls=%async_computation.1 | async-start | bytes 262144 | tf_op jit(solution)/shard_map/all_to_all | solution.py:83
  225.5 6.6 %all-to-all-done.1 = bf16[12,32,128]{2,0,1:T(8,128)(2,1)S(1)} async-done(((bf16[12,32,128]{2,0,1:T(8,128)(2,1)}), bf16[12,32,128]{2,0,1:T(8,128)(2,1)S(1)}, u32[]{:S(2)}, u32[]{:S(2)}) %all-to-all-start.1) | async-done | bytes 98336 | tf_op jit(solution)/shard_map/all_to_all | solution.py:83
  232.2 0.8 fusion.11
  (48 shorter events, 3.0 us)
Async XLA Ops:
  0.0 232.2 %copy-start = (bf16[3072,64]{0,1:T(8,128)(2,1)S(1)}, bf16[3072,64]{0,1:T(8,128)(2,1)}, u32[]{:S(2)}) copy-start(bf16[3072,64]{0,1:T(8,128)(2,1)} %param.12) | copy-start | bytes 1179652
  4.1 197.8 %all-to-all-start = ((bf16[3,96,4,128]{3,2,0,1:T(4,128)(2,1)}), bf16[3,96,4,128]{3,2,0,1:T(4,128)(2,1)S(1)}, u32[]{:S(2)}, u32[]{:S(2)}) async-start(bf16[3,96,4,128]{3,2,0,1:T(4,128)(2,1)} %copy.29), calls=%async_computation | async-start | bytes 589824 | tf_op jit(solution)/shard_map/all_to_all | solution.py:54
  16.8 47.0 %copy-start.2 = (bf16[64,1000]{1,0:T(8,128)(2,1)S(1)}, bf16[64,1000]{1,0:T(8,128)(2,1)}, u32[]{:S(2)}) copy-start(bf16[64,1000]{1,0:T(8,128)(2,1)} %param.17) | copy-start | bytes 384004
  16.8 87.6 %copy-start.3 = (s32[4]{0:T(128)S(1)}, s32[4]{0:T(128)}, u32[]{:S(2)}) copy-start(s32[4]{0:T(128)} %param.18) | copy-start | bytes 52
  179.9 6.1 %copy-start.5 = (u32[32]{0:T(128)S(1)}, u32[32]{0:T(128)}, u32[]{:S(2)}) copy-start(u32[32]{0:T(128)} %constant.123) | copy-start | bytes 388
  179.9 7.4 %copy-start.1 = (bf16[64,2048]{1,0:T(8,128)(2,1)S(1)}, bf16[64,2048]{1,0:T(8,128)(2,1)}, u32[]{:S(2)}) copy-start(bf16[64,2048]{1,0:T(8,128)(2,1)} %param.14) | copy-start | bytes 786436
  179.9 45.5 %copy-start.4 = (s32[4]{0:T(128)S(1)}, s32[4]{0:T(128)}, u32[]{:S(2)}) copy-start(s32[4]{0:T(128)} %param.19) | copy-start | bytes 52
  222.1 10.1 %all-to-all-start.1 = ((bf16[12,32,128]{2,0,1:T(8,128)(2,1)}), bf16[12,32,128]{2,0,1:T(8,128)(2,1)S(1)}, u32[]{:S(2)}, u32[]{:S(2)}) async-start(bf16[12,32,128]{2,0,1:T(8,128)(2,1)} %copy.34), calls=%async_computation.1 | async-start | bytes 262144 | tf_op jit(solution)/shard_map/all_to_all | solution.py:83
where the time goes:
time: 234 us; the launch traced here: 233 us
  blocking collectives  179 us (76%)
  matrix products  29.8 us (13%)
  starting transfers between devices  9.72 us (4%)
  waiting for transfers between devices  6.62 us (3%)
  local copies, waits for them, and re-layouts  3.35 us (1%)
  other arithmetic  3.16 us (1%)
    all_gather x1, blocking collectives, per_device(): dpool = lax.all_gather(grad_share, ('seq', 'tp'), axis=1, tiled=True)  66.3 us
    psum x1, blocking collectives, per_device(): pooled = lax.psum(partial_pool, ('seq', 'tp')) / seq_len  40.9 us
    psum x1, blocking collectives, per_device(): logits = lax.psum(logit_terms, ('seq', 'tp'))  40 us
    unnamed x1, blocking collectives  13.9 us
    all_gather x1, blocking collectives, per_device(): key_piece = lax.all_gather(moved[1], 'tp', axis=1, tiled=True)  9.33 us
    all_gather x1, blocking collectives, per_device(): value_piece = lax.all_gather(moved[2], 'tp', axis=1, tiled=True)  8.92 us
    dot_general x1, matrix products, per_device(): jnp.dot(dpool, down_w.astype(jnp.float32).T, precision=lax.Precision.HIGH...  8.9 us
    all_to_all x1, waiting for transfers between devices, per_device(): lax.all_to_all(attended, 'seq', split_axis=1, concat_axis=0, tiled=True)  6.62 us
  transfers between devices with their start and end apart: 2, of which 1 were waited for; matrix products, arithmetic and copies ran while one was open for 13% of the time, Pallas kernels for 0%

commit v1 on v0

--- a/solution.py
+++ b/solution.py
@@ -3,7 +3,6 @@
 from jax import lax
 from jax.sharding import PartitionSpec as P
 
-HEADS = 24
 HEAD_DIM = 128
 
 
@@ -41,13 +40,14 @@
 
 def pairs_first(array):
     samples, tokens = (array.shape[0], array.shape[1])
-    return array.transpose(0, 2, 1, 3).reshape(samples * HEADS, tokens, HEAD_DIM)
-
-
-def per_device(qkv, positions, w_proj, latents, embed_w, up_w, down_w, head_w, labels, timesteps):
+    return array.transpose(0, 2, 1, 3).reshape(samples * array.shape[2], tokens, HEAD_DIM)
+
+
+def per_device_general(qkv, positions, w_proj, latents, embed_w, up_w, down_w, head_w, labels, timesteps):
     samples, tok_dev = (qkv.shape[1], qkv.shape[2])
     angles = rope_angles(positions.astype(jnp.float32), HEAD_DIM)
-    shaped = (samples, tok_dev, HEADS, HEAD_DIM)
+    heads = qkv.shape[3] // HEAD_DIM
+    shaped = (samples, tok_dev, heads, HEAD_DIM)
     queries = rotate(qkv[0].reshape(shaped), angles)
     keys_tok = rotate(qkv[1].reshape(shaped), angles)
     values_tok = qkv[2].reshape(shaped)
@@ -81,8 +81,8 @@
     running, total, accum = (newest, total, accum)
     attended = (accum / total[..., None]).astype(jnp.bfloat16)
     returned = lax.all_to_all(attended, "seq", split_axis=1, concat_axis=0, tiled=True)
-    returned = returned.reshape(samples, HEADS, tok_dev, HEAD_DIM).transpose(0, 2, 1, 3)
-    returned = returned.reshape(samples, tok_dev, HEADS * HEAD_DIM)
+    returned = returned.reshape(samples, heads, tok_dev, HEAD_DIM).transpose(0, 2, 1, 3)
+    returned = returned.reshape(samples, tok_dev, qkv.shape[3])
     eps = jnp.dot(returned, w_proj, preferred_element_type=jnp.float32)
     seq_len = latents.shape[1] * lax.axis_size("seq")
     tp_index = lax.axis_index("tp")
@@ -121,6 +121,138 @@
     return (eps - scale[:, None, None] * dx_total).astype(jnp.bfloat16)
 
 
+def split_rows(values):
+    high = values.astype(jnp.bfloat16)
+    rest = values - high.astype(jnp.float32)
+    middle = rest.astype(jnp.bfloat16)
+    low = (rest - middle.astype(jnp.float32)).astype(jnp.bfloat16)
+    return jnp.concatenate([high, middle, low], axis=0)
+
+
+def split_dot(values, weights, contract=0):
+    rows = values.shape[0]
+    product = lax.dot_general(
+        split_rows(values),
+        weights,
+        (((1,), (contract,)), ((), ())),
+        preferred_element_type=jnp.float32,
+    )
+    return product[:rows] + product[rows : 2 * rows] + product[2 * rows :]
+
+
+def per_device_fast(qkv, positions, w_proj, latents, embed_w, up_w, down_w, head_w, labels, timesteps):
+    both = ("seq", "tp")
+    n_seq, n_tp = (lax.axis_size("seq"), lax.axis_size("tp"))
+    count = n_seq * n_tp
+    seq_index, tp_index = (lax.axis_index("seq"), lax.axis_index("tp"))
+    flat_index = seq_index * n_tp + tp_index
+    samples, tok_dev, width = qkv.shape[1:]
+    seq_len = tok_dev * count
+    lat = latents.shape[2]
+    heads = width // HEAD_DIM
+    per_sample = count // samples
+    heads_dev = heads // per_sample
+    chunk = heads_dev * HEAD_DIM
+
+    lat_all = lax.all_to_all(
+        jnp.broadcast_to(latents[None], (n_seq,) + latents.shape), "seq", 0, 0, tiled=True
+    )
+    lat_all = lat_all.transpose(1, 0, 2, 3).reshape(samples * seq_len, lat)
+
+    angles = rope_angles(positions.astype(jnp.float32), HEAD_DIM)
+    shaped = (samples, tok_dev, heads, HEAD_DIM)
+    queries = rotate(qkv[0].reshape(shaped), angles).reshape(samples, tok_dev, width)
+    keys = rotate(qkv[1].reshape(shaped), angles).reshape(samples, tok_dev, width)
+    packed = jnp.stack([queries, keys, qkv[2]])
+    packed = packed.reshape(3, samples, tok_dev, per_sample, chunk).transpose(1, 3, 0, 2, 4)
+    packed = packed.reshape(count, 3, tok_dev, chunk)
+    moved = lax.all_to_all(packed, both, 0, 0, tiled=True)
+
+    units = up_w.shape[1] // n_seq
+    up_mine = lax.dynamic_slice_in_dim(up_w, seq_index * units, units, 1)
+    down_mine = lax.dynamic_slice_in_dim(down_w, seq_index * units, units, 0)
+    joint = jnp.dot(embed_w, up_mine, preferred_element_type=jnp.float32)
+    joint_high = joint.astype(jnp.bfloat16)
+    joint_low = (joint - joint_high.astype(jnp.float32)).astype(jnp.bfloat16)
+    hidden = jnp.dot(lat_all, joint_high, preferred_element_type=jnp.float32) + jnp.dot(
+        lat_all, joint_low, preferred_element_type=jnp.float32
+    )
+    act = jax.nn.gelu(hidden, approximate=False)
+    act_sum = jnp.sum(act.reshape(samples, seq_len, units), axis=1)
+    pool_terms = split_dot(act_sum, down_mine)
+    rows_dev = head_w.shape[0]
+    pool_terms = pool_terms.reshape(samples, count, rows_dev).transpose(1, 0, 2)
+    pool_terms = lax.all_to_all(pool_terms, both, 0, 0, tiled=True)
+    lat_sum = jnp.sum(lat_all.astype(jnp.float32).reshape(samples, seq_len, lat), axis=1)
+    embed_mine = lax.dynamic_slice_in_dim(embed_w, flat_index * rows_dev, rows_dev, 1)
+    pooled = (jnp.sum(pool_terms, axis=0) + split_dot(lat_sum, embed_mine)) / seq_len
+
+    def head_view(index):
+        return moved[:, index].reshape(seq_len, heads_dev, HEAD_DIM)
+
+    scores = jnp.einsum(
+        "qhd,khd->hqk", head_view(0), head_view(1), preferred_element_type=jnp.float32
+    ) * HEAD_DIM ** (-0.5)
+    weights = jnp.exp(scores - jnp.max(scores, axis=-1, keepdims=True))
+    total = jnp.sum(weights, axis=-1)
+    mixed = jnp.einsum(
+        "hqk,khd->hqd",
+        weights.astype(jnp.bfloat16),
+        head_view(2),
+        preferred_element_type=jnp.float32,
+    )
+    attended = (mixed / total[..., None]).astype(jnp.bfloat16)
+    attended = attended.transpose(1, 0, 2).reshape(count, tok_dev, chunk)
+    returned = lax.all_to_all(attended, both, 0, 0, tiled=True)
+    returned = returned.reshape(samples, per_sample, tok_dev, chunk).transpose(0, 2, 1, 3)
+    eps = jnp.dot(
+        returned.reshape(samples, tok_dev, width), w_proj, preferred_element_type=jnp.float32
+    )
+
+    classes = head_w.shape[1]
+    padded = -(-classes // (128 * n_tp)) * (128 * n_tp)
+    terms = split_dot(pooled, head_w)
+    terms = lax.all_to_all(
+        jnp.broadcast_to(terms[None], (count,) + terms.shape), both, 0, 0, tiled=True
+    )
+    logits = jnp.sum(terms, axis=0)
+    probs = jax.nn.softmax(logits, axis=-1)
+    onehot = (labels[:, None] == jnp.arange(classes, dtype=jnp.int32)[None, :]).astype(jnp.float32)
+    share = split_dot(onehot - probs, head_w, 1)
+    dpool = lax.all_to_all(
+        jnp.broadcast_to(share[None], (count,) + share.shape), both, 0, 0, tiled=True
+    )
+    dpool = dpool.transpose(1, 0, 2).reshape(samples, count * rows_dev)
+
+    dact = split_dot(dpool, down_mine, 1)
+    slope = gelu_slope(hidden).reshape(samples, seq_len, units)
+    dh1 = (slope * dact[:, None, :]).astype(jnp.bfloat16).reshape(samples * seq_len, units)
+    dx_terms = lax.dot_general(
+        dh1, joint_high, (((1,), (1,)), ((), ())), preferred_element_type=jnp.float32
+    ) + lax.dot_general(
+        dh1, joint_low, (((1,), (1,)), ((), ())), preferred_element_type=jnp.float32
+    )
+    dx_terms = dx_terms.astype(jnp.bfloat16).reshape(samples, count, tok_dev, lat)
+    dx_terms = lax.all_to_all(dx_terms.transpose(1, 0, 2, 3), both, 0, 0, tiled=True)
+    dx = jnp.sum(dx_terms.astype(jnp.float32), axis=0)
+    dx = dx + split_dot(dpool, embed_w, 1)[:, None, :]
+    phase = (timesteps.astype(jnp.float32) / 1000.0 + 0.008) / 1.008 * (jnp.pi / 2)
+    abar = jnp.cos(phase) ** 2
+    scale = GUIDANCE * jnp.sqrt(1.0 - abar)
+    return (eps - scale[:, None, None] * dx).astype(jnp.bfloat16)
+
+
+def per_device(qkv, positions, w_proj, latents, embed_w, up_w, down_w, head_w, labels, timesteps):
+    args = (qkv, positions, w_proj, latents, embed_w, up_w, down_w, head_w, labels, timesteps)
+    n_seq = lax.axis_size("seq")
+    count = n_seq * lax.axis_size("tp")
+    samples, heads = (qkv.shape[1], qkv.shape[3] // HEAD_DIM)
+    even = count % samples == 0 and heads % max(1, count // samples) == 0
+    if even and up_w.shape[1] % (128 * n_seq) == 0:
+        return per_device_fast(*args)
+    return per_device_general(*args)
+
+
 def solution(mesh):
     placed = (
         P(None, None, ("seq", "tp"), None),

time: 234 us -> 103 us (0.44)
  blocking collectives: 179 us -> 0 us
  waiting for transfers between devices: 6.62 us -> 53.1 us
  matrix products: 29.8 us -> 8.73 us
  starting transfers between devices: 9.72 us -> 25.1 us
  local copies, waits for them, and re-layouts: 3.35 us -> 9.61 us
    all_gather x3 -> x0, blocking collectives: 84.6 us -> none  [the longest x1 66.3 us: per_device(): dpool = lax.all_gather(grad_share, ('seq', 'tp'), axis=1, tiled=True)]
    psum x2 -> x0, blocking collectives: 81 us -> none  [the longest x1 40.9 us: per_device(): pooled = lax.psum(partial_pool, ('seq', 'tp')) / seq_len]
    all_to_all x2 -> x7, waiting for transfers between devices: 6.62 us -> 53.1 us  [the longest x1 14.7 us: per_device_fast(): lax.all_to_all(jnp.broadcast_to(terms[None], (count,) + terms.shape), bot...]
    dot_general x12 -> x14, matrix products: 29.8 us -> 8.73 us  [the longest x6 3.76 us: split_dot(): lax.dot_general(split_rows(values), weights, (((1,), (contract,)), ((), (...]
    all_to_all x2 -> x7, starting transfers between devices: 9.72 us -> 25.1 us  [the longest x1 6.35 us: per_device_fast(): lax.all_to_all(jnp.broadcast_to(latents[None], (n_seq,) + latents.shape),...]
    unnamed x1 -> x0, blocking collectives: 13.9 us -> none
    unnamed x14 -> x18, local copies, waits for them, and re-layouts: 0.71 us -> 3.46 us
  transfers between devices with their start and end apart: 2 -> 7, of which waited for: 1 -> 7; matrix products, arithmetic and copies ran while one was open for 13% -> 10% of each run, Pallas kernels for 0% -> 0%
where the time goes in v1:
time: 103 us; the launch traced here: 102 us
  waiting for transfers between devices  53.1 us (52%)
  starting transfers between devices  25.1 us (24%)
  local copies, waits for them, and re-layouts  9.61 us (9%)
  matrix products  8.73 us (8%)
  other arithmetic  5.25 us (5%)
    all_to_all x1, waiting for transfers between devices, per_device_fast(): lax.all_to_all(jnp.broadcast_to(terms[None], (count,) + terms.shape), bot...  14.7 us
    all_to_all x1, waiting for transfers between devices, per_device_fast(): moved = lax.all_to_all(packed, both, 0, 0, tiled=True)  10 us
    all_to_all x1, waiting for transfers between devices, per_device_fast(): lax.all_to_all(dx_terms.transpose(1, 0, 2, 3), both, 0, 0, tiled=True)  7.48 us
    all_to_all x1, waiting for transfers between devices, per_device_fast(): lax.all_to_all(jnp.broadcast_to(share[None], (count,) + share.shape), bot...  7.18 us
    all_to_all x1, waiting for transfers between devices, per_device_fast(): pool_terms = lax.all_to_all(pool_terms, both, 0, 0, tiled=True)  7.09 us
    all_to_all x1, waiting for transfers between devices, per_device_fast(): returned = lax.all_to_all(attended, both, 0, 0, tiled=True)  6.49 us
    all_to_all x1, starting transfers between devices, per_device_fast(): lax.all_to_all(jnp.broadcast_to(latents[None], (n_seq,) + latents.shape),...  6.35 us
    all_to_all x1, starting transfers between devices, per_device_fast(): pool_terms = lax.all_to_all(pool_terms, both, 0, 0, tiled=True)  5.9 us
  transfers between devices with their start and end apart: 7, of which 7 were waited for; matrix products, arithmetic and copies ran while one was open for 10% of the time, Pallas kernels for 0%

profile of v1, /device:TPU:0, one launch (start us, length us, event | category | flops | bytes accessed | tf_op | source)
XLA Modules:
  0.0 102.3 jit_solution(8537353494464722491)
XLA Ops:
  0.0 0.8 broadcast_in_dim.6
  0.8 0.8 reshape.138
  1.6 6.4 %all-to-all-start.2 = ((bf16[8,2,2048]{2,1,0:T(2,128)(2,1)}), bf16[8,2,2048]{2,1,0:T(2,128)(2,1)S(1)}, u32[]{:S(2)}, u32[]{:S(2)}) async-start(bf16[8,2,2048]{2,1,0:T(2,128)(2,1)} %reshape.138), calls=%async_computation.2 | async-start | bytes 131072 | tf_op jit(solution)/shard_map/all_to_all | solution.py:157
  8.9 1.0 %slice_convert_fusion.1 = (f32[1,4,4,3072]{3,2,1,0:T(4,128)S(1)}, bf16[1,4,4,3072]{3,2,1,0:T(4,128)(2,1)S(1)}, f32[1,4,4,3072]{3,2,1,0:T(4,128)S(1)}) fusion(bf16[3,4,4,3072]{3,2,1,0:T(4,128)(2,1)} %param.10), kind=kLoop, calls=%fused_computation.61 | loop fusion | flops 98304 | bytes 786432 | tf_op jit(solution)/shard_map/convert_element_type | solution.py:24
  11.2 1.6 %convolution_bitcast_fusion.1 = f32[64,256]{1,0:T(8,128)S(1)} fusion(bf16[64,2048]{1,0:T(8,128)(2,1)} %param.14, bf16[2048,2048]{1,0:T(8,128)(2,1)} %param.15, s32[]{:T(128)S(6)} %select_n.7), kind=kOutput, calls=%fused_computation.8 | convolution fusion | flops 67108864 | bytes 1376260 | tf_op jit(solution)/shard_map/dot_general | solution.py:174
  12.8 0.9 copy.139
  14.4 1.5 %fusion.17 = (f32[512,256]{0,1:T(8,128)S(1)}, f32[512,256]{0,1:T(8,128)S(1)}) fusion(f32[256,512]{1,0:T(8,128)S(1)} %fusion.79, bf16[512,64]{1,0:T(8,128)(2,1)S(1)} %bitcast.70, f32[64,256]{1,0:T(8,128)S(1)} %convolution_bitcast_fusion.1), kind=kOutput, calls=%fused_computation.25 | convolution fusion | flops 25362432 | bytes 1703936 | tf_op jit(solution)/shard_map/dot_general | solution.py:177
  16.5 1.5 %fusion.8 = f32[12,2048]{1,0:T(8,128)S(1)} fusion(bf16[2048,2048]{1,0:T(8,128)(2,1)} %param.16, s32[]{:T(128)S(6)} %select_n.7, bf16[4,256]{1,0:T(4,128)(2,1)S(1)} %get-tuple-element.36, bf16[4,256]{1,0:T(4,128)(2,1)S(1)} %get-tuple-element.37, bf16[4,256]{1,0:T(4,128)(2,1)S(1)} %get-tuple-element.35), kind=kOutput, calls=%fused_computation.14 | convolution fusion | flops 12601344 | bytes 1153028 | tf_op jit(solution)/shard_map/dot_general | solution.py:134
  18.9 5.9 %all-to-all-start.3 = ((f32[32,1,256]{2,1,0:T(1,128)}), f32[32,1,256]{2,1,0:T(1,128)S(1)}, u32[]{:S(2)}, u32[]{:S(2)}) async-start(f32[32,1,256]{2,1,0:T(1,128)} %reshape.140), calls=%async_computation.3 | async-start | bytes 65536 | tf_op jit(solution)/shard_map/all_to_all | solution.py:185
  25.0 7.1 %all-to-all-done.3 = f32[32,1,256]{2,1,0:T(1,128)S(1)} async-done(((f32[32,1,256]{2,1,0:T(1,128)}), f32[32,1,256]{2,1,0:T(1,128)S(1)}, u32[]{:S(2)}, u32[]{:S(2)}) %all-to-all-start.3) | async-done | bytes 32800 | tf_op jit(solution)/shard_map/all_to_all | solution.py:185
  32.1 2.6 %all-to-all-start = ((bf16[32,3,4,384]{3,2,1,0:T(4,128)(2,1)}), bf16[32,3,4,384]{3,2,1,0:T(4,128)(2,1)S(1)}, u32[]{:S(2)}, u32[]{:S(2)}) async-start(bf16[32,3,4,384]{3,2,1,0:T(4,128)(2,1)} %copy.139), calls=%async_computation | async-start | bytes 589824 | tf_op jit(solution)/shard_map/all_to_all | solution.py:169
  36.3 10.0 %all-to-all-done = bf16[32,3,4,384]{3,2,1,0:T(4,128)(2,1)S(1)} async-done(((bf16[32,3,4,384]{3,2,1,0:T(4,128)(2,1)}), bf16[32,3,4,384]{3,2,1,0:T(4,128)(2,1)S(1)}, u32[]{:S(2)}, u32[]{:S(2)}) %all-to-all-start) | async-done | bytes 294944 | tf_op jit(solution)/shard_map/all_to_all | solution.py:169
  46.3 0.9 broadcast_in_dim.7
  47.2 2.6 %all-to-all-start.4 = ((f32[32,4,1000]{2,1,0:T(4,128)}), f32[32,4,1000]{2,1,0:T(4,128)S(1)}, u32[]{:S(2)}, u32[]{:S(2)}) async-start(f32[32,4,1000]{2,1,0:T(4,128)} %broadcast_in_dim.7), calls=%async_computation.4 | async-start | bytes 1048576 | tf_op jit(solution)/shard_map/all_to_all | solution.py:215
  51.4 14.7 %all-to-all-done.4 = f32[32,4,1000]{2,1,0:T(4,128)S(1)} async-done(((f32[32,4,1000]{2,1,0:T(4,128)}), f32[32,4,1000]{2,1,0:T(4,128)S(1)}, u32[]{:S(2)}, u32[]{:S(2)}) %all-to-all-start.4) | async-done | bytes 512032 | tf_op jit(solution)/shard_map/all_to_all | solution.py:215
  66.1 2.6 %all-to-all-start.1 = ((bf16[32,4,384]{2,1,0:T(4,128)(2,1)}), bf16[32,4,384]{2,1,0:T(4,128)(2,1)S(1)}, u32[]{:S(2)}, u32[]{:S(2)}) async-start(bf16[32,4,384]{2,1,0:T(4,128)(2,1)} %reshape.125), calls=%async_computation.1 | async-start | bytes 196608 | tf_op jit(solution)/shard_map/all_to_all | solution.py:206
  70.1 6.5 %all-to-all-done.1 = bf16[32,4,384]{2,1,0:T(4,128)(2,1)S(1)} async-done(((bf16[32,4,384]{2,1,0:T(4,128)(2,1)}), bf16[32,4,384]{2,1,0:T(4,128)(2,1)S(1)}, u32[]{:S(2)}, u32[]{:S(2)}) %all-to-all-start.1) | async-done | bytes 98336 | tf_op jit(solution)/shard_map/all_to_all | solution.py:206
  76.6 2.5 %all-to-all-start.5 = ((f32[32,1,256]{2,1,0:T(1,128)}), f32[32,1,256]{2,1,0:T(1,128)S(1)}, u32[]{:S(2)}, u32[]{:S(2)}) async-start(f32[32,1,256]{2,1,0:T(1,128)} %reshape.142), calls=%async_computation.5 | async-start | bytes 65536 | tf_op jit(solution)/shard_map/all_to_all | solution.py:222
  79.2 7.2 %all-to-all-done.5 = f32[32,1,256]{2,1,0:T(1,128)S(1)} async-done(((f32[32,1,256]{2,1,0:T(1,128)}), f32[32,1,256]{2,1,0:T(1,128)S(1)}, u32[]{:S(2)}, u32[]{:S(2)}) %all-to-all-start.5) | async-done | bytes 32800 | tf_op jit(solution)/shard_map/all_to_all | solution.py:222
  87.5 1.6 %fusion.6 = f32[12,256]{1,0:T(8,128)S(1)} fusion(bf16[2048,2048]{1,0:T(8,128)(2,1)} %param.16, s32[]{:T(128)S(6)} %select_n.7, bf16[4,2048]{1,0:T(4,128)(2,1)S(1)} %get-tuple-element.24, bf16[4,2048]{1,0:T(4,128)(2,1)S(1)} %get-tuple-element.25, bf16[4,2048]{1,0:T(4,128)(2,1)S(1)} %get-tuple-element.23), kind=kOutput, calls=%fused_computation.12 | convolution fusion | flops 12730368 | bytes 1110020 | tf_op jit(solution)/shard_map/dot_general | solution.py:134
  90.4 0.8 reshape.144
  91.2 2.6 %all-to-all-start.6 = ((bf16[32,2,512]{2,1,0:T(2,128)(2,1)}), bf16[32,2,512]{2,1,0:T(2,128)(2,1)S(1)}, u32[]{:S(2)}, u32[]{:S(2)}) async-start(bf16[32,2,512]{2,1,0:T(2,128)(2,1)} %reshape.144), calls=%async_computation.6 | async-start | bytes 131072 | tf_op jit(solution)/shard_map/all_to_all | solution.py:236
  93.7 7.5 %all-to-all-done.6 = bf16[32,2,512]{2,1,0:T(2,128)(2,1)S(1)} async-done(((bf16[32,2,512]{2,1,0:T(2,128)(2,1)}), bf16[32,2,512]{2,1,0:T(2,128)(2,1)S(1)}, u32[]{:S(2)}, u32[]{:S(2)}) %all-to-all-start.6) | async-done | bytes 65568 | tf_op jit(solution)/shard_map/all_to_all | solution.py:236
  101.5 0.8 fusion.4
  (91 shorter events, 11.6 us)
Async XLA Ops:
  0.0 101.5 %copy-start = (bf16[3072,64]{0,1:T(8,128)(2,1)S(1)}, bf16[3072,64]{0,1:T(8,128)(2,1)}, u32[]{:S(2)}) copy-start(bf16[3072,64]{0,1:T(8,128)(2,1)} %param.12) | copy-start | bytes 1179652
  1.6 12.3 %all-to-all-start.2 = ((bf16[8,2,2048]{2,1,0:T(2,128)(2,1)}), bf16[8,2,2048]{2,1,0:T(2,128)(2,1)S(1)}, u32[]{:S(2)}, u32[]{:S(2)}) async-start(bf16[8,2,2048]{2,1,0:T(2,128)(2,1)} %reshape.138), calls=%async_computation.2 | async-start | bytes 131072 | tf_op jit(solution)/shard_map/all_to_all | solution.py:157
  14.0 10.8 %copy-start.2 = (bf16[64,2048]{1,0:T(8,128)(2,1)S(1)}, bf16[64,2048]{1,0:T(8,128)(2,1)}, u32[]{:S(2)}) copy-start(bf16[64,2048]{1,0:T(8,128)(2,1)} %param.14) | copy-start | bytes 786436
  14.3 21.8 %copy-start.1 = (bf16[64,1000]{1,0:T(8,128)(2,1)S(1)}, bf16[64,1000]{1,0:T(8,128)(2,1)}, u32[]{:S(2)}) copy-start(bf16[64,1000]{1,0:T(8,128)(2,1)} %param.17) | copy-start | bytes 384004
  14.4 54.7 %copy-start.3 = (s32[4]{0:T(128)S(1)}, s32[4]{0:T(128)}, u32[]{:S(2)}) copy-start(s32[4]{0:T(128)} %param.18) | copy-start | bytes 52
  15.9 63.2 %copy-start.4 = (s32[4]{0:T(128)S(1)}, s32[4]{0:T(128)}, u32[]{:S(2)}) copy-start(s32[4]{0:T(128)} %param.19) | copy-start | bytes 52
  18.9 13.2 %all-to-all-start.3 = ((f32[32,1,256]{2,1,0:T(1,128)}), f32[32,1,256]{2,1,0:T(1,128)S(1)}, u32[]{:S(2)}, u32[]{:S(2)}) async-start(f32[32,1,256]{2,1,0:T(1,128)} %reshape.140), calls=%async_computation.3 | async-start | bytes 65536 | tf_op jit(solution)/shard_map/all_to_all | solution.py:185
  32.1 14.2 %all-to-all-start = ((bf16[32,3,4,384]{3,2,1,0:T(4,128)(2,1)}), bf16[32,3,4,384]{3,2,1,0:T(4,128)(2,1)S(1)}, u32[]{:S(2)}, u32[]{:S(2)}) async-start(bf16[32,3,4,384]{3,2,1,0:T(4,128)(2,1)} %copy.139), calls=%async_computation | async-start | bytes 589824 | tf_op jit(solution)/shard_map/all_to_all | solution.py:169
  47.2 18.9 %all-to-all-start.4 = ((f32[32,4,1000]{2,1,0:T(4,128)}), f32[32,4,1000]{2,1,0:T(4,128)S(1)}, u32[]{:S(2)}, u32[]{:S(2)}) async-start(f32[32,4,1000]{2,1,0:T(4,128)} %broadcast_in_dim.7), calls=%async_computation.4 | async-start | bytes 1048576 | tf_op jit(solution)/shard_map/all_to_all | solution.py:215
  66.1 10.5 %all-to-all-start.1 = ((bf16[32,4,384]{2,1,0:T(4,128)(2,1)}), bf16[32,4,384]{2,1,0:T(4,128)(2,1)S(1)}, u32[]{:S(2)}, u32[]{:S(2)}) async-start(bf16[32,4,384]{2,1,0:T(4,128)(2,1)} %reshape.125), calls=%async_computation.1 | async-start | bytes 196608 | tf_op jit(solution)/shard_map/all_to_all | solution.py:206
  76.6 9.8 %all-to-all-start.5 = ((f32[32,1,256]{2,1,0:T(1,128)}), f32[32,1,256]{2,1,0:T(1,128)S(1)}, u32[]{:S(2)}, u32[]{:S(2)}) async-start(f32[32,1,256]{2,1,0:T(1,128)} %reshape.142), calls=%async_computation.5 | async-start | bytes 65536 | tf_op jit(solution)/shard_map/all_to_all | solution.py:222
  91.2 10.1 %all-to-all-start.6 = ((bf16[32,2,512]{2,1,0:T(2,128)(2,1)}), bf16[32,2,512]{2,1,0:T(2,128)(2,1)S(1)}, u32[]{:S(2)}, u32[]{:S(2)}) async-start(bf16[32,2,512]{2,1,0:T(2,128)(2,1)} %reshape.144), calls=%async_computation.6 | async-start | bytes 131072 | tf_op jit(solution)/shard_map/all_to_all | solution.py:236

commit v2 on v1

--- a/solution.py
+++ b/solution.py
@@ -140,100 +140,114 @@
     return product[:rows] + product[rows : 2 * rows] + product[2 * rows :]
 
 
+def split_two(values, axis):
+    high = values.astype(jnp.bfloat16)
+    low = (values - high.astype(jnp.float32)).astype(jnp.bfloat16)
+    return jnp.concatenate([high, low], axis=axis)
+
+
 def per_device_fast(qkv, positions, w_proj, latents, embed_w, up_w, down_w, head_w, labels, timesteps):
     both = ("seq", "tp")
     n_seq, n_tp = (lax.axis_size("seq"), lax.axis_size("tp"))
     count = n_seq * n_tp
-    seq_index, tp_index = (lax.axis_index("seq"), lax.axis_index("tp"))
-    flat_index = seq_index * n_tp + tp_index
+    seq_index = lax.axis_index("seq")
+    half = seq_index % 2
     samples, tok_dev, width = qkv.shape[1:]
     seq_len = tok_dev * count
     lat = latents.shape[2]
     heads = width // HEAD_DIM
     per_sample = count // samples
     heads_dev = heads // per_sample
-    chunk = heads_dev * HEAD_DIM
-
-    lat_all = lax.all_to_all(
-        jnp.broadcast_to(latents[None], (n_seq,) + latents.shape), "seq", 0, 0, tiled=True
-    )
-    lat_all = lat_all.transpose(1, 0, 2, 3).reshape(samples * seq_len, lat)
+    rows_dev, classes = head_w.shape
+    partner = [(i, i ^ n_tp) for i in range(count)]
+
+    def in_order(own):
+        other = lax.ppermute(own, both, partner)
+        mine = jnp.broadcast_to(half == 0, own.shape)
+        return jnp.stack([jnp.where(mine, own, other), jnp.where(mine, other, own)])
+
+    lat_pair = in_order(latents)
+    lat_rows = lat_pair.transpose(1, 0, 2, 3).reshape(-1, lat)
+    tok_pair = lat_rows.shape[0] // samples
+    head_pair = in_order(head_w).reshape(2 * rows_dev, classes)
+
+    units = up_w.shape[1] // 2
+    up_mine = lax.dynamic_slice_in_dim(up_w, half * units, units, 1)
+    down_mine = lax.dynamic_slice_in_dim(down_w, half * units, units, 0)
+    joint = split_two(jnp.dot(embed_w, up_mine, preferred_element_type=jnp.float32), 0)
+    hidden = jnp.dot(
+        jnp.concatenate([lat_rows, lat_rows], axis=1), joint, preferred_element_type=jnp.float32
+    )
+    act = jax.nn.gelu(hidden, approximate=False)
+    act_sum = jnp.sum(act.reshape(samples, tok_pair, units), axis=1)
+    lat_sum = jnp.sum(lat_rows.astype(jnp.float32).reshape(samples, tok_pair, lat), axis=1)
+    pool_terms = split_dot(act_sum, down_mine) + split_dot(lat_sum / (2 * n_tp), embed_w)
+    pool_terms = pool_terms.reshape(samples, n_seq // 2, 2, n_tp, rows_dev)
+    pool_terms = pool_terms.transpose(1, 3, 0, 2, 4).reshape(n_seq // 2, 1, n_tp, samples, 2 * rows_dev)
+    pool_terms = jnp.broadcast_to(pool_terms, (n_seq // 2, 2) + pool_terms.shape[2:])
+    pool_terms = split_two(pool_terms.reshape(count, samples, 2 * rows_dev), 1)
 
     angles = rope_angles(positions.astype(jnp.float32), HEAD_DIM)
     shaped = (samples, tok_dev, heads, HEAD_DIM)
-    queries = rotate(qkv[0].reshape(shaped), angles).reshape(samples, tok_dev, width)
-    keys = rotate(qkv[1].reshape(shaped), angles).reshape(samples, tok_dev, width)
-    packed = jnp.stack([queries, keys, qkv[2]])
-    packed = packed.reshape(3, samples, tok_dev, per_sample, chunk).transpose(1, 3, 0, 2, 4)
-    packed = packed.reshape(count, 3, tok_dev, chunk)
-    moved = lax.all_to_all(packed, both, 0, 0, tiled=True)
-
-    units = up_w.shape[1] // n_seq
-    up_mine = lax.dynamic_slice_in_dim(up_w, seq_index * units, units, 1)
-    down_mine = lax.dynamic_slice_in_dim(down_w, seq_index * units, units, 0)
-    joint = jnp.dot(embed_w, up_mine, preferred_element_type=jnp.float32)
-    joint_high = joint.astype(jnp.bfloat16)
-    joint_low = (joint - joint_high.astype(jnp.float32)).astype(jnp.bfloat16)
-    hidden = jnp.dot(lat_all, joint_high, preferred_element_type=jnp.float32) + jnp.dot(
-        lat_all, joint_low, preferred_element_type=jnp.float32
-    )
-    act = jax.nn.gelu(hidden, approximate=False)
-    act_sum = jnp.sum(act.reshape(samples, seq_len, units), axis=1)
-    pool_terms = split_dot(act_sum, down_mine)
-    rows_dev = head_w.shape[0]
-    pool_terms = pool_terms.reshape(samples, count, rows_dev).transpose(1, 0, 2)
-    pool_terms = lax.all_to_all(pool_terms, both, 0, 0, tiled=True)
-    lat_sum = jnp.sum(lat_all.astype(jnp.float32).reshape(samples, seq_len, lat), axis=1)
-    embed_mine = lax.dynamic_slice_in_dim(embed_w, flat_index * rows_dev, rows_dev, 1)
-    pooled = (jnp.sum(pool_terms, axis=0) + split_dot(lat_sum, embed_mine)) / seq_len
-
-    def head_view(index):
-        return moved[:, index].reshape(seq_len, heads_dev, HEAD_DIM)
-
+    queries = rotate(qkv[0].reshape(shaped), angles)
+    keys = rotate(qkv[1].reshape(shaped), angles)
+    packed = jnp.stack([queries, keys, qkv[2].reshape(shaped)])
+    packed = packed.reshape(3, samples, tok_dev, per_sample, heads_dev, HEAD_DIM)
+    packed = packed.transpose(1, 3, 0, 4, 2, 5).reshape(count, 3 * heads_dev * tok_dev, HEAD_DIM)
+    qkv_rows = packed.shape[1]
+    moved = lax.all_to_all(
+        jnp.concatenate([packed, pool_terms], axis=1), both, 0, 0, tiled=True
+    )
+
+    pooled = jnp.sum(moved[:, qkv_rows:].astype(jnp.float32), axis=0)
+    pooled = (pooled[:samples] + pooled[samples:]) / seq_len
+    padded = -(-classes // 256) * 256
+    terms = jnp.pad(split_dot(pooled, head_pair), ((0, 0), (0, padded - classes)))
+    terms = lax.dynamic_slice_in_dim(terms, half * (padded // 2), padded // 2, 1)
+    terms = lax.all_to_all(
+        jnp.broadcast_to(terms[None], (count,) + terms.shape), both, 0, 0, tiled=True
+    )
+
+    views = moved[:, :qkv_rows].reshape(count, 3, heads_dev, tok_dev, HEAD_DIM)
+    views = views.transpose(1, 2, 0, 3, 4).reshape(3, heads_dev, seq_len, HEAD_DIM)
     scores = jnp.einsum(
-        "qhd,khd->hqk", head_view(0), head_view(1), preferred_element_type=jnp.float32
+        "hqd,hkd->hqk", views[0], views[1], preferred_element_type=jnp.float32
     ) * HEAD_DIM ** (-0.5)
     weights = jnp.exp(scores - jnp.max(scores, axis=-1, keepdims=True))
     total = jnp.sum(weights, axis=-1)
     mixed = jnp.einsum(
-        "hqk,khd->hqd",
-        weights.astype(jnp.bfloat16),
-        head_view(2),
-        preferred_element_type=jnp.float32,
+        "hqk,hkd->hqd", weights.astype(jnp.bfloat16), views[2], preferred_element_type=jnp.float32
     )
     attended = (mixed / total[..., None]).astype(jnp.bfloat16)
-    attended = attended.transpose(1, 0, 2).reshape(count, tok_dev, chunk)
-    returned = lax.all_to_all(attended, both, 0, 0, tiled=True)
-    returned = returned.reshape(samples, per_sample, tok_dev, chunk).transpose(0, 2, 1, 3)
-    eps = jnp.dot(
-        returned.reshape(samples, tok_dev, width), w_proj, preferred_element_type=jnp.float32
-    )
-
-    classes = head_w.shape[1]
-    padded = -(-classes // (128 * n_tp)) * (128 * n_tp)
-    terms = split_dot(pooled, head_w)
-    terms = lax.all_to_all(
-        jnp.broadcast_to(terms[None], (count,) + terms.shape), both, 0, 0, tiled=True
-    )
-    logits = jnp.sum(terms, axis=0)
+    attended = attended.reshape(heads_dev, count, tok_dev, HEAD_DIM).transpose(1, 0, 2, 3)
+    attended = attended.reshape(count, heads_dev * tok_dev, HEAD_DIM)
+
+    logits = jnp.sum(terms.reshape(n_seq // 2, 2, n_tp, samples, padded // 2), axis=(0, 2))
+    logits = logits.transpose(1, 0, 2).reshape(samples, padded)[:, :classes]
     probs = jax.nn.softmax(logits, axis=-1)
     onehot = (labels[:, None] == jnp.arange(classes, dtype=jnp.int32)[None, :]).astype(jnp.float32)
-    share = split_dot(onehot - probs, head_w, 1)
-    dpool = lax.all_to_all(
-        jnp.broadcast_to(share[None], (count,) + share.shape), both, 0, 0, tiled=True
-    )
-    dpool = dpool.transpose(1, 0, 2).reshape(samples, count * rows_dev)
+    share = split_two(split_dot(onehot - probs, head_w, 1), 1)
+    share = jnp.broadcast_to(share[None], (count,) + share.shape)
+    att_rows = attended.shape[1]
+    second = lax.all_to_all(
+        jnp.concatenate([attended, share], axis=1), both, 0, 0, tiled=True
+    )
+    returned = second[:, :att_rows].reshape(samples, per_sample, heads_dev, tok_dev, HEAD_DIM)
+    returned = returned.transpose(0, 3, 1, 2, 4).reshape(samples, tok_dev, width)
+    eps = jnp.dot(returned, w_proj, preferred_element_type=jnp.float32)
+    dpool = second[:, att_rows:].astype(jnp.float32)
+    dpool = (dpool[..., :rows_dev] + dpool[..., rows_dev:]).transpose(1, 0, 2).reshape(samples, -1)
 
     dact = split_dot(dpool, down_mine, 1)
-    slope = gelu_slope(hidden).reshape(samples, seq_len, units)
-    dh1 = (slope * dact[:, None, :]).astype(jnp.bfloat16).reshape(samples * seq_len, units)
+    slope = gelu_slope(hidden).reshape(samples, tok_pair, units)
+    dh1 = (slope * dact[:, None, :]).astype(jnp.bfloat16).reshape(samples * tok_pair, units)
     dx_terms = lax.dot_general(
-        dh1, joint_high, (((1,), (1,)), ((), ())), preferred_element_type=jnp.float32
-    ) + lax.dot_general(
-        dh1, joint_low, (((1,), (1,)), ((), ())), preferred_element_type=jnp.float32
-    )
-    dx_terms = dx_terms.astype(jnp.bfloat16).reshape(samples, count, tok_dev, lat)
-    dx_terms = lax.all_to_all(dx_terms.transpose(1, 0, 2, 3), both, 0, 0, tiled=True)
+        dh1, joint, (((1,), (1,)), ((), ())), preferred_element_type=jnp.float32
+    )
+    dx_terms = (dx_terms[:, :lat] + dx_terms[:, lat:]).astype(jnp.bfloat16)
+    dx_terms = dx_terms.reshape(samples, 2 * n_tp, tok_dev, lat).transpose(1, 0, 2, 3)
+    planes = [[first + k for k in range(2 * n_tp)] for first in range(0, count, 2 * n_tp)]
+    dx_terms = lax.all_to_all(dx_terms, both, 0, 0, tiled=True, axis_index_groups=planes)
     dx = jnp.sum(dx_terms.astype(jnp.float32), axis=0)
     dx = dx + split_dot(dpool, embed_w, 1)[:, None, :]
     phase = (timesteps.astype(jnp.float32) / 1000.0 + 0.008) / 1.008 * (jnp.pi / 2)
@@ -248,7 +262,7 @@
     count = n_seq * lax.axis_size("tp")
     samples, heads = (qkv.shape[1], qkv.shape[3] // HEAD_DIM)
     even = count % samples == 0 and heads % max(1, count // samples) == 0
-    if even and up_w.shape[1] % (128 * n_seq) == 0:
+    if even and n_seq % 2 == 0 and up_w.shape[1] % 256 == 0:
         return per_device_fast(*args)
     return per_device_general(*args)
 

time: 103 us -> 75.4 us (0.73)
  waiting for transfers between devices: 53.1 us -> 36.3 us
  starting transfers between devices: 25.1 us -> 16.2 us
  local copies, waits for them, and re-layouts: 9.61 us -> 4.19 us
  matrix products: 8.73 us -> 12.9 us
    all_to_all x6 -> x3, waiting for transfers between devices: 38.4 us -> 24.8 us  [the longest x1 12.1 us: per_device_fast(): lax.all_to_all(jnp.concatenate([packed, pool_terms], axis=1), both, 0, 0,...]
    all_to_all x6 -> x3, starting transfers between devices: 22.5 us -> 12.8 us  [the longest x1 6.95 us: per_device_fast(): lax.all_to_all(jnp.concatenate([packed, pool_terms], axis=1), both, 0, 0,...]
    all_to_all x1, waiting for transfers between devices: 14.7 us -> 10.4 us  [per_device_fast(): lax.all_to_all(jnp.broadcast_to(terms[None], (count,) + terms.shape), bot...]
    dot_general x6, matrix products: 3.76 us -> 6.86 us  [split_dot(): lax.dot_general(split_rows(values), weights, (((1,), (contract,)), ((), (...]
    unnamed x18 -> x14, local copies, waits for them, and re-layouts: 3.46 us -> 0.88 us
    reshape x7 -> x5, local copies, waits for them, and re-layouts: 2.03 us -> 0.33 us  [the longest x2 0.14 us: per_device_fast(): pool_terms = pool_terms.reshape(samples, n_seq // 2, 2, n_tp, rows_dev)]
    concatenate x0 -> x2, local copies, waits for them, and re-layouts: none -> 1.59 us  [the longest x1 0.89 us: per_device_fast(): jnp.concatenate([packed, pool_terms], axis=1)]
    all_to_all x2 -> x0, other arithmetic: 1.44 us -> none  [the longest x1 0.72 us: per_device_fast(): lax.all_to_all(jnp.broadcast_to(share[None], (count,) + share.shape), bot...]
  transfers between devices with their start and end apart: 7 -> 6, of which waited for: 7 -> 5; matrix products, arithmetic and copies ran while one was open for 10% -> 9% of each run, Pallas kernels for 0% -> 0%
where the time goes in v2:
time: 75.4 us; the launch traced here: 74.8 us
  waiting for transfers between devices  36.3 us (48%)
  starting transfers between devices  16.2 us (21%)
  matrix products  12.9 us (17%)
  other arithmetic  4.77 us (6%)
  local copies, waits for them, and re-layouts  4.19 us (6%)
    all_to_all x1, waiting for transfers between devices, per_device_fast(): lax.all_to_all(jnp.concatenate([packed, pool_terms], axis=1), both, 0, 0,...  12.1 us
    all_to_all x1, waiting for transfers between devices, per_device_fast(): lax.all_to_all(jnp.broadcast_to(terms[None], (count,) + terms.shape), bot...  10.4 us
    all_to_all x1, waiting for transfers between devices, per_device_fast(): lax.all_to_all(jnp.concatenate([attended, share], axis=1), both, 0, 0, ti...  8.32 us
    all_to_all x1, starting transfers between devices, per_device_fast(): lax.all_to_all(jnp.concatenate([packed, pool_terms], axis=1), both, 0, 0,...  6.95 us
    dot_general x6, matrix products, split_dot(): lax.dot_general(split_rows(values), weights, (((1,), (contract,)), ((), (...  6.86 us
    all_to_all x1, waiting for transfers between devices, per_device_fast(): lax.all_to_all(dx_terms, both, 0, 0, tiled=True, axis_index_groups=planes)  4.41 us
    all_to_all x1, starting transfers between devices, per_device_fast(): lax.all_to_all(dx_terms, both, 0, 0, tiled=True, axis_index_groups=planes)  3.32 us
    dot_general x1, matrix products, per_device_fast(): jnp.dot(embed_w, up_mine, preferred_element_type=jnp.float32)  3.13 us
  transfers between devices with their start and end apart: 6, of which 5 were waited for; matrix products, arithmetic and copies ran while one was open for 9% of the time, Pallas kernels for 0%

profile of v2, /device:TPU:0, one launch (start us, length us, event | category | flops | bytes accessed | tf_op | source)
XLA Modules:
  0.0 74.8 jit_solution(2631045122658273688)
XLA Ops:
  0.0 0.5 collective-permute-start
  0.5 0.7 convert_element_type.180
  1.2 1.0 %bitcast_convert_fusion.1 = (f32[4,4,24,128]{3,1,2,0:T(4,128)S(1)}, bf16[1,4,4,3072]{3,2,1,0:T(4,128)(2,1)S(1)}, f32[4,4,24,128]{3,1,2,0:T(4,128)S(1)}) fusion(bf16[3,4,4,3072]{3,2,1,0:T(4,128)(2,1)} %param.10), kind=kLoop, calls=%fused_computation.58 | loop fusion | flops 98304 | bytes 786432 | tf_op jit(solution)/shard_map/convert_element_type | solution.py:24
  2.4 3.1 %fusion.87 = (bf16[64,1024]{1,0:T(8,128)(2,1)S(1)}, bf16[64,1024]{1,0:T(8,128)(2,1)S(1)}) fusion(bf16[64,2048]{1,0:T(8,128)(2,1)} %param.14, bf16[2048,2048]{1,0:T(8,128)(2,1)} %param.15, s32[]{:T(128)S(6)} %select_n.31), kind=kOutput, calls=%fused_computation.165 | convolution fusion | flops 268697600 | bytes 4718596 | tf_op jit(solution)/shard_map/dot_general | solution.py:177
  5.7 0.3 subtract_convert_fusion.2
  6.5 0.7 select_bitcast_fusion.3
  7.2 1.4 %bitcast_reduce_fusion = (f32[4,1024]{1,0:T(4,128)S(1)}, f32[128,1024]{1,0:T(8,128)S(1)}) fusion(bf16[64,1024]{1,0:T(8,128)(2,1)S(1)} %get-tuple-element.18, bf16[64,1024]{1,0:T(8,128)(2,1)S(1)} %get-tuple-element.17, bf16[128,64]{1,0:T(8,128)(2,1)S(1)} %bitcast.104), kind=kOutput, calls=%fused_computation.22 | convolution fusion | flops 42659840 | bytes 819200 | tf_op jit(solution)/shard_map/dot_general | solution.py:178
  8.8 2.9 %fusion.4 = f32[12,2048]{1,0:T(8,128)S(1)} fusion(bf16[2048,2048]{1,0:T(8,128)(2,1)} %param.16, s32[]{:T(128)S(6)} %select_n.31, bf16[4,1024]{1,0:T(4,128)(2,1)S(1)} %get-tuple-element.37, bf16[4,1024]{1,0:T(4,128)(2,1)S(1)} %get-tuple-element.38, bf16[4,1024]{1,0:T(4,128)(2,1)S(1)} %get-tuple-element.36), kind=kOutput, calls=%fused_computation.4 | convolution fusion | flops 50405376 | bytes 4317188 | tf_op jit(solution)/shard_map/dot_general | solution.py:134
  12.1 0.9 %copy.59 = bf16[32,44,128]{2,1,0:T(8,128)(2,1)} copy(bf16[32,44,128]{2,0,1:T(8,128)(2,1)S(1)} %pad_maximum_fusion) | data formatting | bytes 720896 | tf_op jit(solution)/shard_map/concatenate | solution.py:199
  13.0 6.9 %all-to-all-start = ((bf16[32,44,128]{2,1,0:T(8,128)(2,1)}), bf16[32,44,128]{2,1,0:T(8,128)(2,1)S(1)}, u32[]{:S(2)}, u32[]{:S(2)}) async-start(bf16[32,44,128]{2,1,0:T(8,128)(2,1)} %copy.59), calls=%async_computation | async-start | bytes 786432 | tf_op jit(solution)/shard_map/all_to_all | solution.py:198
  19.9 0.3 collective-permute-start.1
  20.3 1.1 %collective-permute-done.1 = bf16[64,1000]{1,0:T(8,128)(2,1)S(1)} collective-permute-done((bf16[64,1000]{1,0:T(8,128)(2,1)S(1)}, bf16[64,1000]{1,0:T(8,128)(2,1)S(1)}, u32[]{:S(2)}, u32[]{:S(2)}) %collective-permute-start.1) | collective-permute-done | bytes 128032 | tf_op jit(solution)/shard_map/ppermute | solution.py:165
  21.4 12.1 %all-to-all-done = bf16[32,44,128]{2,1,0:T(8,128)(2,1)S(1)} async-done(((bf16[32,44,128]{2,1,0:T(8,128)(2,1)}), bf16[32,44,128]{2,1,0:T(8,128)(2,1)S(1)}, u32[]{:S(2)}, u32[]{:S(2)}) %all-to-all-start) | async-done | bytes 360480 | tf_op jit(solution)/shard_map/all_to_all | solution.py:198
  34.1 0.7 broadcast_in_dim.16
  34.8 2.6 %all-to-all-start.1 = ((f32[32,4,512]{2,1,0:T(4,128)}), f32[32,4,512]{2,1,0:T(4,128)S(1)}, u32[]{:S(2)}, u32[]{:S(2)}) async-start(f32[32,4,512]{2,1,0:T(4,128)} %broadcast_in_dim.16), calls=%async_computation.1 | async-start | bytes 524288 | tf_op jit(solution)/shard_map/all_to_all | solution.py:207
  37.9 10.4 %all-to-all-done.1 = f32[32,4,512]{2,1,0:T(4,128)S(1)} async-done(((f32[32,4,512]{2,1,0:T(4,128)}), f32[32,4,512]{2,1,0:T(4,128)S(1)}, u32[]{:S(2)}, u32[]{:S(2)}) %all-to-all-start.1) | async-done | bytes 262176 | tf_op jit(solution)/shard_map/all_to_all | solution.py:207
  49.1 0.7 copy.66
  49.8 2.6 %all-to-all-start.2 = ((bf16[32,16,128]{2,1,0:T(8,128)(2,1)}), bf16[32,16,128]{2,1,0:T(8,128)(2,1)S(1)}, u32[]{:S(2)}, u32[]{:S(2)}) async-start(bf16[32,16,128]{2,1,0:T(8,128)(2,1)} %copy.66), calls=%async_computation.2 | async-start | bytes 262144 | tf_op jit(solution)/shard_map/all_to_all | solution.py:232
  52.4 8.3 %all-to-all-done.2 = bf16[32,16,128]{2,1,0:T(8,128)(2,1)S(1)} async-done(((bf16[32,16,128]{2,1,0:T(8,128)(2,1)}), bf16[32,16,128]{2,1,0:T(8,128)(2,1)S(1)}, u32[]{:S(2)}, u32[]{:S(2)}) %all-to-all-start.2) | async-done | bytes 131104 | tf_op jit(solution)/shard_map/all_to_all | solution.py:232
  61.2 3.4 %fusion.2 = f32[12,1024]{1,0:T(8,128)S(1)} fusion(bf16[2048,2048]{1,0:T(8,128)(2,1)} %param.16, s32[]{:T(128)S(6)} %select_n.31, bf16[4,2048]{1,0:T(4,128)(2,1)S(1)} %get-tuple-element.26, bf16[4,2048]{1,0:T(4,128)(2,1)S(1)} %get-tuple-element.27, bf16[4,2048]{1,0:T(4,128)(2,1)S(1)} %get-tuple-element.25), kind=kOutput, calls=%fused_computation.2 | convolution fusion | flops 50479104 | bytes 4292612 | tf_op jit(solution)/shard_map/dot_general | solution.py:134
  65.2 0.7 reshape.215
  65.9 3.3 %all-to-all-start.3 = ((bf16[8,2,512]{2,1,0:T(2,128)(2,1)}), bf16[8,2,512]{2,1,0:T(2,128)(2,1)S(1)}, u32[]{:S(2)}, u32[]{:S(2)}) async-start(bf16[8,2,512]{2,1,0:T(2,128)(2,1)} %reshape.215), calls=%async_computation.3 | async-start | bytes 32768 | tf_op jit(solution)/shard_map/all_to_all | solution.py:250
  69.4 4.4 %all-to-all-done.3 = bf16[8,2,512]{2,1,0:T(2,128)(2,1)S(1)} async-done(((bf16[8,2,512]{2,1,0:T(2,128)(2,1)}), bf16[8,2,512]{2,1,0:T(2,128)(2,1)S(1)}, u32[]{:S(2)}, u32[]{:S(2)}) %all-to-all-start.3) | async-done | bytes 16416 | tf_op jit(solution)/shard_map/all_to_all | solution.py:250
  74.0 0.8 %fusion.10 = bf16[4,4,64]{2,1,0:T(4,128)(2,1)} fusion(bf16[4,4,3072]{2,1,0:T(4,128)(2,1)S(1)} %reshape.209, bf16[3072,64]{0,1:T(8,128)(2,1)S(1)} %copy-done, f32[4,4,64]{2,1,0:T(4,128)S(1)} %convert_reduce_fusion.1, f32[4,64]{1,0:T(4,128)S(1)} %slice_add_fusion.10, f32[4]{0:T(128)S(1)} %sqrt_multiply_fusion), kind=kOutput, calls=%fused_computation.11 | convolution fusion | flops 6295552 | bytes 498704 | tf_op jit(solution)/shard_map/dot_general | solution.py:237
  (79 shorter events, 4.5 us)
Async XLA Ops:
  0.0 74.0 %copy-start = (bf16[3072,64]{0,1:T(8,128)(2,1)S(1)}, bf16[3072,64]{0,1:T(8,128)(2,1)}, u32[]{:S(2)}) copy-start(bf16[3072,64]{0,1:T(8,128)(2,1)} %param.12) | copy-start | bytes 1179652
  0.0 6.4 %collective-permute-start = (bf16[4,16,64]{2,1,0:T(8,128)(2,1)}, bf16[4,16,64]{2,1,0:T(8,128)(2,1)S(1)}, u32[]{:S(2)}, u32[]{:S(2)}) collective-permute-start(bf16[4,16,64]{2,1,0:T(8,128)(2,1)} %param.13), channel_id=1, source_target_pairs={{0,4},{1,5},{2,6},{3,7},{4,0},{5,1},{6,2},{7,3},{8,12},{9,13},{10,... | collective-permute-start | bytes 24584 | tf_op jit(solution)/shard_map/ppermute | solution.py:165
  5.5 3.2 %copy-start.1 = (bf16[64,2048]{1,0:T(8,128)(2,1)S(1)}, bf16[64,2048]{1,0:T(8,128)(2,1)}, u32[]{:S(2)}) copy-start(bf16[64,2048]{1,0:T(8,128)(2,1)} %param.14) | copy-start | bytes 786436
  7.2 12.7 %copy-start.2 = (bf16[64,1000]{1,0:T(8,128)(2,1)S(1)}, bf16[64,1000]{1,0:T(8,128)(2,1)}, u32[]{:S(2)}) copy-start(bf16[64,1000]{1,0:T(8,128)(2,1)} %param.17) | copy-start | bytes 384004
  8.6 40.1 %copy-start.3 = (s32[4]{0:T(128)S(1)}, s32[4]{0:T(128)}, u32[]{:S(2)}) copy-start(s32[4]{0:T(128)} %param.18) | copy-start | bytes 52
  8.6 43.7 %copy-start.4 = (s32[4]{0:T(128)S(1)}, s32[4]{0:T(128)}, u32[]{:S(2)}) copy-start(s32[4]{0:T(128)} %param.19) | copy-start | bytes 52
  13.0 20.6 %all-to-all-start = ((bf16[32,44,128]{2,1,0:T(8,128)(2,1)}), bf16[32,44,128]{2,1,0:T(8,128)(2,1)S(1)}, u32[]{:S(2)}, u32[]{:S(2)}) async-start(bf16[32,44,128]{2,1,0:T(8,128)(2,1)} %copy.59), calls=%async_computation | async-start | bytes 786432 | tf_op jit(solution)/shard_map/all_to_all | solution.py:198
  19.9 1.4 %collective-permute-start.1 = (bf16[64,1000]{1,0:T(8,128)(2,1)S(1)}, bf16[64,1000]{1,0:T(8,128)(2,1)S(1)}, u32[]{:S(2)}, u32[]{:S(2)}) collective-permute-start(bf16[64,1000]{1,0:T(8,128)(2,1)S(1)} %copy-done.2), channel_id=1, source_target_pairs={{0,4},{1,5},{2,6},{3,7},{4,0},{5,1},{6,2},{7,3},{8,12},{9,13},{10,... | collective-permute-start | bytes 384008 | tf_op jit(solution)/shard_map/ppermute | solution.py:165
  34.8 13.5 %all-to-all-start.1 = ((f32[32,4,512]{2,1,0:T(4,128)}), f32[32,4,512]{2,1,0:T(4,128)S(1)}, u32[]{:S(2)}, u32[]{:S(2)}) async-start(f32[32,4,512]{2,1,0:T(4,128)} %broadcast_in_dim.16), calls=%async_computation.1 | async-start | bytes 524288 | tf_op jit(solution)/shard_map/all_to_all | solution.py:207
  49.8 10.9 %all-to-all-start.2 = ((bf16[32,16,128]{2,1,0:T(8,128)(2,1)}), bf16[32,16,128]{2,1,0:T(8,128)(2,1)S(1)}, u32[]{:S(2)}, u32[]{:S(2)}) async-start(bf16[32,16,128]{2,1,0:T(8,128)(2,1)} %copy.66), calls=%async_computation.2 | async-start | bytes 262144 | tf_op jit(solution)/shard_map/all_to_all | solution.py:232
  65.9 8.0 %all-to-all-start.3 = ((bf16[8,2,512]{2,1,0:T(2,128)(2,1)}), bf16[8,2,512]{2,1,0:T(2,128)(2,1)S(1)}, u32[]{:S(2)}, u32[]{:S(2)}) async-start(bf16[8,2,512]{2,1,0:T(2,128)(2,1)} %reshape.215), calls=%async_computation.3 | async-start | bytes 32768 | tf_op jit(solution)/shard_map/all_to_all | solution.py:250

commit v3 on v2

--- a/solution.py
+++ b/solution.py
@@ -1,6 +1,11 @@
+import functools
+
 import jax
 import jax.numpy as jnp
+import numpy as np
 from jax import lax
+from jax.experimental import pallas as pl
+from jax.experimental.pallas import tpu as pltpu
 from jax.sharding import PartitionSpec as P
 
 HEAD_DIM = 128
@@ -146,6 +151,303 @@
     return jnp.concatenate([high, low], axis=axis)
 
 
+LANES = 128
+
+
+def lane_frequencies():
+    frame_width = HEAD_DIM // 8
+    plane_width = (HEAD_DIM - frame_width) // 2
+    freqs, axes = [], []
+    for axis, width in zip(range(3), (frame_width, plane_width, plane_width)):
+        steps = np.arange(0, width, 2, dtype=np.float32) / np.float32(width)
+        freqs.append(np.float32(10000.0) ** (-steps))
+        axes.append(np.full(width // 2, axis, np.float32))
+    freqs, axes = (np.concatenate(freqs), np.concatenate(axes))
+    table = np.stack([np.tile(freqs, 2), np.tile(axes, 2)]).astype(np.float32)
+    return np.pad(table, ((0, 6), (0, 0)))
+
+
+def forward_kernel(
+    sizes,
+    pos_ref,
+    table_ref,
+    qkv_hbm,
+    own_hbm,
+    other_hbm,
+    embed_hbm,
+    up_hbm,
+    down_hbm,
+    pay_ref,
+    slope_ref,
+    joint_ref,
+    qkv_ref,
+    lat_ref,
+    embed_ref,
+    up_ref,
+    down_ref,
+    rows_ref,
+    sems,
+):
+    n_seq, n_tp, steps, seq_len = sizes
+    samples, tok_dev, width = qkv_ref.shape[1:]
+    count = n_seq * n_tp
+    per_sample = count // samples
+    heads_dev = width // HEAD_DIM // per_sample
+    tok_seq, lat = own_hbm.shape[1:]
+    units = down_ref.shape[0]
+    part = units // steps
+    half = lax.axis_index("seq") % 2
+
+    def up_copy(step):
+        start = pl.multiple_of(half * units + step * part, LANES)
+        return pltpu.make_async_copy(
+            up_hbm.at[:, pl.ds(start, part)], up_ref.at[step], sems.at[4 + step]
+        )
+
+    def down_copy(step):
+        start = pl.multiple_of(half * units + step * part, LANES)
+        return pltpu.make_async_copy(
+            down_hbm.at[pl.ds(start, part)],
+            down_ref.at[pl.ds(step * part, part)],
+            sems.at[4 + steps + step],
+        )
+
+    own_copy = pltpu.make_async_copy(own_hbm, lat_ref.at[half], sems.at[0])
+    other_copy = pltpu.make_async_copy(other_hbm, lat_ref.at[1 - half], sems.at[1])
+    embed_copy = pltpu.make_async_copy(embed_hbm, embed_ref, sems.at[2])
+    qkv_copy = pltpu.make_async_copy(qkv_hbm, qkv_ref, sems.at[3])
+    for copy in (own_copy, other_copy, qkv_copy, embed_copy):
+        copy.start()
+    for step in range(steps):
+        up_copy(step).start()
+    for step in range(steps):
+        down_copy(step).start()
+
+    shape = (samples * tok_dev, LANES)
+    row = lax.broadcasted_iota(jnp.int32, shape, 0)
+    lane = lax.broadcasted_iota(jnp.int32, shape, 1)
+    axis = jnp.broadcast_to(table_ref[1:2, :], shape)
+    angles = jnp.zeros(shape, jnp.float32)
+    for index in range(samples * tok_dev):
+        sample, token = divmod(index, tok_dev)
+        frame, line, column = (pos_ref[k, sample, token].astype(jnp.float32) for k in range(3))
+        value = jnp.where(axis < 0.5, frame, jnp.where(axis < 1.5, line, column))
+        angles = jnp.where(row == index, value, angles)
+    angles = angles * jnp.broadcast_to(table_ref[0:1, :], shape)
+    cosine = jnp.cos(angles)
+    sine = jnp.sin(angles)
+    sine = jnp.where(lane < HEAD_DIM // 2, -sine, sine)
+
+    qkv_copy.wait()
+    for sample in range(samples):
+        cos_rows = cosine[sample * tok_dev : (sample + 1) * tok_dev]
+        sin_rows = sine[sample * tok_dev : (sample + 1) * tok_dev]
+        for head in range(width // HEAD_DIM):
+            target = sample * per_sample + head // heads_dev
+            span = slice(head * HEAD_DIM, (head + 1) * HEAD_DIM)
+            for kind in range(3):
+                group = 2 + kind * heads_dev + head % heads_dev
+                values = qkv_ref[kind, sample, :, span]
+                if kind < 2:
+                    values = values.astype(jnp.float32)
+                    values = values * cos_rows + pltpu.roll(values, HEAD_DIM // 2, 1) * sin_rows
+                pay_ref[target, group] = values.astype(jnp.bfloat16)
+
+    own_copy.wait()
+    other_copy.wait()
+    tok_pair = 2 * tok_seq
+    sums = []
+    for sample in range(samples):
+        pieces = [lat_ref[0, sample], lat_ref[1, sample]]
+        rows = jnp.concatenate(pieces, axis=0)
+        rows_ref[sample * tok_pair : (sample + 1) * tok_pair] = jnp.concatenate([rows, rows], axis=1)
+        sums.append(jnp.sum(rows.astype(jnp.float32), axis=0, keepdims=True))
+    lat_sum = jnp.concatenate(sums, axis=0) * (1.0 / (2 * n_tp))
+    lat_high = lat_sum.astype(jnp.bfloat16)
+    lat_low = (lat_sum - lat_high.astype(jnp.float32)).astype(jnp.bfloat16)
+    lat_rows = rows_ref[...]
+
+    embed_copy.wait()
+    embed = embed_ref[...]
+    total = jnp.dot(
+        jnp.concatenate([lat_high, lat_low], axis=0), embed, preferred_element_type=jnp.float32
+    )
+    parts = []
+    for step in range(steps):
+        up_copy(step).wait()
+        joint = jnp.dot(embed, up_ref[step], preferred_element_type=jnp.float32)
+        high = joint.astype(jnp.bfloat16)
+        low = (joint - high.astype(jnp.float32)).astype(jnp.bfloat16)
+        joint = jnp.concatenate([high, low], axis=0)
+        span = slice(step * part, (step + 1) * part)
+        joint_ref[:, span] = joint
+        hidden = jnp.dot(lat_rows, joint, preferred_element_type=jnp.float32)
+        cdf = 0.5 * (1.0 + lax.erf(hidden * 0.7071067811865476))
+        pdf = jnp.exp(-0.5 * hidden * hidden) * 0.3989422804014327
+        slope_ref[:, span] = cdf + hidden * pdf
+        act_sum = jnp.sum((hidden * cdf).reshape(samples, tok_pair, part), axis=1)
+        high = act_sum.astype(jnp.bfloat16)
+        low = (act_sum - high.astype(jnp.float32)).astype(jnp.bfloat16)
+        parts.append(jnp.concatenate([high, low], axis=0))
+    for step in range(steps):
+        down_copy(step).wait()
+        total = total + jnp.dot(
+            parts[step],
+            down_ref[step * part : (step + 1) * part],
+            preferred_element_type=jnp.float32,
+        )
+    pool = (total[:samples] + total[samples:]) * (1.0 / seq_len)
+    side = lax.broadcasted_iota(jnp.int32, (samples, LANES), 1) < LANES // 2
+    for plane in range(n_seq // 2):
+        for column in range(n_tp):
+            first = (plane * 2 * n_tp + column) // 2
+            second = (plane * 2 * n_tp + n_tp + column) // 2
+            first = pool[:, first * LANES : (first + 1) * LANES]
+            second = pool[:, second * LANES : (second + 1) * LANES]
+            if column % 2 == 0:
+                block = jnp.where(side, first, pltpu.roll(second, LANES // 2, 1))
+            else:
+                block = jnp.where(side, pltpu.roll(first, LANES // 2, 1), second)
+            high = block.astype(jnp.bfloat16)
+            low = (block - high.astype(jnp.float32)).astype(jnp.bfloat16)
+            for core in range(2):
+                target = (plane * 2 + core) * n_tp + column
+                pay_ref[target, 0] = high
+                pay_ref[target, 1] = low
+
+
+def forward(qkv, positions, own, other, embed_w, up_w, down_w, n_seq, n_tp):
+    samples, tok_dev, width = qkv.shape[1:]
+    count = n_seq * n_tp
+    groups = 2 + 3 * (width // HEAD_DIM // (count // samples))
+    tok_seq, lat = own.shape[1:]
+    units, features = (up_w.shape[1] // 2, up_w.shape[0])
+    steps = units // 256
+    rows = 2 * tok_seq * samples
+    any_spec = pl.BlockSpec(memory_space=pl.ANY)
+    hbm_spec = pl.BlockSpec(memory_space=pltpu.HBM)
+    vmem_spec = pl.BlockSpec(memory_space=pltpu.VMEM)
+    return pl.pallas_call(
+        functools.partial(forward_kernel, (n_seq, n_tp, steps, tok_dev * count)),
+        out_shape=(
+            jax.ShapeDtypeStruct((count, groups, tok_dev, LANES), jnp.bfloat16),
+            jax.ShapeDtypeStruct((rows, units), jnp.float32),
+            jax.ShapeDtypeStruct((2 * lat, units), jnp.bfloat16),
+        ),
+        in_specs=[
+            pl.BlockSpec(memory_space=pltpu.SMEM),
+            vmem_spec,
+            hbm_spec,
+            any_spec,
+            any_spec,
+            hbm_spec,
+            hbm_spec,
+            hbm_spec,
+        ],
+        out_specs=(vmem_spec,) * 3,
+        scratch_shapes=[
+            pltpu.VMEM(qkv.shape, jnp.bfloat16),
+            pltpu.VMEM((2,) + own.shape, jnp.bfloat16),
+            pltpu.VMEM(embed_w.shape, jnp.bfloat16),
+            pltpu.VMEM((steps, features, 256), jnp.bfloat16),
+            pltpu.VMEM((units, features), jnp.bfloat16),
+            pltpu.VMEM((rows, 2 * lat), jnp.bfloat16),
+            pltpu.SemaphoreType.DMA((4 + 2 * steps,)),
+        ],
+        compiler_params=pltpu.CompilerParams(vmem_limit_bytes=52 << 20),
+        cost_estimate=pl.CostEstimate(
+            flops=4 * features * units * 64, bytes_accessed=4 * features * units, transcendentals=0
+        ),
+        name="forward",
+    )(positions, jnp.asarray(lane_frequencies()), qkv, own, other, embed_w, up_w, down_w)
+
+
+def backward_kernel(
+    steps, second_ref, slope_ref, joint_ref, down_hbm, out_ref, dpool_ref, down_ref, sems
+):
+    count, groups, samples, _ = second_ref.shape
+    units = down_ref.shape[0]
+    part = units // steps
+    half = lax.axis_index("seq") % 2
+
+    def down_copy(step):
+        start = pl.multiple_of(half * units + step * part, LANES)
+        return pltpu.make_async_copy(
+            down_hbm.at[pl.ds(start, part)],
+            down_ref.at[pl.ds(step * part, part)],
+            sems.at[step],
+        )
+
+    for step in range(steps):
+        down_copy(step).start()
+    rows = slope_ref.shape[0] // samples
+    side = lax.broadcasted_iota(jnp.int32, (samples, LANES), 1) < LANES // 2
+    for pair in range(count // 2):
+        first = second_ref[2 * pair, groups - 1].astype(jnp.float32)
+        second = second_ref[2 * pair + 1, groups - 1].astype(jnp.float32)
+        first = first + pltpu.roll(first, LANES // 2, 1)
+        second = second + pltpu.roll(second, LANES // 2, 1)
+        block = jnp.where(side, first, second)
+        high = block.astype(jnp.bfloat16)
+        low = (block - high.astype(jnp.float32)).astype(jnp.bfloat16)
+        dpool_ref[:, pair * LANES : (pair + 1) * LANES] = jnp.concatenate([high, low], axis=0)
+    dpool = dpool_ref[...]
+    pieces = []
+    for step in range(steps):
+        down_copy(step).wait()
+        pieces.append(
+            lax.dot_general(
+                dpool,
+                down_ref[step * part : (step + 1) * part],
+                (((1,), (1,)), ((), ())),
+                preferred_element_type=jnp.float32,
+            )
+        )
+    dact = jnp.concatenate(pieces, axis=1)
+    dact = dact[:samples] + dact[samples:]
+    halves = []
+    for sample in range(samples):
+        dh1 = slope_ref[sample * rows : (sample + 1) * rows] * dact[sample : sample + 1]
+        halves.append(dh1.astype(jnp.bfloat16))
+    dx = lax.dot_general(
+        jnp.concatenate(halves, axis=0),
+        joint_ref[...],
+        (((1,), (1,)), ((), ())),
+        preferred_element_type=jnp.float32,
+    )
+    dx = dx + pltpu.roll(dx, LANES // 2, 1)
+    side = lax.broadcasted_iota(jnp.int32, (rows, LANES), 1) < LANES // 2
+    tok_dev = out_ref.shape[2]
+    for pair in range(samples // 2):
+        first = dx[2 * pair * rows : (2 * pair + 1) * rows]
+        second = dx[(2 * pair + 1) * rows : (2 * pair + 2) * rows]
+        both = jnp.where(side, first, second)
+        for target in range(rows // tok_dev):
+            out_ref[target, pair] = both[target * tok_dev : (target + 1) * tok_dev].astype(jnp.bfloat16)
+
+
+def backward(second, slope, joint, down, tok_dev):
+    samples = second.shape[2]
+    targets = slope.shape[0] // samples // tok_dev
+    units, steps = (slope.shape[1], slope.shape[1] // 256)
+    vmem_spec = pl.BlockSpec(memory_space=pltpu.VMEM)
+    return pl.pallas_call(
+        functools.partial(backward_kernel, steps),
+        out_shape=(
+            jax.ShapeDtypeStruct((targets, samples // 2, tok_dev, LANES), jnp.bfloat16),
+            jax.ShapeDtypeStruct((2 * samples, down.shape[1]), jnp.bfloat16),
+        ),
+        in_specs=[vmem_spec] * 3 + [pl.BlockSpec(memory_space=pltpu.HBM)],
+        out_specs=(vmem_spec,) * 2,
+        scratch_shapes=[
+            pltpu.VMEM((units, down.shape[1]), jnp.bfloat16),
+            pltpu.SemaphoreType.DMA((steps,)),
+        ],
+        compiler_params=pltpu.CompilerParams(vmem_limit_bytes=52 << 20),
+        name="backward",
+    )(second, slope, joint, down)
+
+
 def per_device_fast(qkv, positions, w_proj, latents, embed_w, up_w, down_w, head_w, labels, timesteps):
     both = ("seq", "tp")
     n_seq, n_tp = (lax.axis_size("seq"), lax.axis_size("tp"))
@@ -166,41 +468,15 @@
         mine = jnp.broadcast_to(half == 0, own.shape)
         return jnp.stack([jnp.where(mine, own, other), jnp.where(mine, other, own)])
 
-    lat_pair = in_order(latents)
-    lat_rows = lat_pair.transpose(1, 0, 2, 3).reshape(-1, lat)
-    tok_pair = lat_rows.shape[0] // samples
+    other = lax.ppermute(latents, both, partner)
     head_pair = in_order(head_w).reshape(2 * rows_dev, classes)
 
-    units = up_w.shape[1] // 2
-    up_mine = lax.dynamic_slice_in_dim(up_w, half * units, units, 1)
-    down_mine = lax.dynamic_slice_in_dim(down_w, half * units, units, 0)
-    joint = split_two(jnp.dot(embed_w, up_mine, preferred_element_type=jnp.float32), 0)
-    hidden = jnp.dot(
-        jnp.concatenate([lat_rows, lat_rows], axis=1), joint, preferred_element_type=jnp.float32
-    )
-    act = jax.nn.gelu(hidden, approximate=False)
-    act_sum = jnp.sum(act.reshape(samples, tok_pair, units), axis=1)
-    lat_sum = jnp.sum(lat_rows.astype(jnp.float32).reshape(samples, tok_pair, lat), axis=1)
-    pool_terms = split_dot(act_sum, down_mine) + split_dot(lat_sum / (2 * n_tp), embed_w)
-    pool_terms = pool_terms.reshape(samples, n_seq // 2, 2, n_tp, rows_dev)
-    pool_terms = pool_terms.transpose(1, 3, 0, 2, 4).reshape(n_seq // 2, 1, n_tp, samples, 2 * rows_dev)
-    pool_terms = jnp.broadcast_to(pool_terms, (n_seq // 2, 2) + pool_terms.shape[2:])
-    pool_terms = split_two(pool_terms.reshape(count, samples, 2 * rows_dev), 1)
-
-    angles = rope_angles(positions.astype(jnp.float32), HEAD_DIM)
-    shaped = (samples, tok_dev, heads, HEAD_DIM)
-    queries = rotate(qkv[0].reshape(shaped), angles)
-    keys = rotate(qkv[1].reshape(shaped), angles)
-    packed = jnp.stack([queries, keys, qkv[2].reshape(shaped)])
-    packed = packed.reshape(3, samples, tok_dev, per_sample, heads_dev, HEAD_DIM)
-    packed = packed.transpose(1, 3, 0, 4, 2, 5).reshape(count, 3 * heads_dev * tok_dev, HEAD_DIM)
-    qkv_rows = packed.shape[1]
-    moved = lax.all_to_all(
-        jnp.concatenate([packed, pool_terms], axis=1), both, 0, 0, tiled=True
-    )
-
-    pooled = jnp.sum(moved[:, qkv_rows:].astype(jnp.float32), axis=0)
-    pooled = (pooled[:samples] + pooled[samples:]) / seq_len
+    payload, slope, joint = forward(
+        qkv, positions, latents, other, embed_w, up_w, down_w, n_seq, n_tp
+    )
+    moved = lax.all_to_all(payload, both, 0, 0, tiled=True)
+
+    pooled = jnp.sum(moved[:, :2].astype(jnp.float32), axis=(0, 1))
     padded = -(-classes // 256) * 256
     terms = jnp.pad(split_dot(pooled, head_pair), ((0, 0), (0, padded - classes)))
     terms = lax.dynamic_slice_in_dim(terms, half * (padded // 2), padded // 2, 1)
@@ -208,7 +484,7 @@
         jnp.broadcast_to(terms[None], (count,) + terms.shape), both, 0, 0, tiled=True
     )
 
-    views = moved[:, :qkv_rows].reshape(count, 3, heads_dev, tok_dev, HEAD_DIM)
+    views = moved[:, 2:].reshape(count, 3, heads_dev, tok_dev, HEAD_DIM)
     views = views.transpose(1, 2, 0, 3, 4).reshape(3, heads_dev, seq_len, HEAD_DIM)
     scores = jnp.einsum(
         "hqd,hkd->hqk", views[0], views[1], preferred_element_type=jnp.float32
@@ -220,36 +496,29 @@
     )
     attended = (mixed / total[..., None]).astype(jnp.bfloat16)
     attended = attended.reshape(heads_dev, count, tok_dev, HEAD_DIM).transpose(1, 0, 2, 3)
-    attended = attended.reshape(count, heads_dev * tok_dev, HEAD_DIM)
 
     logits = jnp.sum(terms.reshape(n_seq // 2, 2, n_tp, samples, padded // 2), axis=(0, 2))
     logits = logits.transpose(1, 0, 2).reshape(samples, padded)[:, :classes]
     probs = jax.nn.softmax(logits, axis=-1)
     onehot = (labels[:, None] == jnp.arange(classes, dtype=jnp.int32)[None, :]).astype(jnp.float32)
     share = split_two(split_dot(onehot - probs, head_w, 1), 1)
-    share = jnp.broadcast_to(share[None], (count,) + share.shape)
-    att_rows = attended.shape[1]
+    share = jnp.broadcast_to(share[None, None], (count, 1) + share.shape)
     second = lax.all_to_all(
         jnp.concatenate([attended, share], axis=1), both, 0, 0, tiled=True
     )
-    returned = second[:, :att_rows].reshape(samples, per_sample, heads_dev, tok_dev, HEAD_DIM)
+    returned = second[:, :heads_dev].reshape(samples, per_sample, heads_dev, tok_dev, HEAD_DIM)
     returned = returned.transpose(0, 3, 1, 2, 4).reshape(samples, tok_dev, width)
     eps = jnp.dot(returned, w_proj, preferred_element_type=jnp.float32)
-    dpool = second[:, att_rows:].astype(jnp.float32)
-    dpool = (dpool[..., :rows_dev] + dpool[..., rows_dev:]).transpose(1, 0, 2).reshape(samples, -1)
-
-    dact = split_dot(dpool, down_mine, 1)
-    slope = gelu_slope(hidden).reshape(samples, tok_pair, units)
-    dh1 = (slope * dact[:, None, :]).astype(jnp.bfloat16).reshape(samples * tok_pair, units)
-    dx_terms = lax.dot_general(
-        dh1, joint, (((1,), (1,)), ((), ())), preferred_element_type=jnp.float32
-    )
-    dx_terms = (dx_terms[:, :lat] + dx_terms[:, lat:]).astype(jnp.bfloat16)
-    dx_terms = dx_terms.reshape(samples, 2 * n_tp, tok_dev, lat).transpose(1, 0, 2, 3)
+    dx_terms, dpool = backward(second, slope, joint, down_w, tok_dev)
     planes = [[first + k for k in range(2 * n_tp)] for first in range(0, count, 2 * n_tp)]
     dx_terms = lax.all_to_all(dx_terms, both, 0, 0, tiled=True, axis_index_groups=planes)
     dx = jnp.sum(dx_terms.astype(jnp.float32), axis=0)
-    dx = dx + split_dot(dpool, embed_w, 1)[:, None, :]
+    dx = dx.reshape(samples // 2, tok_dev, 2, lat).transpose(0, 2, 1, 3)
+    dx = dx.reshape(samples, tok_dev, lat)
+    dx_pool = lax.dot_general(
+        dpool, embed_w, (((1,), (1,)), ((), ())), preferred_element_type=jnp.float32
+    )
+    dx = dx + (dx_pool[:samples] + dx_pool[samples:])[:, None, :]
     phase = (timesteps.astype(jnp.float32) / 1000.0 + 0.008) / 1.008 * (jnp.pi / 2)
     abar = jnp.cos(phase) ** 2
     scale = GUIDANCE * jnp.sqrt(1.0 - abar)
@@ -261,8 +530,12 @@
     n_seq = lax.axis_size("seq")
     count = n_seq * lax.axis_size("tp")
     samples, heads = (qkv.shape[1], qkv.shape[3] // HEAD_DIM)
+    tok_dev, tok_seq, lat = (qkv.shape[2], latents.shape[1], latents.shape[2])
     even = count % samples == 0 and heads % max(1, count // samples) == 0
-    if even and n_seq % 2 == 0 and up_w.shape[1] % 256 == 0:
+    even = even and n_seq % 2 == 0 and count // n_seq % 2 == 0 and samples == 4 and tok_dev == 4
+    even = even and lat == 64 and head_w.shape[0] == 64 and tok_seq % 16 == 0
+    even = even and up_w.shape[1] % 512 == 0 and tok_seq == tok_dev * (count // n_seq)
+    if even and count * head_w.shape[0] == up_w.shape[0]:
         return per_device_fast(*args)
     return per_device_general(*args)
 

time: 75.4 us -> 72.9 us (0.967)
  matrix products: 12.9 us -> 1.75 us
  Pallas kernels: 0 us -> 10.8 us
  other arithmetic: 4.77 us -> 1.59 us
  local copies, waits for them, and re-layouts: 4.19 us -> 5.27 us
    pallas_call x0 -> x2, Pallas kernels: none -> 10.8 us  [the longest x1 6.15 us: forward(): pl.pallas_call(functools.partial(forward_kernel, (n_seq, n_tp, steps, tok...]
    dot_general x6 -> x2, matrix products: 6.86 us -> 0.3 us  [split_dot(): lax.dot_general(split_rows(values), weights, (((1,), (contract,)), ((), (...]
    dot_general x3 -> x1, matrix products: 4.72 us -> 0.17 us  [per_device_fast(): lax.dot_general(dpool, embed_w, (((1,), (1,)), ((), ())), preferred_eleme...]
    unnamed x14 -> x20, local copies, waits for them, and re-layouts: 0.88 us -> 4.03 us
    convert_element_type x5 -> x0, other arithmetic: 1.98 us -> none  [the longest x1 1.04 us: rotate(): floats = values.astype(jnp.float32)]
    concatenate x2 -> x0, local copies, waits for them, and re-layouts: 1.59 us -> none  [the longest x1 0.89 us: per_device_fast(): jnp.concatenate([packed, pool_terms], axis=1)]
    ppermute x0 -> x1, waiting for transfers between devices: none -> 1.05 us  [per_device_fast(): other = lax.ppermute(latents, both, partner)]
  transfers between devices with their start and end apart: 6 -> 6, of which waited for: 5 -> 6; matrix products, arithmetic and copies ran while one was open for 9% -> 2% of each run, Pallas kernels for 0% -> 0%
where the time goes in v3:
time: 72.9 us; the launch traced here: 72.4 us
  waiting for transfers between devices  36.3 us (50%)
  starting transfers between devices  16.5 us (23%)
  Pallas kernels  10.8 us (15%)
  local copies, waits for them, and re-layouts  5.27 us (7%)
  matrix products  1.75 us (2%)
  other arithmetic  1.59 us (2%)
    all_to_all x1, waiting for transfers between devices, per_device_fast(): moved = lax.all_to_all(payload, both, 0, 0, tiled=True)  11.4 us
    all_to_all x1, waiting for transfers between devices, per_device_fast(): lax.all_to_all(jnp.broadcast_to(terms[None], (count,) + terms.shape), bot...  9.99 us
    all_to_all x1, waiting for transfers between devices, per_device_fast(): lax.all_to_all(jnp.concatenate([attended, share], axis=1), both, 0, 0, ti...  8.32 us
    all_to_all x1, starting transfers between devices, per_device_fast(): moved = lax.all_to_all(payload, both, 0, 0, tiled=True)  7.19 us
    pallas_call x1, Pallas kernels, forward(): pl.pallas_call(functools.partial(forward_kernel, (n_seq, n_tp, steps, tok...  6.15 us
    pallas_call x1, Pallas kernels, backward(): pl.pallas_call(functools.partial(backward_kernel, steps), out_shape=(jax....  4.66 us
    all_to_all x1, waiting for transfers between devices, per_device_fast(): lax.all_to_all(dx_terms, both, 0, 0, tiled=True, axis_index_groups=planes)  4.4 us
    unnamed x20, local copies, waits for them, and re-layouts  4.03 us
  transfers between devices with their start and end apart: 6, of which 6 were waited for; matrix products, arithmetic and copies ran while one was open for 2% of the time, Pallas kernels for 0%

profile of v3, /device:TPU:0, one launch (start us, length us, event | category | flops | bytes accessed | tf_op | source)
XLA Modules:
  0.0 72.4 jit_solution(12504187837048559786)
XLA Ops:
  0.0 0.5 collective-permute-start
  0.5 1.0 %collective-permute-done.other_hbm = bf16[4,16,64]{2,1,0:T(8,128)(2,1)S(1)} collective-permute-done((bf16[4,16,64]{2,1,0:T(8,128)(2,1)}, bf16[4,16,64]{2,1,0:T(8,128)(2,1)S(1)}, u32[]{:S(2)}, u32[]{:S(2)}) %collective-permute-start) | collective-permute-done | bytes 8224 | tf_op jit(solution)/shard_map/ppermute | solution.py:471
  1.5 0.9 %copy-done.1 = bf16[64,2048]{1,0:T(8,128)(2,1)S(1)} copy-done((bf16[64,2048]{1,0:T(8,128)(2,1)S(1)}, bf16[64,2048]{1,0:T(8,128)(2,1)}, u32[]{:S(2)}) %copy-start.1) | copy-done | bytes 262168
  2.5 1.0 %copy-done.3 = bf16[3,4,4,3072]{3,2,1,0:T(4,128)(2,1)S(1)} copy-done((bf16[3,4,4,3072]{3,2,1,0:T(4,128)(2,1)S(1)}, bf16[3,4,4,3072]{3,2,1,0:T(4,128)(2,1)}, u32[]{:S(2)}) %copy-start.3) | copy-done | bytes 294936
  3.5 0.7 copy-done.4
  4.2 0.7 copy-done.5
  4.9 0.7 copy-done.6
  5.6 6.2 %forward.1 = (bf16[32,11,4,128]{3,2,1,0:T(4,128)(2,1)}, f32[128,1024]{1,0:T(8,128)S(1)}, bf16[128,1024]{1,0:T(8,128)(2,1)S(1)}) custom-call(s32[3,4,4]{2,1,0:T(4,128)S(1)} %copy-done.5, f32[8,128]{1,0:T(8,128)S(1)} %copy-done.6, bf16[3,4,4,3072]{3,2,1,0:T(4,128)(2,1)S(1)} %copy-done.3, bf16[4,16,64]{2,1,0:T(8,128)(2,1)S(1)} %copy-done.4, ...), custom_call_target="tpu_custom_call" | custom-call | flops 536870912 | bytes 8388608 | tf_op jit(solution)/shard_map/forward/pallas_call | solution.py:330
  11.7 7.2 %all-to-all-start = ((bf16[32,11,4,128]{3,2,1,0:T(4,128)(2,1)}), bf16[32,11,4,128]{3,2,1,0:T(4,128)(2,1)S(1)}, u32[]{:S(2)}, u32[]{:S(2)}) async-start(bf16[32,11,4,128]{3,2,1,0:T(4,128)(2,1)} %get-tuple-element.10), calls=%async_computation | async-start | bytes 720896 | tf_op jit(solution)/shard_map/all_to_all | solution.py:477
  18.9 0.3 collective-permute-start.1
  19.3 1.1 %collective-permute-done.1 = bf16[64,1000]{1,0:T(8,128)(2,1)S(1)} collective-permute-done((bf16[64,1000]{1,0:T(8,128)(2,1)S(1)}, bf16[64,1000]{1,0:T(8,128)(2,1)S(1)}, u32[]{:S(2)}, u32[]{:S(2)}) %collective-permute-start.1) | collective-permute-done | bytes 128032 | tf_op jit(solution)/shard_map/ppermute | solution.py:467
  20.4 11.4 %all-to-all-done = bf16[32,11,4,128]{3,2,1,0:T(4,128)(2,1)S(1)} async-done(((bf16[32,11,4,128]{3,2,1,0:T(4,128)(2,1)}), bf16[32,11,4,128]{3,2,1,0:T(4,128)(2,1)S(1)}, u32[]{:S(2)}, u32[]{:S(2)}) %all-to-all-start) | async-done | bytes 360480 | tf_op jit(solution)/shard_map/all_to_all | solution.py:477
  32.1 0.7 %broadcast_in_dim.7 = f32[32,4,512]{2,1,0:T(4,128)} broadcast(f32[4,512]{1,0:T(4,128)S(1)} %pad_dynamic-slice_fusion), dimensions={1,2} | broadcast | bytes 270336 | tf_op jit(solution)/shard_map/broadcast_in_dim | solution.py:484
  32.9 2.6 %all-to-all-start.1 = ((f32[32,4,512]{2,1,0:T(4,128)}), f32[32,4,512]{2,1,0:T(4,128)S(1)}, u32[]{:S(2)}, u32[]{:S(2)}) async-start(f32[32,4,512]{2,1,0:T(4,128)} %broadcast_in_dim.7), calls=%async_computation.1 | async-start | bytes 524288 | tf_op jit(solution)/shard_map/all_to_all | solution.py:483
  35.8 0.2 fusion.30
  36.1 0.2 fusion
  36.4 10.0 %all-to-all-done.1 = f32[32,4,512]{2,1,0:T(4,128)S(1)} async-done(((f32[32,4,512]{2,1,0:T(4,128)}), f32[32,4,512]{2,1,0:T(4,128)S(1)}, u32[]{:S(2)}, u32[]{:S(2)}) %all-to-all-start.1) | async-done | bytes 262176 | tf_op jit(solution)/shard_map/all_to_all | solution.py:483
  47.1 0.7 %pad_maximum_fusion.1 = bf16[32,4,4,128]{3,2,1,0:T(4,128)(2,1)} fusion(bf16[32,1,4,128]{3,2,1,0:T(4,128)(2,1)S(1)} %broadcast_in_dim.8, bf16[32,3,4,128]{3,2,1,0:T(4,128)(2,1)S(1)} %bitcast.39), kind=kLoop, calls=%fused_computation.10 | loop fusion | flops 65536 | bytes 262144 | tf_op jit(solution)/shard_map/concatenate | solution.py:507
  47.9 2.6 %all-to-all-start.2 = ((bf16[32,4,4,128]{3,2,1,0:T(4,128)(2,1)}), bf16[32,4,4,128]{3,2,1,0:T(4,128)(2,1)S(1)}, u32[]{:S(2)}, u32[]{:S(2)}) async-start(bf16[32,4,4,128]{3,2,1,0:T(4,128)(2,1)} %pad_maximum_fusion.1), calls=%async_computation.2 | async-start | bytes 262144 | tf_op jit(solution)/shard_map/all_to_all | solution.py:506
  50.5 8.3 %all-to-all-done.2.second_ref = bf16[32,4,4,128]{3,2,1,0:T(4,128)(2,1)S(1)} async-done(((bf16[32,4,4,128]{3,2,1,0:T(4,128)(2,1)}), bf16[32,4,4,128]{3,2,1,0:T(4,128)(2,1)S(1)}, u32[]{:S(2)}, u32[]{:S(2)}) %all-to-all-start.2) | async-done | bytes 131104 | tf_op jit(solution)/shard_map/all_to_all | solution.py:506
  58.8 4.7 %backward.1 = (bf16[8,2,4,128]{3,2,1,0:T(4,128)(2,1)}, bf16[8,2048]{1,0:T(8,128)(2,1)S(1)}) custom-call(bf16[32,4,4,128]{3,2,1,0:T(4,128)(2,1)S(1)} %all-to-all-done.2.second_ref, f32[128,1024]{1,0:T(8,128)S(1)} %get-tuple-element.11.slope_ref, bf16[128,1024]{1,0:T(8,128)(2,1)S(1)} %get-tuple-element.12.joint_ref, bf16[2048,2048]{1,0:T(8,128)(2,1)} %down_hbm.3), custom_call_target="tpu_custom_call" | custom-call | tf_op jit(solution)/shard_map/backward/pallas_call | solution.py:434
  63.5 3.3 %all-to-all-start.3 = ((bf16[8,2,4,128]{3,2,1,0:T(4,128)(2,1)}), bf16[8,2,4,128]{3,2,1,0:T(4,128)(2,1)S(1)}, u32[]{:S(2)}, u32[]{:S(2)}) async-start(bf16[8,2,4,128]{3,2,1,0:T(4,128)(2,1)} %get-tuple-element.13), calls=%async_computation.3 | async-start | bytes 32768 | tf_op jit(solution)/shard_map/all_to_all | solution.py:514
  67.1 4.4 %all-to-all-done.3 = bf16[8,2,4,128]{3,2,1,0:T(4,128)(2,1)S(1)} async-done(((bf16[8,2,4,128]{3,2,1,0:T(4,128)(2,1)}), bf16[8,2,4,128]{3,2,1,0:T(4,128)(2,1)S(1)}, u32[]{:S(2)}, u32[]{:S(2)}) %all-to-all-start.3) | async-done | bytes 16416 | tf_op jit(solution)/shard_map/all_to_all | solution.py:514
  71.6 0.8 %fusion.1 = bf16[4,4,64]{2,1,0:T(4,128)(2,1)} fusion(bf16[4,4,3072]{2,1,0:T(4,128)(2,1)S(1)} %bitcast.45, bf16[3072,64]{0,1:T(8,128)(2,1)S(1)} %copy-done, f32[4,4,64]{2,1,0:T(4,128)S(1)} %bitcast.48, f32[4,64]{1,0:T(4,128)S(1)} %slice_add_fusion.4, f32[4]{0:T(128)S(1)} %sqrt_multiply_fusion), kind=kOutput, calls=%fused_computation.4 | convolution fusion | flops 6295552 | bytes 498704 | tf_op jit(solution)/shard_map/dot_general | solution.py:511
  (45 shorter events, 1.8 us)
Async XLA Ops:
  0.0 71.6 %copy-start = (bf16[3072,64]{0,1:T(8,128)(2,1)S(1)}, bf16[3072,64]{0,1:T(8,128)(2,1)}, u32[]{:S(2)}) copy-start(bf16[3072,64]{0,1:T(8,128)(2,1)} %param.13) | copy-start | bytes 1179652
  0.0 1.5 %collective-permute-start = (bf16[4,16,64]{2,1,0:T(8,128)(2,1)}, bf16[4,16,64]{2,1,0:T(8,128)(2,1)S(1)}, u32[]{:S(2)}, u32[]{:S(2)}) collective-permute-start(bf16[4,16,64]{2,1,0:T(8,128)(2,1)} %own_hbm.1), channel_id=1, source_target_pairs={{0,4},{1,5},{2,6},{3,7},{4,0},{5,1},{6,2},{7,3},{8,12},{9,13},{10,... | collective-permute-start | bytes 24584 | tf_op jit(solution)/shard_map/ppermute | solution.py:471
  1.5 0.9 %copy-start.1 = (bf16[64,2048]{1,0:T(8,128)(2,1)S(1)}, bf16[64,2048]{1,0:T(8,128)(2,1)}, u32[]{:S(2)}) copy-start(bf16[64,2048]{1,0:T(8,128)(2,1)} %embed_hbm.1) | copy-start | bytes 786436
  2.5 1.0 %copy-start.3 = (bf16[3,4,4,3072]{3,2,1,0:T(4,128)(2,1)S(1)}, bf16[3,4,4,3072]{3,2,1,0:T(4,128)(2,1)}, u32[]{:S(2)}) copy-start(bf16[3,4,4,3072]{3,2,1,0:T(4,128)(2,1)} %qkv_hbm.1) | copy-start | bytes 884740
  3.5 0.7 copy-start.4
  4.2 0.7 copy-start.5
  4.9 0.7 copy-start.6
  5.6 13.4 %copy-start.7 = (bf16[64,1000]{1,0:T(8,128)(2,1)S(1)}, bf16[64,1000]{1,0:T(8,128)(2,1)}, u32[]{:S(2)}) copy-start(bf16[64,1000]{1,0:T(8,128)(2,1)} %param.18) | copy-start | bytes 384004
  5.6 41.2 %copy-start.8 = (s32[4]{0:T(128)S(1)}, s32[4]{0:T(128)}, u32[]{:S(2)}) copy-start(s32[4]{0:T(128)} %param.19) | copy-start | bytes 52
  5.6 44.9 %copy-start.9 = (s32[4]{0:T(128)S(1)}, s32[4]{0:T(128)}, u32[]{:S(2)}) copy-start(s32[4]{0:T(128)} %param.20) | copy-start | bytes 52
  11.7 55.1 %copy-start.2 = (bf16[64,2048]{1,0:T(8,128)(2,1)S(1)}, bf16[64,2048]{1,0:T(8,128)(2,1)}, u32[]{:S(2)}) copy-start(bf16[64,2048]{1,0:T(8,128)(2,1)} %embed_hbm.1) | copy-start | bytes 786436
  11.7 20.1 %all-to-all-start = ((bf16[32,11,4,128]{3,2,1,0:T(4,128)(2,1)}), bf16[32,11,4,128]{3,2,1,0:T(4,128)(2,1)S(1)}, u32[]{:S(2)}, u32[]{:S(2)}) async-start(bf16[32,11,4,128]{3,2,1,0:T(4,128)(2,1)} %get-tuple-element.10), calls=%async_computation | async-start | bytes 720896 | tf_op jit(solution)/shard_map/all_to_all | solution.py:477
  18.9 1.4 %collective-permute-start.1 = (bf16[64,1000]{1,0:T(8,128)(2,1)S(1)}, bf16[64,1000]{1,0:T(8,128)(2,1)S(1)}, u32[]{:S(2)}, u32[]{:S(2)}) collective-permute-start(bf16[64,1000]{1,0:T(8,128)(2,1)S(1)} %copy-done.7), channel_id=1, source_target_pairs={{0,4},{1,5},{2,6},{3,7},{4,0},{5,1},{6,2},{7,3},{8,12},{9,13},{10,... | collective-permute-start | bytes 384008 | tf_op jit(solution)/shard_map/ppermute | solution.py:467
  32.9 13.5 %all-to-all-start.1 = ((f32[32,4,512]{2,1,0:T(4,128)}), f32[32,4,512]{2,1,0:T(4,128)S(1)}, u32[]{:S(2)}, u32[]{:S(2)}) async-start(f32[32,4,512]{2,1,0:T(4,128)} %broadcast_in_dim.7), calls=%async_computation.1 | async-start | bytes 524288 | tf_op jit(solution)/shard_map/all_to_all | solution.py:483
  47.9 10.9 %all-to-all-start.2 = ((bf16[32,4,4,128]{3,2,1,0:T(4,128)(2,1)}), bf16[32,4,4,128]{3,2,1,0:T(4,128)(2,1)S(1)}, u32[]{:S(2)}, u32[]{:S(2)}) async-start(bf16[32,4,4,128]{3,2,1,0:T(4,128)(2,1)} %pad_maximum_fusion.1), calls=%async_computation.2 | async-start | bytes 262144 | tf_op jit(solution)/shard_map/all_to_all | solution.py:506
  63.5 8.0 %all-to-all-start.3 = ((bf16[8,2,4,128]{3,2,1,0:T(4,128)(2,1)}), bf16[8,2,4,128]{3,2,1,0:T(4,128)(2,1)S(1)}, u32[]{:S(2)}, u32[]{:S(2)}) async-start(bf16[8,2,4,128]{3,2,1,0:T(4,128)(2,1)} %get-tuple-element.13), calls=%async_computation.3 | async-start | bytes 32768 | tf_op jit(solution)/shard_map/all_to_all | solution.py:514

commit v4 on v3

--- a/solution.py
+++ b/solution.py
@@ -154,6 +154,13 @@
 LANES = 128
 
 
+KEPT = 1
+
+
+def in_hbm(*arrays):
+    return [pltpu.with_memory_space_constraint(array, pltpu.HBM) for array in arrays]
+
+
 def lane_frequencies():
     frame_width = HEAD_DIM // 8
     plane_width = (HEAD_DIM - frame_width) // 2
@@ -169,8 +176,8 @@
 
 def forward_kernel(
     sizes,
-    pos_ref,
-    table_ref,
+    pos_hbm,
+    table_hbm,
     qkv_hbm,
     own_hbm,
     other_hbm,
@@ -180,6 +187,9 @@
     pay_ref,
     slope_ref,
     joint_ref,
+    keep_ref,
+    pos_ref,
+    table_ref,
     qkv_ref,
     lat_ref,
     embed_ref,
@@ -194,34 +204,45 @@
     per_sample = count // samples
     heads_dev = width // HEAD_DIM // per_sample
     tok_seq, lat = own_hbm.shape[1:]
-    units = down_ref.shape[0]
+    units = slope_ref.shape[1]
     part = units // steps
+    kept = keep_ref.shape[0] // part
     half = lax.axis_index("seq") % 2
 
     def up_copy(step):
         start = pl.multiple_of(half * units + step * part, LANES)
         return pltpu.make_async_copy(
-            up_hbm.at[:, pl.ds(start, part)], up_ref.at[step], sems.at[4 + step]
+            up_hbm.at[:, pl.ds(start, part)], up_ref.at[step], sems.at[6 + step]
         )
+
+    def down_at(step):
+        if step < kept:
+            return keep_ref.at[pl.ds(step * part, part)]
+        return down_ref.at[pl.ds((step - kept) * part, part)]
 
     def down_copy(step):
         start = pl.multiple_of(half * units + step * part, LANES)
         return pltpu.make_async_copy(
             down_hbm.at[pl.ds(start, part)],
-            down_ref.at[pl.ds(step * part, part)],
-            sems.at[4 + steps + step],
+            down_at(step),
+            sems.at[6 + steps + step],
         )
 
     own_copy = pltpu.make_async_copy(own_hbm, lat_ref.at[half], sems.at[0])
     other_copy = pltpu.make_async_copy(other_hbm, lat_ref.at[1 - half], sems.at[1])
     embed_copy = pltpu.make_async_copy(embed_hbm, embed_ref, sems.at[2])
     qkv_copy = pltpu.make_async_copy(qkv_hbm, qkv_ref, sems.at[3])
-    for copy in (own_copy, other_copy, qkv_copy, embed_copy):
+    pos_copy = pltpu.make_async_copy(pos_hbm, pos_ref, sems.at[4])
+    table_copy = pltpu.make_async_copy(table_hbm, table_ref, sems.at[5])
+    for copy in (pos_copy, table_copy, own_copy, other_copy, qkv_copy, embed_copy):
         copy.start()
     for step in range(steps):
         up_copy(step).start()
     for step in range(steps):
         down_copy(step).start()
+
+    pos_copy.wait()
+    table_copy.wait()
 
     shape = (samples * tok_dev, LANES)
     row = lax.broadcasted_iota(jnp.int32, shape, 0)
@@ -293,7 +314,7 @@
         down_copy(step).wait()
         total = total + jnp.dot(
             parts[step],
-            down_ref[step * part : (step + 1) * part],
+            down_at(step)[...],
             preferred_element_type=jnp.float32,
         )
     pool = (total[:samples] + total[samples:]) * (1.0 / seq_len)
@@ -325,7 +346,6 @@
     steps = units // 256
     rows = 2 * tok_seq * samples
     any_spec = pl.BlockSpec(memory_space=pl.ANY)
-    hbm_spec = pl.BlockSpec(memory_space=pltpu.HBM)
     vmem_spec = pl.BlockSpec(memory_space=pltpu.VMEM)
     return pl.pallas_call(
         functools.partial(forward_kernel, (n_seq, n_tp, steps, tok_dev * count)),
@@ -333,52 +353,47 @@
             jax.ShapeDtypeStruct((count, groups, tok_dev, LANES), jnp.bfloat16),
             jax.ShapeDtypeStruct((rows, units), jnp.float32),
             jax.ShapeDtypeStruct((2 * lat, units), jnp.bfloat16),
+            jax.ShapeDtypeStruct((KEPT * 256, features), jnp.bfloat16),
         ),
-        in_specs=[
-            pl.BlockSpec(memory_space=pltpu.SMEM),
-            vmem_spec,
-            hbm_spec,
-            any_spec,
-            any_spec,
-            hbm_spec,
-            hbm_spec,
-            hbm_spec,
-        ],
-        out_specs=(vmem_spec,) * 3,
+        in_specs=[any_spec] * 8,
+        out_specs=(vmem_spec,) * 4,
         scratch_shapes=[
+            pltpu.SMEM(positions.shape, jnp.int32),
+            pltpu.VMEM((8, LANES), jnp.float32),
             pltpu.VMEM(qkv.shape, jnp.bfloat16),
             pltpu.VMEM((2,) + own.shape, jnp.bfloat16),
             pltpu.VMEM(embed_w.shape, jnp.bfloat16),
             pltpu.VMEM((steps, features, 256), jnp.bfloat16),
-            pltpu.VMEM((units, features), jnp.bfloat16),
+            pltpu.VMEM((units - KEPT * 256, features), jnp.bfloat16),
             pltpu.VMEM((rows, 2 * lat), jnp.bfloat16),
-            pltpu.SemaphoreType.DMA((4 + 2 * steps,)),
+            pltpu.SemaphoreType.DMA((6 + 2 * steps,)),
         ],
-        compiler_params=pltpu.CompilerParams(vmem_limit_bytes=52 << 20),
+        compiler_params=pltpu.CompilerParams(vmem_limit_bytes=32 << 20),
         cost_estimate=pl.CostEstimate(
             flops=4 * features * units * 64, bytes_accessed=4 * features * units, transcendentals=0
         ),
         name="forward",
-    )(positions, jnp.asarray(lane_frequencies()), qkv, own, other, embed_w, up_w, down_w)
+    )(*in_hbm(positions, jnp.asarray(lane_frequencies()), qkv, own), other, *in_hbm(embed_w, up_w, down_w))
 
 
 def backward_kernel(
-    steps, second_ref, slope_ref, joint_ref, down_hbm, out_ref, dpool_ref, down_ref, sems
+    steps, second_ref, slope_ref, joint_ref, keep_ref, down_hbm, out_ref, dpool_ref, down_ref, sems
 ):
     count, groups, samples, _ = second_ref.shape
-    units = down_ref.shape[0]
+    units = slope_ref.shape[1]
     part = units // steps
+    kept = keep_ref.shape[0] // part
     half = lax.axis_index("seq") % 2
 
     def down_copy(step):
         start = pl.multiple_of(half * units + step * part, LANES)
         return pltpu.make_async_copy(
             down_hbm.at[pl.ds(start, part)],
-            down_ref.at[pl.ds(step * part, part)],
-            sems.at[step],
+            down_ref.at[pl.ds((step - kept) * part, part)],
+            sems.at[step - kept],
         )
 
-    for step in range(steps):
+    for step in range(kept, steps):
         down_copy(step).start()
     rows = slope_ref.shape[0] // samples
     side = lax.broadcasted_iota(jnp.int32, (samples, LANES), 1) < LANES // 2
@@ -392,29 +407,21 @@
         low = (block - high.astype(jnp.float32)).astype(jnp.bfloat16)
         dpool_ref[:, pair * LANES : (pair + 1) * LANES] = jnp.concatenate([high, low], axis=0)
     dpool = dpool_ref[...]
-    pieces = []
+    across = (((1,), (1,)), ((), ()))
+    dx = None
     for step in range(steps):
-        down_copy(step).wait()
-        pieces.append(
-            lax.dot_general(
-                dpool,
-                down_ref[step * part : (step + 1) * part],
-                (((1,), (1,)), ((), ())),
-                preferred_element_type=jnp.float32,
-            )
-        )
-    dact = jnp.concatenate(pieces, axis=1)
-    dact = dact[:samples] + dact[samples:]
-    halves = []
-    for sample in range(samples):
-        dh1 = slope_ref[sample * rows : (sample + 1) * rows] * dact[sample : sample + 1]
-        halves.append(dh1.astype(jnp.bfloat16))
-    dx = lax.dot_general(
-        jnp.concatenate(halves, axis=0),
-        joint_ref[...],
-        (((1,), (1,)), ((), ())),
-        preferred_element_type=jnp.float32,
-    )
+        if step < kept:
+            weights = keep_ref[step * part : (step + 1) * part]
+        else:
+            down_copy(step).wait()
+            weights = down_ref[(step - kept) * part : (step - kept + 1) * part]
+        dact = lax.dot_general(dpool, weights, across, preferred_element_type=jnp.float32)
+        dact = dact[:samples] + dact[samples:]
+        span = slice(step * part, (step + 1) * part)
+        slope = slope_ref[:, span].reshape(samples, rows, part)
+        dh1 = (slope * dact[:, None, :]).reshape(samples * rows, part).astype(jnp.bfloat16)
+        term = lax.dot_general(dh1, joint_ref[:, span], across, preferred_element_type=jnp.float32)
+        dx = term if dx is None else dx + term
     dx = dx + pltpu.roll(dx, LANES // 2, 1)
     side = lax.broadcasted_iota(jnp.int32, (rows, LANES), 1) < LANES // 2
     tok_dev = out_ref.shape[2]
@@ -426,7 +433,7 @@
             out_ref[target, pair] = both[target * tok_dev : (target + 1) * tok_dev].astype(jnp.bfloat16)
 
 
-def backward(second, slope, joint, down, tok_dev):
+def backward(second, slope, joint, keep, down, tok_dev):
     samples = second.shape[2]
     targets = slope.shape[0] // samples // tok_dev
     units, steps = (slope.shape[1], slope.shape[1] // 256)
@@ -437,15 +444,15 @@
             jax.ShapeDtypeStruct((targets, samples // 2, tok_dev, LANES), jnp.bfloat16),
             jax.ShapeDtypeStruct((2 * samples, down.shape[1]), jnp.bfloat16),
         ),
-        in_specs=[vmem_spec] * 3 + [pl.BlockSpec(memory_space=pltpu.HBM)],
+        in_specs=[vmem_spec] * 4 + [pl.BlockSpec(memory_space=pl.ANY)],
         out_specs=(vmem_spec,) * 2,
         scratch_shapes=[
-            pltpu.VMEM((units, down.shape[1]), jnp.bfloat16),
-            pltpu.SemaphoreType.DMA((steps,)),
+            pltpu.VMEM((units - keep.shape[0], down.shape[1]), jnp.bfloat16),
+            pltpu.SemaphoreType.DMA((steps - KEPT,)),
         ],
-        compiler_params=pltpu.CompilerParams(vmem_limit_bytes=52 << 20),
+        compiler_params=pltpu.CompilerParams(vmem_limit_bytes=32 << 20),
         name="backward",
-    )(second, slope, joint, down)
+    )(second, slope, joint, keep, *in_hbm(down))
 
 
 def per_device_fast(qkv, positions, w_proj, latents, embed_w, up_w, down_w, head_w, labels, timesteps):
@@ -471,7 +478,7 @@
     other = lax.ppermute(latents, both, partner)
     head_pair = in_order(head_w).reshape(2 * rows_dev, classes)
 
-    payload, slope, joint = forward(
+    payload, slope, joint, keep = forward(
         qkv, positions, latents, other, embed_w, up_w, down_w, n_seq, n_tp
     )
     moved = lax.all_to_all(payload, both, 0, 0, tiled=True)
@@ -481,7 +488,11 @@
     terms = jnp.pad(split_dot(pooled, head_pair), ((0, 0), (0, padded - classes)))
     terms = lax.dynamic_slice_in_dim(terms, half * (padded // 2), padded // 2, 1)
     terms = lax.all_to_all(
-        jnp.broadcast_to(terms[None], (count,) + terms.shape), both, 0, 0, tiled=True
+        jnp.broadcast_to(terms.astype(jnp.bfloat16)[None], (count,) + terms.shape),
+        both,
+        0,
+        0,
+        tiled=True,
     )
 
     views = moved[:, 2:].reshape(count, 3, heads_dev, tok_dev, HEAD_DIM)
@@ -497,7 +508,8 @@
     attended = (mixed / total[..., None]).astype(jnp.bfloat16)
     attended = attended.reshape(heads_dev, count, tok_dev, HEAD_DIM).transpose(1, 0, 2, 3)
 
-    logits = jnp.sum(terms.reshape(n_seq // 2, 2, n_tp, samples, padded // 2), axis=(0, 2))
+    terms = terms.astype(jnp.float32).reshape(n_seq // 2, 2, n_tp, samples, padded // 2)
+    logits = jnp.sum(terms, axis=(0, 2))
     logits = logits.transpose(1, 0, 2).reshape(samples, padded)[:, :classes]
     probs = jax.nn.softmax(logits, axis=-1)
     onehot = (labels[:, None] == jnp.arange(classes, dtype=jnp.int32)[None, :]).astype(jnp.float32)
@@ -509,7 +521,8 @@
     returned = second[:, :heads_dev].reshape(samples, per_sample, heads_dev, tok_dev, HEAD_DIM)
     returned = returned.transpose(0, 3, 1, 2, 4).reshape(samples, tok_dev, width)
     eps = jnp.dot(returned, w_proj, preferred_element_type=jnp.float32)
-    dx_terms, dpool = backward(second, slope, joint, down_w, tok_dev)
+    eps = lax.optimization_barrier(eps)
+    dx_terms, dpool = backward(second, slope, joint, keep, down_w, tok_dev)
     planes = [[first + k for k in range(2 * n_tp)] for first in range(0, count, 2 * n_tp)]
     dx_terms = lax.all_to_all(dx_terms, both, 0, 0, tiled=True, axis_index_groups=planes)
     dx = jnp.sum(dx_terms.astype(jnp.float32), axis=0)

time: 72.9 us -> 65.5 us (0.90)
  local copies, waits for them, and re-layouts: 5.27 us -> 1.22 us
  waiting for transfers between devices: 36.3 us -> 33.5 us
    unnamed x20 -> x10, local copies, waits for them, and re-layouts: 4.03 us -> 0.02 us
    all_to_all x1, waiting for transfers between devices: 9.99 us -> 7.45 us  [per_device_fast(): lax.all_to_all(jnp.broadcast_to(terms.astype(jnp.bfloat16)[None], (count,...]
where the time goes in v4:
time: 65.5 us; the launch traced here: 65.1 us
  waiting for transfers between devices  33.5 us (51%)
  starting transfers between devices  16.5 us (25%)
  Pallas kernels  10.2 us (16%)
  other arithmetic  2.27 us (3%)
  local copies, waits for them, and re-layouts  1.22 us (2%)
  matrix products  1.14 us (2%)
    all_to_all x1, waiting for transfers between devices, per_device_fast(): moved = lax.all_to_all(payload, both, 0, 0, tiled=True)  11.4 us
    all_to_all x1, waiting for transfers between devices, per_device_fast(): lax.all_to_all(jnp.concatenate([attended, share], axis=1), both, 0, 0, ti...  8.32 us
    all_to_all x1, waiting for transfers between devices, per_device_fast(): lax.all_to_all(jnp.broadcast_to(terms.astype(jnp.bfloat16)[None], (count,...  7.45 us
    all_to_all x1, starting transfers between devices, per_device_fast(): moved = lax.all_to_all(payload, both, 0, 0, tiled=True)  7.18 us
    pallas_call x1, Pallas kernels, forward(): pl.pallas_call(functools.partial(forward_kernel, (n_seq, n_tp, steps, tok...  5.62 us
    pallas_call x1, Pallas kernels, backward(): pl.pallas_call(functools.partial(backward_kernel, steps), out_shape=(jax....  4.61 us
    all_to_all x1, waiting for transfers between devices, per_device_fast(): lax.all_to_all(dx_terms, both, 0, 0, tiled=True, axis_index_groups=planes)  4.16 us
    all_to_all x1, starting transfers between devices, per_device_fast(): lax.all_to_all(dx_terms, both, 0, 0, tiled=True, axis_index_groups=planes)  3.33 us
  transfers between devices with their start and end apart: 6, of which 6 were waited for; matrix products, arithmetic and copies ran while one was open for 2% of the time, Pallas kernels for 0%

profile of v4, /device:TPU:0, one launch (start us, length us, event | category | flops | bytes accessed | tf_op | source)
XLA Modules:
  0.0 65.1 jit_solution(7743177501188030010)
XLA Ops:
  0.0 0.6 collective-permute-start
  0.6 1.0 %collective-permute-done.other_hbm = bf16[4,16,64]{2,1,0:T(8,128)(2,1)S(1)} collective-permute-done((bf16[4,16,64]{2,1,0:T(8,128)(2,1)}, bf16[4,16,64]{2,1,0:T(8,128)(2,1)S(1)}, u32[]{:S(2)}, u32[]{:S(2)}) %collective-permute-start) | collective-permute-done | bytes 8224 | tf_op jit(solution)/shard_map/ppermute | solution.py:478
  1.6 5.6 %forward.1 = (bf16[32,11,4,128]{3,2,1,0:T(4,128)(2,1)}, f32[128,1024]{1,0:T(8,128)S(1)}, bf16[128,1024]{1,0:T(8,128)(2,1)S(1)}, bf16[256,2048]{1,0:T(8,128)(2,1)S(1)}) custom-call(s32[3,4,4]{2,1,0:T(4,128)} %pos_hbm.1, f32[8,128]{1,0:T(8,128)} %constant.48.clone.table_hbm, bf16[3,4,4,3072]{3,2,1,0:T(4,128)(2,1)} %qkv_hbm.1, bf16[4,16,64]{2,1,0:T(8,128)(2,1)} %own_hbm.1, ...), custom_call_target="tpu_custom_call" | custom-call | flops 536870912 | bytes 8388608 | tf_op jit(solution)/shard_map/forward/pallas_call | solution.py:350
  7.3 7.2 %all-to-all-start = ((bf16[32,11,4,128]{3,2,1,0:T(4,128)(2,1)}), bf16[32,11,4,128]{3,2,1,0:T(4,128)(2,1)S(1)}, u32[]{:S(2)}, u32[]{:S(2)}) async-start(bf16[32,11,4,128]{3,2,1,0:T(4,128)(2,1)} %get-tuple-element.11), calls=%async_computation | async-start | bytes 720896 | tf_op jit(solution)/shard_map/all_to_all | solution.py:484
  14.5 0.3 collective-permute-start.1
  14.8 1.1 %collective-permute-done.1 = bf16[64,1000]{1,0:T(8,128)(2,1)S(1)} collective-permute-done((bf16[64,1000]{1,0:T(8,128)(2,1)S(1)}, bf16[64,1000]{1,0:T(8,128)(2,1)S(1)}, u32[]{:S(2)}, u32[]{:S(2)}) %collective-permute-start.1) | collective-permute-done | bytes 128032 | tf_op jit(solution)/shard_map/ppermute | solution.py:474
  15.9 11.4 %all-to-all-done = bf16[32,11,4,128]{3,2,1,0:T(4,128)(2,1)S(1)} async-done(((bf16[32,11,4,128]{3,2,1,0:T(4,128)(2,1)}), bf16[32,11,4,128]{3,2,1,0:T(4,128)(2,1)S(1)}, u32[]{:S(2)}, u32[]{:S(2)}) %all-to-all-start) | async-done | bytes 360480 | tf_op jit(solution)/shard_map/all_to_all | solution.py:484
  27.5 0.1 fusion.16
  27.7 0.7 %broadcast_in_dim.7 = bf16[32,4,512]{2,1,0:T(4,128)(2,1)} broadcast(bf16[4,512]{1,0:T(4,128)(2,1)S(1)} %fusion.15), dimensions={1,2} | broadcast | bytes 135168 | tf_op jit(solution)/shard_map/broadcast_in_dim | solution.py:491
  28.3 2.6 %all-to-all-start.1 = ((bf16[32,4,512]{2,1,0:T(4,128)(2,1)}), bf16[32,4,512]{2,1,0:T(4,128)(2,1)S(1)}, u32[]{:S(2)}, u32[]{:S(2)}) async-start(bf16[32,4,512]{2,1,0:T(4,128)(2,1)} %broadcast_in_dim.7), calls=%async_computation.1 | async-start | bytes 262144 | tf_op jit(solution)/shard_map/all_to_all | solution.py:490
  31.2 0.2 fusion.31
  31.6 0.2 fusion
  31.8 7.5 %all-to-all-done.1 = bf16[32,4,512]{2,1,0:T(4,128)(2,1)S(1)} async-done(((bf16[32,4,512]{2,1,0:T(4,128)(2,1)}), bf16[32,4,512]{2,1,0:T(4,128)(2,1)S(1)}, u32[]{:S(2)}, u32[]{:S(2)}) %all-to-all-start.1) | async-done | bytes 131104 | tf_op jit(solution)/shard_map/all_to_all | solution.py:490
  39.5 0.2 fusion.13
  39.8 0.1 fusion.7
  40.1 0.7 %pad_maximum_fusion.1 = bf16[32,4,4,128]{3,2,1,0:T(4,128)(2,1)} fusion(bf16[32,1,4,128]{3,2,1,0:T(4,128)(2,1)S(1)} %broadcast_in_dim.8, bf16[32,3,4,128]{3,2,1,0:T(4,128)(2,1)S(1)} %bitcast.40), kind=kLoop, calls=%fused_computation.10 | loop fusion | flops 65536 | bytes 262144 | tf_op jit(solution)/shard_map/concatenate | solution.py:519
  40.8 2.6 %all-to-all-start.2 = ((bf16[32,4,4,128]{3,2,1,0:T(4,128)(2,1)}), bf16[32,4,4,128]{3,2,1,0:T(4,128)(2,1)S(1)}, u32[]{:S(2)}, u32[]{:S(2)}) async-start(bf16[32,4,4,128]{3,2,1,0:T(4,128)(2,1)} %pad_maximum_fusion.1), calls=%async_computation.2 | async-start | bytes 262144 | tf_op jit(solution)/shard_map/all_to_all | solution.py:518
  43.4 8.3 %all-to-all-done.2.second_ref = bf16[32,4,4,128]{3,2,1,0:T(4,128)(2,1)S(1)} async-done(((bf16[32,4,4,128]{3,2,1,0:T(4,128)(2,1)}), bf16[32,4,4,128]{3,2,1,0:T(4,128)(2,1)S(1)}, u32[]{:S(2)}, u32[]{:S(2)}) %all-to-all-start.2) | async-done | bytes 131104 | tf_op jit(solution)/shard_map/all_to_all | solution.py:518
  51.8 4.6 %backward.1 = (bf16[8,2,4,128]{3,2,1,0:T(4,128)(2,1)}, bf16[8,2048]{1,0:T(8,128)(2,1)S(1)}) custom-call(bf16[32,4,4,128]{3,2,1,0:T(4,128)(2,1)S(1)} %all-to-all-done.2.second_ref, f32[128,1024]{1,0:T(8,128)S(1)} %get-tuple-element.12.slope_ref, bf16[128,1024]{1,0:T(8,128)(2,1)S(1)} %get-tuple-element.13.joint_ref, ...), custom_call_target="tpu_custom_call" | custom-call | tf_op jit(solution)/shard_map/backward/pallas_call | solution.py:441
  56.4 3.3 %all-to-all-start.3 = ((bf16[8,2,4,128]{3,2,1,0:T(4,128)(2,1)}), bf16[8,2,4,128]{3,2,1,0:T(4,128)(2,1)S(1)}, u32[]{:S(2)}, u32[]{:S(2)}) async-start(bf16[8,2,4,128]{3,2,1,0:T(4,128)(2,1)} %get-tuple-element.15), calls=%async_computation.3 | async-start | bytes 32768 | tf_op jit(solution)/shard_map/all_to_all | solution.py:527
  59.7 0.2 fusion.32
  60.0 0.2 fusion.1
  60.2 4.2 %all-to-all-done.3 = bf16[8,2,4,128]{3,2,1,0:T(4,128)(2,1)S(1)} async-done(((bf16[8,2,4,128]{3,2,1,0:T(4,128)(2,1)}), bf16[8,2,4,128]{3,2,1,0:T(4,128)(2,1)S(1)}, u32[]{:S(2)}, u32[]{:S(2)}) %all-to-all-start.3) | async-done | bytes 16416 | tf_op jit(solution)/shard_map/all_to_all | solution.py:527
  64.5 0.7 %subtract_convert_fusion.1 = bf16[4,4,64]{2,1,0:T(4,128)(2,1)} fusion(f32[4,4,64]{2,1,0:T(4,128)S(1)} %fusion.1, f32[4,4,64]{2,1,0:T(4,128)S(1)} %bitcast.49, f32[4,64]{1,0:T(4,128)S(1)} %slice_add_fusion.4, f32[4]{0:T(128)S(1)} %sqrt_multiply_fusion), kind=kLoop, calls=%fused_computation.36 | loop fusion | flops 4096 | bytes 11280 | tf_op jit(solution)/shard_map/convert_element_type | solution.py:538
  (36 shorter events, 1.2 us)
Async XLA Ops:
  0.0 59.9 %copy-start = (bf16[3072,64]{0,1:T(8,128)(2,1)S(1)}, bf16[3072,64]{0,1:T(8,128)(2,1)}, u32[]{:S(2)}) copy-start(bf16[3072,64]{0,1:T(8,128)(2,1)} %param.13) | copy-start | bytes 1179652
  0.0 14.4 %copy-start.2 = (bf16[64,1000]{1,0:T(8,128)(2,1)S(1)}, bf16[64,1000]{1,0:T(8,128)(2,1)}, u32[]{:S(2)}) copy-start(bf16[64,1000]{1,0:T(8,128)(2,1)} %param.18) | copy-start | bytes 384004
  0.0 39.7 %copy-start.3 = (s32[4]{0:T(128)S(1)}, s32[4]{0:T(128)}, u32[]{:S(2)}) copy-start(s32[4]{0:T(128)} %param.19) | copy-start | bytes 52
  0.0 43.4 %copy-start.4 = (s32[4]{0:T(128)S(1)}, s32[4]{0:T(128)}, u32[]{:S(2)}) copy-start(s32[4]{0:T(128)} %param.20) | copy-start | bytes 52
  0.0 1.6 %collective-permute-start = (bf16[4,16,64]{2,1,0:T(8,128)(2,1)}, bf16[4,16,64]{2,1,0:T(8,128)(2,1)S(1)}, u32[]{:S(2)}, u32[]{:S(2)}) collective-permute-start(bf16[4,16,64]{2,1,0:T(8,128)(2,1)} %own_hbm.1), channel_id=1, source_target_pairs={{0,4},{1,5},{2,6},{3,7},{4,0},{5,1},{6,2},{7,3},{8,12},{9,13},{10,... | collective-permute-start | bytes 24584 | tf_op jit(solution)/shard_map/ppermute | solution.py:478
  7.3 20.1 %all-to-all-start = ((bf16[32,11,4,128]{3,2,1,0:T(4,128)(2,1)}), bf16[32,11,4,128]{3,2,1,0:T(4,128)(2,1)S(1)}, u32[]{:S(2)}, u32[]{:S(2)}) async-start(bf16[32,11,4,128]{3,2,1,0:T(4,128)(2,1)} %get-tuple-element.11), calls=%async_computation | async-start | bytes 720896 | tf_op jit(solution)/shard_map/all_to_all | solution.py:484
  14.5 1.4 %collective-permute-start.1 = (bf16[64,1000]{1,0:T(8,128)(2,1)S(1)}, bf16[64,1000]{1,0:T(8,128)(2,1)S(1)}, u32[]{:S(2)}, u32[]{:S(2)}) collective-permute-start(bf16[64,1000]{1,0:T(8,128)(2,1)S(1)} %copy-done.2), channel_id=1, source_target_pairs={{0,4},{1,5},{2,6},{3,7},{4,0},{5,1},{6,2},{7,3},{8,12},{9,13},{10,... | collective-permute-start | bytes 384008 | tf_op jit(solution)/shard_map/ppermute | solution.py:474
  14.8 44.9 %copy-start.1 = (bf16[64,2048]{1,0:T(8,128)(2,1)S(1)}, bf16[64,2048]{1,0:T(8,128)(2,1)}, u32[]{:S(2)}) copy-start(bf16[64,2048]{1,0:T(8,128)(2,1)} %embed_hbm.1) | copy-start | bytes 786436
  28.3 11.0 %all-to-all-start.1 = ((bf16[32,4,512]{2,1,0:T(4,128)(2,1)}), bf16[32,4,512]{2,1,0:T(4,128)(2,1)S(1)}, u32[]{:S(2)}, u32[]{:S(2)}) async-start(bf16[32,4,512]{2,1,0:T(4,128)(2,1)} %broadcast_in_dim.7), calls=%async_computation.1 | async-start | bytes 262144 | tf_op jit(solution)/shard_map/all_to_all | solution.py:490
  40.8 11.0 %all-to-all-start.2 = ((bf16[32,4,4,128]{3,2,1,0:T(4,128)(2,1)}), bf16[32,4,4,128]{3,2,1,0:T(4,128)(2,1)S(1)}, u32[]{:S(2)}, u32[]{:S(2)}) async-start(bf16[32,4,4,128]{3,2,1,0:T(4,128)(2,1)} %pad_maximum_fusion.1), calls=%async_computation.2 | async-start | bytes 262144 | tf_op jit(solution)/shard_map/all_to_all | solution.py:518
  56.4 8.0 %all-to-all-start.3 = ((bf16[8,2,4,128]{3,2,1,0:T(4,128)(2,1)}), bf16[8,2,4,128]{3,2,1,0:T(4,128)(2,1)S(1)}, u32[]{:S(2)}, u32[]{:S(2)}) async-start(bf16[8,2,4,128]{3,2,1,0:T(4,128)(2,1)} %get-tuple-element.15), calls=%async_computation.3 | async-start | bytes 32768 | tf_op jit(solution)/shard_map/all_to_all | solution.py:527

commit v5 on v4

--- a/solution.py
+++ b/solution.py
@@ -506,7 +506,15 @@
         "hqk,hkd->hqd", weights.astype(jnp.bfloat16), views[2], preferred_element_type=jnp.float32
     )
     attended = (mixed / total[..., None]).astype(jnp.bfloat16)
-    attended = attended.reshape(heads_dev, count, tok_dev, HEAD_DIM).transpose(1, 0, 2, 3)
+    first_row = (seq_index * n_tp + lax.axis_index("tp")) % per_sample * heads_dev * HEAD_DIM
+    proj_mine = lax.dynamic_slice_in_dim(w_proj, first_row, heads_dev * HEAD_DIM, 0)
+    eps_terms = jnp.einsum(
+        "hqd,hdl->ql",
+        attended,
+        proj_mine.reshape(heads_dev, HEAD_DIM, lat),
+        preferred_element_type=jnp.float32,
+    )
+    eps_terms = split_two(eps_terms, 1).reshape(count, 1, tok_dev, 2 * lat)
 
     terms = terms.astype(jnp.float32).reshape(n_seq // 2, 2, n_tp, samples, padded // 2)
     logits = jnp.sum(terms, axis=(0, 2))
@@ -516,11 +524,11 @@
     share = split_two(split_dot(onehot - probs, head_w, 1), 1)
     share = jnp.broadcast_to(share[None, None], (count, 1) + share.shape)
     second = lax.all_to_all(
-        jnp.concatenate([attended, share], axis=1), both, 0, 0, tiled=True
-    )
-    returned = second[:, :heads_dev].reshape(samples, per_sample, heads_dev, tok_dev, HEAD_DIM)
-    returned = returned.transpose(0, 3, 1, 2, 4).reshape(samples, tok_dev, width)
-    eps = jnp.dot(returned, w_proj, preferred_element_type=jnp.float32)
+        jnp.concatenate([eps_terms, share], axis=1), both, 0, 0, tiled=True
+    )
+    eps = second[:, 0].astype(jnp.float32).reshape(samples, per_sample, tok_dev, 2 * lat)
+    eps = jnp.sum(eps, axis=1)
+    eps = eps[..., :lat] + eps[..., lat:]
     eps = lax.optimization_barrier(eps)
     dx_terms, dpool = backward(second, slope, joint, keep, down_w, tok_dev)
     planes = [[first + k for k in range(2 * n_tp)] for first in range(0, count, 2 * n_tp)]

time: 65.5 us -> 64.9 us (level)
    all_to_all x1, waiting for transfers between devices: 8.32 us -> 7.43 us  [per_device_fast(): lax.all_to_all(jnp.concatenate([eps_terms, share], axis=1), both, 0, 0, t...]
where the time goes in v5:
time: 64.9 us; the launch traced here: 64.5 us
  waiting for transfers between devices  32.9 us (51%)
  starting transfers between devices  16.5 us (25%)
  Pallas kernels  10.2 us (16%)
  other arithmetic  2.3 us (4%)
  local copies, waits for them, and re-layouts  1.27 us (2%)
  matrix products  1.08 us (2%)
    all_to_all x1, waiting for transfers between devices, per_device_fast(): moved = lax.all_to_all(payload, both, 0, 0, tiled=True)  11.4 us
    all_to_all x1, waiting for transfers between devices, per_device_fast(): lax.all_to_all(jnp.broadcast_to(terms.astype(jnp.bfloat16)[None], (count,...  7.56 us
    all_to_all x1, waiting for transfers between devices, per_device_fast(): lax.all_to_all(jnp.concatenate([eps_terms, share], axis=1), both, 0, 0, t...  7.43 us
    all_to_all x1, starting transfers between devices, per_device_fast(): moved = lax.all_to_all(payload, both, 0, 0, tiled=True)  7.18 us
    pallas_call x1, Pallas kernels, forward(): pl.pallas_call(functools.partial(forward_kernel, (n_seq, n_tp, steps, tok...  5.6 us
    pallas_call x1, Pallas kernels, backward(): pl.pallas_call(functools.partial(backward_kernel, steps), out_shape=(jax....  4.61 us
    all_to_all x1, waiting for transfers between devices, per_device_fast(): lax.all_to_all(dx_terms, both, 0, 0, tiled=True, axis_index_groups=planes)  4.32 us
    all_to_all x1, starting transfers between devices, per_device_fast(): lax.all_to_all(dx_terms, both, 0, 0, tiled=True, axis_index_groups=planes)  3.33 us
  transfers between devices with their start and end apart: 6, of which 6 were waited for; matrix products, arithmetic and copies ran while one was open for 2% of the time, Pallas kernels for 0%

profile of v5, /device:TPU:0, one launch (start us, length us, event | category | flops | bytes accessed | tf_op | source)
XLA Modules:
  0.0 64.5 jit_solution(706619220719277702)
XLA Ops:
  0.0 0.6 collective-permute-start
  0.6 1.0 %collective-permute-done.other_hbm = bf16[4,16,64]{2,1,0:T(8,128)(2,1)S(1)} collective-permute-done((bf16[4,16,64]{2,1,0:T(8,128)(2,1)}, bf16[4,16,64]{2,1,0:T(8,128)(2,1)S(1)}, u32[]{:S(2)}, u32[]{:S(2)}) %collective-permute-start) | collective-permute-done | bytes 8224 | tf_op jit(solution)/shard_map/ppermute | solution.py:478
  1.6 5.6 %forward.1 = (bf16[32,11,4,128]{3,2,1,0:T(4,128)(2,1)}, f32[128,1024]{1,0:T(8,128)S(1)}, bf16[128,1024]{1,0:T(8,128)(2,1)S(1)}, bf16[256,2048]{1,0:T(8,128)(2,1)S(1)}) custom-call(s32[3,4,4]{2,1,0:T(4,128)} %pos_hbm.1, f32[8,128]{1,0:T(8,128)} %constant.69.clone.table_hbm, bf16[3,4,4,3072]{3,2,1,0:T(4,128)(2,1)} %qkv_hbm.1, bf16[4,16,64]{2,1,0:T(8,128)(2,1)} %own_hbm.1, ...), custom_call_target="tpu_custom_call" | custom-call | flops 536870912 | bytes 8388608 | tf_op jit(solution)/shard_map/forward/pallas_call | solution.py:350
  7.2 7.2 %all-to-all-start = ((bf16[32,11,4,128]{3,2,1,0:T(4,128)(2,1)}), bf16[32,11,4,128]{3,2,1,0:T(4,128)(2,1)S(1)}, u32[]{:S(2)}, u32[]{:S(2)}) async-start(bf16[32,11,4,128]{3,2,1,0:T(4,128)(2,1)} %get-tuple-element.11), calls=%async_computation | async-start | bytes 720896 | tf_op jit(solution)/shard_map/all_to_all | solution.py:484
  14.4 0.3 collective-permute-start.1
  14.8 1.1 %collective-permute-done.1 = bf16[64,1000]{1,0:T(8,128)(2,1)S(1)} collective-permute-done((bf16[64,1000]{1,0:T(8,128)(2,1)S(1)}, bf16[64,1000]{1,0:T(8,128)(2,1)S(1)}, u32[]{:S(2)}, u32[]{:S(2)}) %collective-permute-start.1) | collective-permute-done | bytes 128032 | tf_op jit(solution)/shard_map/ppermute | solution.py:474
  15.9 11.4 %all-to-all-done = bf16[32,11,4,128]{3,2,1,0:T(4,128)(2,1)S(1)} async-done(((bf16[32,11,4,128]{3,2,1,0:T(4,128)(2,1)}), bf16[32,11,4,128]{3,2,1,0:T(4,128)(2,1)S(1)}, u32[]{:S(2)}, u32[]{:S(2)}) %all-to-all-start) | async-done | bytes 360480 | tf_op jit(solution)/shard_map/all_to_all | solution.py:484
  27.8 0.1 fusion.21
  28.0 0.7 %broadcast_in_dim.7 = bf16[32,4,512]{2,1,0:T(4,128)(2,1)} broadcast(bf16[4,512]{1,0:T(4,128)(2,1)S(1)} %fusion.20), dimensions={1,2} | broadcast | bytes 135168 | tf_op jit(solution)/shard_map/broadcast_in_dim | solution.py:491
  28.7 2.6 %all-to-all-start.1 = ((bf16[32,4,512]{2,1,0:T(4,128)(2,1)}), bf16[32,4,512]{2,1,0:T(4,128)(2,1)S(1)}, u32[]{:S(2)}, u32[]{:S(2)}) async-start(bf16[32,4,512]{2,1,0:T(4,128)(2,1)} %broadcast_in_dim.7), calls=%async_computation.1 | async-start | bytes 262144 | tf_op jit(solution)/shard_map/all_to_all | solution.py:490
  31.2 0.2 fusion.36
  31.5 0.4 subtract_convert_fusion
  32.0 7.6 %all-to-all-done.1 = bf16[32,4,512]{2,1,0:T(4,128)(2,1)S(1)} async-done(((bf16[32,4,512]{2,1,0:T(4,128)(2,1)}), bf16[32,4,512]{2,1,0:T(4,128)(2,1)S(1)}, u32[]{:S(2)}, u32[]{:S(2)}) %all-to-all-start.1) | async-done | bytes 131104 | tf_op jit(solution)/shard_map/all_to_all | solution.py:490
  39.7 0.1 slice_reduce_fusion
  39.8 0.2 fusion.18
  40.1 0.1 fusion.12
  40.4 0.7 %pad_maximum_fusion.1 = bf16[32,2,4,128]{3,2,1,0:T(4,128)(2,1)} fusion(bf16[32,1,4,128]{3,2,1,0:T(4,128)(2,1)S(1)} %broadcast_in_dim.8, bf16[32,1,4,128]{3,2,1,0:T(4,128)(2,1)S(1)} %bitcast.51), kind=kLoop, calls=%fused_computation.16 | loop fusion | flops 32768 | bytes 131072 | tf_op jit(solution)/shard_map/concatenate | solution.py:527
  41.0 2.6 %all-to-all-start.2 = ((bf16[32,2,4,128]{3,2,1,0:T(4,128)(2,1)}), bf16[32,2,4,128]{3,2,1,0:T(4,128)(2,1)S(1)}, u32[]{:S(2)}, u32[]{:S(2)}) async-start(bf16[32,2,4,128]{3,2,1,0:T(4,128)(2,1)} %pad_maximum_fusion.1), calls=%async_computation.2 | async-start | bytes 131072 | tf_op jit(solution)/shard_map/all_to_all | solution.py:526
  43.7 7.4 %all-to-all-done.2.second_ref = bf16[32,2,4,128]{3,2,1,0:T(4,128)(2,1)S(1)} async-done(((bf16[32,2,4,128]{3,2,1,0:T(4,128)(2,1)}), bf16[32,2,4,128]{3,2,1,0:T(4,128)(2,1)S(1)}, u32[]{:S(2)}, u32[]{:S(2)}) %all-to-all-start.2) | async-done | bytes 65568 | tf_op jit(solution)/shard_map/all_to_all | solution.py:526
  51.1 4.6 %backward.1 = (bf16[8,2,4,128]{3,2,1,0:T(4,128)(2,1)}, bf16[8,2048]{1,0:T(8,128)(2,1)S(1)}) custom-call(bf16[32,2,4,128]{3,2,1,0:T(4,128)(2,1)S(1)} %all-to-all-done.2.second_ref, f32[128,1024]{1,0:T(8,128)S(1)} %get-tuple-element.12.slope_ref, bf16[128,1024]{1,0:T(8,128)(2,1)S(1)} %get-tuple-element.13.joint_ref, ...), custom_call_target="tpu_custom_call" | custom-call | tf_op jit(solution)/shard_map/backward/pallas_call | solution.py:441
  55.7 3.3 %all-to-all-start.3 = ((bf16[8,2,4,128]{3,2,1,0:T(4,128)(2,1)}), bf16[8,2,4,128]{3,2,1,0:T(4,128)(2,1)S(1)}, u32[]{:S(2)}, u32[]{:S(2)}) async-start(bf16[8,2,4,128]{3,2,1,0:T(4,128)(2,1)} %get-tuple-element.15), calls=%async_computation.3 | async-start | bytes 32768 | tf_op jit(solution)/shard_map/all_to_all | solution.py:535
  59.1 0.2 fusion.39
  59.4 4.3 %all-to-all-done.3 = bf16[8,2,4,128]{3,2,1,0:T(4,128)(2,1)S(1)} async-done(((bf16[8,2,4,128]{3,2,1,0:T(4,128)(2,1)}), bf16[8,2,4,128]{3,2,1,0:T(4,128)(2,1)S(1)}, u32[]{:S(2)}, u32[]{:S(2)}) %all-to-all-start.3) | async-done | bytes 16416 | tf_op jit(solution)/shard_map/all_to_all | solution.py:535
  63.8 0.7 %subtract_convert_fusion.2 = bf16[4,4,64]{2,1,0:T(4,128)(2,1)} fusion(f32[4,4,64]{2,1,0:T(4,128)S(1)} %slice_add_fusion.2, f32[4,4,64]{2,1,0:T(4,128)S(1)} %bitcast.53, f32[4,64]{1,0:T(4,128)S(1)} %slice_add_fusion.5, f32[4]{0:T(128)S(1)} %sqrt_multiply_fusion), kind=kLoop, calls=%fused_computation.44 | loop fusion | flops 4096 | bytes 11280 | tf_op jit(solution)/shard_map/convert_element_type | solution.py:546
  (36 shorter events, 1.2 us)
Async XLA Ops:
  0.0 31.5 %copy-start = (bf16[3072,64]{0,1:T(8,128)(2,1)S(1)}, bf16[3072,64]{0,1:T(8,128)(2,1)}, u32[]{:S(2)}) copy-start(bf16[3072,64]{0,1:T(8,128)(2,1)} %param.13) | copy-start | bytes 1179652
  0.0 14.4 %copy-start.2 = (bf16[64,1000]{1,0:T(8,128)(2,1)S(1)}, bf16[64,1000]{1,0:T(8,128)(2,1)}, u32[]{:S(2)}) copy-start(bf16[64,1000]{1,0:T(8,128)(2,1)} %param.18) | copy-start | bytes 384004
  0.0 40.0 %copy-start.3 = (s32[4]{0:T(128)S(1)}, s32[4]{0:T(128)}, u32[]{:S(2)}) copy-start(s32[4]{0:T(128)} %param.19) | copy-start | bytes 52
  0.0 43.6 %copy-start.4 = (s32[4]{0:T(128)S(1)}, s32[4]{0:T(128)}, u32[]{:S(2)}) copy-start(s32[4]{0:T(128)} %param.20) | copy-start | bytes 52
  0.0 1.6 %collective-permute-start = (bf16[4,16,64]{2,1,0:T(8,128)(2,1)}, bf16[4,16,64]{2,1,0:T(8,128)(2,1)S(1)}, u32[]{:S(2)}, u32[]{:S(2)}) collective-permute-start(bf16[4,16,64]{2,1,0:T(8,128)(2,1)} %own_hbm.1), channel_id=1, source_target_pairs={{0,4},{1,5},{2,6},{3,7},{4,0},{5,1},{6,2},{7,3},{8,12},{9,13},{10,... | collective-permute-start | bytes 24584 | tf_op jit(solution)/shard_map/ppermute | solution.py:478
  7.2 20.1 %all-to-all-start = ((bf16[32,11,4,128]{3,2,1,0:T(4,128)(2,1)}), bf16[32,11,4,128]{3,2,1,0:T(4,128)(2,1)S(1)}, u32[]{:S(2)}, u32[]{:S(2)}) async-start(bf16[32,11,4,128]{3,2,1,0:T(4,128)(2,1)} %get-tuple-element.11), calls=%async_computation | async-start | bytes 720896 | tf_op jit(solution)/shard_map/all_to_all | solution.py:484
  14.4 44.6 %copy-start.1 = (bf16[64,2048]{1,0:T(8,128)(2,1)S(1)}, bf16[64,2048]{1,0:T(8,128)(2,1)}, u32[]{:S(2)}) copy-start(bf16[64,2048]{1,0:T(8,128)(2,1)} %embed_hbm.1) | copy-start | bytes 786436
  14.4 1.4 %collective-permute-start.1 = (bf16[64,1000]{1,0:T(8,128)(2,1)S(1)}, bf16[64,1000]{1,0:T(8,128)(2,1)S(1)}, u32[]{:S(2)}, u32[]{:S(2)}) collective-permute-start(bf16[64,1000]{1,0:T(8,128)(2,1)S(1)} %copy-done.2), channel_id=1, source_target_pairs={{0,4},{1,5},{2,6},{3,7},{4,0},{5,1},{6,2},{7,3},{8,12},{9,13},{10,... | collective-permute-start | bytes 384008 | tf_op jit(solution)/shard_map/ppermute | solution.py:474
  28.7 11.0 %all-to-all-start.1 = ((bf16[32,4,512]{2,1,0:T(4,128)(2,1)}), bf16[32,4,512]{2,1,0:T(4,128)(2,1)S(1)}, u32[]{:S(2)}, u32[]{:S(2)}) async-start(bf16[32,4,512]{2,1,0:T(4,128)(2,1)} %broadcast_in_dim.7), calls=%async_computation.1 | async-start | bytes 262144 | tf_op jit(solution)/shard_map/all_to_all | solution.py:490
  41.0 10.1 %all-to-all-start.2 = ((bf16[32,2,4,128]{3,2,1,0:T(4,128)(2,1)}), bf16[32,2,4,128]{3,2,1,0:T(4,128)(2,1)S(1)}, u32[]{:S(2)}, u32[]{:S(2)}) async-start(bf16[32,2,4,128]{3,2,1,0:T(4,128)(2,1)} %pad_maximum_fusion.1), calls=%async_computation.2 | async-start | bytes 131072 | tf_op jit(solution)/shard_map/all_to_all | solution.py:526
  55.7 8.0 %all-to-all-start.3 = ((bf16[8,2,4,128]{3,2,1,0:T(4,128)(2,1)}), bf16[8,2,4,128]{3,2,1,0:T(4,128)(2,1)S(1)}, u32[]{:S(2)}, u32[]{:S(2)}) async-start(bf16[8,2,4,128]{3,2,1,0:T(4,128)(2,1)} %get-tuple-element.15), calls=%async_computation.3 | async-start | bytes 32768 | tf_op jit(solution)/shard_map/all_to_all | solution.py:535

commit v6 on v5

--- a/solution.py
+++ b/solution.py
@@ -126,12 +126,15 @@
     return (eps - scale[:, None, None] * dx_total).astype(jnp.bfloat16)
 
 
+def rounded(values):
+    return lax.reduce_precision(values, exponent_bits=8, mantissa_bits=7)
+
+
 def split_rows(values):
-    high = values.astype(jnp.bfloat16)
-    rest = values - high.astype(jnp.float32)
-    middle = rest.astype(jnp.bfloat16)
-    low = (rest - middle.astype(jnp.float32)).astype(jnp.bfloat16)
-    return jnp.concatenate([high, middle, low], axis=0)
+    high = rounded(values)
+    middle = rounded(values - high)
+    low = values - high - middle
+    return jnp.concatenate([high, middle, low], axis=0).astype(jnp.bfloat16)
 
 
 def split_dot(values, weights, contract=0):
@@ -146,15 +149,14 @@
 
 
 def split_two(values, axis):
-    high = values.astype(jnp.bfloat16)
-    low = (values - high.astype(jnp.float32)).astype(jnp.bfloat16)
-    return jnp.concatenate([high, low], axis=axis)
+    high = rounded(values)
+    return jnp.concatenate([high, values - high], axis=axis).astype(jnp.bfloat16)
 
 
 LANES = 128
 
 
-KEPT = 1
+KEPT = 2
 
 
 def in_hbm(*arrays):
@@ -184,10 +186,12 @@
     embed_hbm,
     up_hbm,
     down_hbm,
+    proj_hbm,
     pay_ref,
     slope_ref,
     joint_ref,
     keep_ref,
+    proj_ref,
     pos_ref,
     table_ref,
     qkv_ref,
@@ -232,6 +236,12 @@
     other_copy = pltpu.make_async_copy(other_hbm, lat_ref.at[1 - half], sems.at[1])
     embed_copy = pltpu.make_async_copy(embed_hbm, embed_ref, sems.at[2])
     qkv_copy = pltpu.make_async_copy(qkv_hbm, qkv_ref, sems.at[3])
+    chunk = proj_ref.shape[1]
+    flat = lax.axis_index("seq") * n_tp + lax.axis_index("tp")
+    first_column = pl.multiple_of(lax.rem(flat, per_sample) * chunk, chunk)
+    proj_copy = pltpu.make_async_copy(
+        proj_hbm.at[:, pl.ds(first_column, chunk)], proj_ref, sems.at[6 + 2 * steps]
+    )
     pos_copy = pltpu.make_async_copy(pos_hbm, pos_ref, sems.at[4])
     table_copy = pltpu.make_async_copy(table_hbm, table_ref, sems.at[5])
     for copy in (pos_copy, table_copy, own_copy, other_copy, qkv_copy, embed_copy):
@@ -240,6 +250,7 @@
         up_copy(step).start()
     for step in range(steps):
         down_copy(step).start()
+    proj_copy.start()
 
     pos_copy.wait()
     table_copy.wait()
@@ -267,7 +278,7 @@
             target = sample * per_sample + head // heads_dev
             span = slice(head * HEAD_DIM, (head + 1) * HEAD_DIM)
             for kind in range(3):
-                group = 2 + kind * heads_dev + head % heads_dev
+                group = 1 + kind * heads_dev + head % heads_dev
                 values = qkv_ref[kind, sample, :, span]
                 if kind < 2:
                     values = values.astype(jnp.float32)
@@ -305,7 +316,7 @@
         hidden = jnp.dot(lat_rows, joint, preferred_element_type=jnp.float32)
         cdf = 0.5 * (1.0 + lax.erf(hidden * 0.7071067811865476))
         pdf = jnp.exp(-0.5 * hidden * hidden) * 0.3989422804014327
-        slope_ref[:, span] = cdf + hidden * pdf
+        slope_ref[:, span] = (cdf + hidden * pdf).astype(jnp.bfloat16)
         act_sum = jnp.sum((hidden * cdf).reshape(samples, tok_pair, part), axis=1)
         high = act_sum.astype(jnp.bfloat16)
         low = (act_sum - high.astype(jnp.float32)).astype(jnp.bfloat16)
@@ -317,6 +328,7 @@
             down_at(step)[...],
             preferred_element_type=jnp.float32,
         )
+    proj_copy.wait()
     pool = (total[:samples] + total[samples:]) * (1.0 / seq_len)
     side = lax.broadcasted_iota(jnp.int32, (samples, LANES), 1) < LANES // 2
     for plane in range(n_seq // 2):
@@ -329,18 +341,15 @@
                 block = jnp.where(side, first, pltpu.roll(second, LANES // 2, 1))
             else:
                 block = jnp.where(side, pltpu.roll(first, LANES // 2, 1), second)
-            high = block.astype(jnp.bfloat16)
-            low = (block - high.astype(jnp.float32)).astype(jnp.bfloat16)
             for core in range(2):
                 target = (plane * 2 + core) * n_tp + column
-                pay_ref[target, 0] = high
-                pay_ref[target, 1] = low
-
-
-def forward(qkv, positions, own, other, embed_w, up_w, down_w, n_seq, n_tp):
+                pay_ref[target, 0] = block.astype(jnp.bfloat16)
+
+
+def forward(qkv, positions, own, other, embed_w, up_w, down_w, w_proj, n_seq, n_tp):
     samples, tok_dev, width = qkv.shape[1:]
     count = n_seq * n_tp
-    groups = 2 + 3 * (width // HEAD_DIM // (count // samples))
+    groups = 1 + 3 * (width // HEAD_DIM // (count // samples))
     tok_seq, lat = own.shape[1:]
     units, features = (up_w.shape[1] // 2, up_w.shape[0])
     steps = units // 256
@@ -351,12 +360,13 @@
         functools.partial(forward_kernel, (n_seq, n_tp, steps, tok_dev * count)),
         out_shape=(
             jax.ShapeDtypeStruct((count, groups, tok_dev, LANES), jnp.bfloat16),
-            jax.ShapeDtypeStruct((rows, units), jnp.float32),
+            jax.ShapeDtypeStruct((rows, units), jnp.bfloat16),
             jax.ShapeDtypeStruct((2 * lat, units), jnp.bfloat16),
             jax.ShapeDtypeStruct((KEPT * 256, features), jnp.bfloat16),
+            jax.ShapeDtypeStruct((lat, width * samples // count), jnp.bfloat16),
         ),
-        in_specs=[any_spec] * 8,
-        out_specs=(vmem_spec,) * 4,
+        in_specs=[any_spec] * 9,
+        out_specs=(vmem_spec,) * 5,
         scratch_shapes=[
             pltpu.SMEM(positions.shape, jnp.int32),
             pltpu.VMEM((8, LANES), jnp.float32),
@@ -366,14 +376,14 @@
             pltpu.VMEM((steps, features, 256), jnp.bfloat16),
             pltpu.VMEM((units - KEPT * 256, features), jnp.bfloat16),
             pltpu.VMEM((rows, 2 * lat), jnp.bfloat16),
-            pltpu.SemaphoreType.DMA((6 + 2 * steps,)),
+            pltpu.SemaphoreType.DMA((7 + 2 * steps,)),
         ],
         compiler_params=pltpu.CompilerParams(vmem_limit_bytes=32 << 20),
         cost_estimate=pl.CostEstimate(
             flops=4 * features * units * 64, bytes_accessed=4 * features * units, transcendentals=0
         ),
         name="forward",
-    )(*in_hbm(positions, jnp.asarray(lane_frequencies()), qkv, own), other, *in_hbm(embed_w, up_w, down_w))
+    )(*in_hbm(positions, jnp.asarray(lane_frequencies()), qkv, own), other, *in_hbm(embed_w, up_w, down_w, w_proj))
 
 
 def backward_kernel(
@@ -418,7 +428,7 @@
         dact = lax.dot_general(dpool, weights, across, preferred_element_type=jnp.float32)
         dact = dact[:samples] + dact[samples:]
         span = slice(step * part, (step + 1) * part)
-        slope = slope_ref[:, span].reshape(samples, rows, part)
+        slope = slope_ref[:, span].astype(jnp.float32).reshape(samples, rows, part)
         dh1 = (slope * dact[:, None, :]).reshape(samples * rows, part).astype(jnp.bfloat16)
         term = lax.dot_general(dh1, joint_ref[:, span], across, preferred_element_type=jnp.float32)
         dx = term if dx is None else dx + term
@@ -478,24 +488,20 @@
     other = lax.ppermute(latents, both, partner)
     head_pair = in_order(head_w).reshape(2 * rows_dev, classes)
 
-    payload, slope, joint, keep = forward(
-        qkv, positions, latents, other, embed_w, up_w, down_w, n_seq, n_tp
+    payload, slope, joint, keep, proj_mine = forward(
+        qkv, positions, latents, other, embed_w, up_w, down_w, w_proj.T, n_seq, n_tp
     )
     moved = lax.all_to_all(payload, both, 0, 0, tiled=True)
 
-    pooled = jnp.sum(moved[:, :2].astype(jnp.float32), axis=(0, 1))
+    pooled = jnp.sum(moved[:, 0].astype(jnp.float32), axis=0)
     padded = -(-classes // 256) * 256
     terms = jnp.pad(split_dot(pooled, head_pair), ((0, 0), (0, padded - classes)))
     terms = lax.dynamic_slice_in_dim(terms, half * (padded // 2), padded // 2, 1)
-    terms = lax.all_to_all(
-        jnp.broadcast_to(terms.astype(jnp.bfloat16)[None], (count,) + terms.shape),
-        both,
-        0,
-        0,
-        tiled=True,
-    )
-
-    views = moved[:, 2:].reshape(count, 3, heads_dev, tok_dev, HEAD_DIM)
+    terms = jnp.broadcast_to(terms.astype(jnp.bfloat16)[None], (count,) + terms.shape)
+    terms, moved = lax.optimization_barrier((terms, moved))
+    terms = lax.all_to_all(terms, both, 0, 0, tiled=True)
+
+    views = moved[:, 1:].reshape(count, 3, heads_dev, tok_dev, HEAD_DIM)
     views = views.transpose(1, 2, 0, 3, 4).reshape(3, heads_dev, seq_len, HEAD_DIM)
     scores = jnp.einsum(
         "hqd,hkd->hqk", views[0], views[1], preferred_element_type=jnp.float32
@@ -506,12 +512,10 @@
         "hqk,hkd->hqd", weights.astype(jnp.bfloat16), views[2], preferred_element_type=jnp.float32
     )
     attended = (mixed / total[..., None]).astype(jnp.bfloat16)
-    first_row = (seq_index * n_tp + lax.axis_index("tp")) % per_sample * heads_dev * HEAD_DIM
-    proj_mine = lax.dynamic_slice_in_dim(w_proj, first_row, heads_dev * HEAD_DIM, 0)
     eps_terms = jnp.einsum(
-        "hqd,hdl->ql",
+        "hqd,lhd->ql",
         attended,
-        proj_mine.reshape(heads_dev, HEAD_DIM, lat),
+        proj_mine.reshape(lat, heads_dev, HEAD_DIM),
         preferred_element_type=jnp.float32,
     )
     eps_terms = split_two(eps_terms, 1).reshape(count, 1, tok_dev, 2 * lat)

time: 64.9 us -> 65 us (level)
  waiting for transfers between devices: 32.9 us -> 30.3 us
  matrix products: 1.08 us -> 2.66 us
  other arithmetic: 2.3 us -> 3.62 us
  Pallas kernels: 10.2 us -> 9.5 us
    all_to_all x1, waiting for transfers between devices: 7.56 us -> 6.25 us  [per_device_fast(): terms = lax.all_to_all(terms, both, 0, 0, tiled=True)]
    dot_general x2, matrix products: 0.3 us -> 1.2 us  [split_dot(): lax.dot_general(split_rows(values), weights, (((1,), (contract,)), ((), (...]
    another operation x0 -> x4, other arithmetic: none -> 0.78 us
    pallas_call x1, Pallas kernels: 4.61 us -> 3.85 us  [backward(): pl.pallas_call(functools.partial(backward_kernel, steps), out_shape=(jax....]
    dot_general x1, matrix products: 0.39 us -> 1.07 us  [per_device_fast(): jnp.einsum('hqd,lhd->ql', attended, proj_mine.reshape(lat, heads_dev, HEA...]
    all_to_all x1, waiting for transfers between devices: 11.4 us -> 10.8 us  [per_device_fast(): moved = lax.all_to_all(payload, both, 0, 0, tiled=True)]
    mul x1, other arithmetic: 0.05 us -> 0.71 us  [per_device_fast(): scale = GUIDANCE * jnp.sqrt(1.0 - abar)]
  transfers between devices with their start and end apart: 6 -> 6, of which waited for: 6 -> 6; matrix products, arithmetic and copies ran while one was open for 2% -> 4% of each run, Pallas kernels for 0% -> 0%
where the time goes in v6:
time: 65 us; the launch traced here: 64.6 us
  waiting for transfers between devices  30.3 us (47%)
  starting transfers between devices  16.5 us (25%)
  Pallas kernels  9.5 us (15%)
  other arithmetic  3.62 us (6%)
  matrix products  2.66 us (4%)
  local copies, waits for them, and re-layouts  1.91 us (3%)
    all_to_all x1, waiting for transfers between devices, per_device_fast(): moved = lax.all_to_all(payload, both, 0, 0, tiled=True)  10.8 us
    all_to_all x1, starting transfers between devices, per_device_fast(): moved = lax.all_to_all(payload, both, 0, 0, tiled=True)  7.18 us
    all_to_all x1, waiting for transfers between devices, per_device_fast(): lax.all_to_all(jnp.concatenate([eps_terms, share], axis=1), both, 0, 0, t...  6.79 us
    all_to_all x1, waiting for transfers between devices, per_device_fast(): terms = lax.all_to_all(terms, both, 0, 0, tiled=True)  6.25 us
    pallas_call x1, Pallas kernels, forward(): pl.pallas_call(functools.partial(forward_kernel, (n_seq, n_tp, steps, tok...  5.65 us
    all_to_all x1, waiting for transfers between devices, per_device_fast(): lax.all_to_all(dx_terms, both, 0, 0, tiled=True, axis_index_groups=planes)  4.32 us
    pallas_call x1, Pallas kernels, backward(): pl.pallas_call(functools.partial(backward_kernel, steps), out_shape=(jax....  3.85 us
    all_to_all x1, starting transfers between devices, per_device_fast(): lax.all_to_all(dx_terms, both, 0, 0, tiled=True, axis_index_groups=planes)  3.34 us
  transfers between devices with their start and end apart: 6, of which 6 were waited for; matrix products, arithmetic and copies ran while one was open for 4% of the time, Pallas kernels for 0%

profile of v6, /device:TPU:0, one launch (start us, length us, event | category | flops | bytes accessed | tf_op | source)
XLA Modules:
  0.0 64.6 jit_solution(3920133830186894991)
XLA Ops:
  0.0 0.5 collective-permute-start
  0.5 1.0 %collective-permute-done.other_hbm = bf16[4,16,64]{2,1,0:T(8,128)(2,1)S(1)} collective-permute-done((bf16[4,16,64]{2,1,0:T(8,128)(2,1)}, bf16[4,16,64]{2,1,0:T(8,128)(2,1)S(1)}, u32[]{:S(2)}, u32[]{:S(2)}) %collective-permute-start) | collective-permute-done | bytes 8224 | tf_op jit(solution)/shard_map/ppermute | solution.py:488
  1.5 5.6 %forward.1 = (bf16[32,10,4,128]{3,2,1,0:T(4,128)(2,1)}, bf16[128,1024]{1,0:T(8,128)(2,1)S(1)}, bf16[128,1024]{1,0:T(8,128)(2,1)S(1)}, bf16[512,2048]{1,0:T(8,128)(2,1)S(1)}, bf16[64,384]{1,0:T(8,128)(2,1)S(1)}) custom-call(s32[3,4,4]{2,1,0:T(4,128)} %pos_hbm.1, f32[8,128]{1,0:T(8,128)} %constant.48.clone.table_hbm, bf16[3,4,4,3072]{3,2,1,0:T(4,128)(2,1)} %qkv_hbm.1, ...), custom_call_target="tpu_custom_call" | custom-call | flops 536870912 | bytes 8388608 | tf_op jit(solution)/shard_map/forward/pallas_call | solution.py:359
  7.2 7.2 %all-to-all-start = ((bf16[32,10,4,128]{3,2,1,0:T(4,128)(2,1)}), bf16[32,10,4,128]{3,2,1,0:T(4,128)(2,1)S(1)}, u32[]{:S(2)}, u32[]{:S(2)}) async-start(bf16[32,10,4,128]{3,2,1,0:T(4,128)(2,1)} %get-tuple-element.14), calls=%async_computation | async-start | bytes 655360 | tf_op jit(solution)/shard_map/all_to_all | solution.py:494
  14.4 0.3 collective-permute-start.1
  14.7 1.1 %collective-permute-done.1 = bf16[64,1000]{1,0:T(8,128)(2,1)S(1)} collective-permute-done((bf16[64,1000]{1,0:T(8,128)(2,1)S(1)}, bf16[64,1000]{1,0:T(8,128)(2,1)S(1)}, u32[]{:S(2)}, u32[]{:S(2)}) %collective-permute-start.1) | collective-permute-done | bytes 128032 | tf_op jit(solution)/shard_map/ppermute | solution.py:484
  15.9 10.8 %all-to-all-done = bf16[32,10,4,128]{3,2,1,0:T(4,128)(2,1)S(1)} async-done(((bf16[32,10,4,128]{3,2,1,0:T(4,128)(2,1)}), bf16[32,10,4,128]{3,2,1,0:T(4,128)(2,1)S(1)}, u32[]{:S(2)}, u32[]{:S(2)}) %all-to-all-start) | async-done | bytes 327712 | tf_op jit(solution)/shard_map/all_to_all | solution.py:494
  26.9 0.7 %broadcast_in_dim.7 = bf16[32,4,512]{2,1,0:T(4,128)(2,1)} broadcast(bf16[4,512]{1,0:T(4,128)(2,1)S(1)} %fusion.21), dimensions={1,2} | broadcast | bytes 135168 | tf_op jit(solution)/shard_map/broadcast_in_dim | solution.py:500
  27.9 2.6 %all-to-all-start.1 = ((bf16[32,4,512]{2,1,0:T(4,128)(2,1)}), bf16[32,4,512]{2,1,0:T(4,128)(2,1)S(1)}, u32[]{:S(2)}, u32[]{:S(2)}) async-start(bf16[32,4,512]{2,1,0:T(4,128)(2,1)} %broadcast_in_dim.7), calls=%async_computation.1 | async-start | bytes 262144 | tf_op jit(solution)/shard_map/all_to_all | solution.py:502
  30.5 0.2 fusion.34
  30.8 0.5 copy-done.2
  31.3 1.1 %reduce-precision_convert_fusion = (bf16[128,64]{0,1:T(8,128)(2,1)S(1)}, bf16[128,64]{0,1:T(8,128)(2,1)S(1)}) fusion(bf16[3,128,128]{2,1,0:T(8,128)(2,1)S(1)} %bitcast.56, f32[3,128,128]{1,2,0:T(8,128)S(1)} %get-tuple-element.42, f32[3,128]{1,0:T(4,128)S(1)} %fusion.3, f32[3,128]{1,0:T(4,128)} %copy-done.2, bf16[64,384]{1,0:T(8,128)(2,1)S(1)} %get-tuple-element.16), kind=kOutput, calls=%fused_computation.21 | convolution fusion | flops 19103744 | bytes 379904 | tf_op jit(solution)/shard_map/hqd,lhd->ql/dot_general | solution.py:515
  32.6 6.3 %all-to-all-done.1 = bf16[32,4,512]{2,1,0:T(4,128)(2,1)S(1)} async-done(((bf16[32,4,512]{2,1,0:T(4,128)(2,1)}), bf16[32,4,512]{2,1,0:T(4,128)(2,1)S(1)}, u32[]{:S(2)}, u32[]{:S(2)}) %all-to-all-start.1) | async-done | bytes 131104 | tf_op jit(solution)/shard_map/all_to_all | solution.py:502
  39.1 0.2 fusion.20
  39.3 0.7 %reduce-precision_convert_fusion.2 = (bf16[4,1000]{1,0:T(4,128)(2,1)S(1)}, f32[4,1000]{1,0:T(4,128)S(1)}) fusion(f32[4]{0:T(128)S(1)} %fusion.20, f32[4]{0:T(128)S(1)} %slice_reduce_fusion, f32[4,1024]{1,0:T(4,128)S(1)} %bitcast.52, s32[4]{0:T(128)} %param.19), kind=kLoop, calls=%fused_computation.33 | loop fusion | flops 28000 | bytes 40048 | tf_op jit(solution)/shard_map/convert.4
  40.0 1.1 %fusion.13 = f32[12,64]{1,0:T(8,128)S(1)} fusion(bf16[64,1000]{1,0:T(8,128)(2,1)} %param.18, bf16[4,1000]{1,0:T(4,128)(2,1)S(1)} %get-tuple-element.33, bf16[4,1000]{1,0:T(4,128)(2,1)S(1)} %get-tuple-element.32, bf16[4,1000]{1,0:T(4,128)(2,1)S(1)} %get-tuple-element.23), kind=kOutput, calls=%fused_computation.23 | convolution fusion | flops 1608000 | bytes 155072 | tf_op jit(solution)/shard_map/dot_general | solution.py:142
  41.2 0.7 %pad_maximum_fusion.1 = bf16[32,2,4,128]{3,2,1,0:T(4,128)(2,1)} fusion(bf16[32,1,4,128]{3,2,1,0:T(4,128)(2,1)S(1)} %broadcast_in_dim.8, bf16[32,1,4,64]{3,2,1,0:T(4,128)(2,1)S(1)} %bitcast.54, bf16[32,1,4,64]{3,2,1,0:T(4,128)(2,1)S(1)} %bitcast.53), kind=kLoop, calls=%fused_computation.15 | loop fusion | flops 196608 | bytes 131072 | tf_op jit(solution)/shard_map/concatenate | solution.py:531
  41.9 2.6 %all-to-all-start.2 = ((bf16[32,2,4,128]{3,2,1,0:T(4,128)(2,1)}), bf16[32,2,4,128]{3,2,1,0:T(4,128)(2,1)S(1)}, u32[]{:S(2)}, u32[]{:S(2)}) async-start(bf16[32,2,4,128]{3,2,1,0:T(4,128)(2,1)} %pad_maximum_fusion.1), calls=%async_computation.2 | async-start | bytes 131072 | tf_op jit(solution)/shard_map/all_to_all | solution.py:530
  44.5 0.7 %sqrt_multiply_fusion = f32[4]{0:T(128)S(1)} fusion(s32[4]{0:T(128)} %param.20), kind=kLoop, calls=%fused_computation.65 | loop fusion | flops 28 | bytes 32 | tf_op jit(solution)/shard_map/mul | solution.py:549
  45.2 6.8 %all-to-all-done.2.second_ref = bf16[32,2,4,128]{3,2,1,0:T(4,128)(2,1)S(1)} async-done(((bf16[32,2,4,128]{3,2,1,0:T(4,128)(2,1)}), bf16[32,2,4,128]{3,2,1,0:T(4,128)(2,1)S(1)}, u32[]{:S(2)}, u32[]{:S(2)}) %all-to-all-start.2) | async-done | bytes 65568 | tf_op jit(solution)/shard_map/all_to_all | solution.py:530
  52.0 3.8 %backward.1 = (bf16[8,2,4,128]{3,2,1,0:T(4,128)(2,1)}, bf16[8,2048]{1,0:T(8,128)(2,1)S(1)}) custom-call(bf16[32,2,4,128]{3,2,1,0:T(4,128)(2,1)S(1)} %all-to-all-done.2.second_ref, bf16[128,1024]{1,0:T(8,128)(2,1)S(1)} %get-tuple-element.18.slope_ref, bf16[128,1024]{1,0:T(8,128)(2,1)S(1)} %get-tuple-element.19.joint_ref, ...), custom_call_target="tpu_custom_call" | custom-call | tf_op jit(solution)/shard_map/backward/pallas_call | solution.py:451
  55.8 3.3 %all-to-all-start.3 = ((bf16[8,2,4,128]{3,2,1,0:T(4,128)(2,1)}), bf16[8,2,4,128]{3,2,1,0:T(4,128)(2,1)S(1)}, u32[]{:S(2)}, u32[]{:S(2)}) async-start(bf16[8,2,4,128]{3,2,1,0:T(4,128)(2,1)} %get-tuple-element.21), calls=%async_computation.3 | async-start | bytes 32768 | tf_op jit(solution)/shard_map/all_to_all | solution.py:539
  59.5 4.3 %all-to-all-done.3 = bf16[8,2,4,128]{3,2,1,0:T(4,128)(2,1)S(1)} async-done(((bf16[8,2,4,128]{3,2,1,0:T(4,128)(2,1)}), bf16[8,2,4,128]{3,2,1,0:T(4,128)(2,1)S(1)}, u32[]{:S(2)}, u32[]{:S(2)}) %all-to-all-start.3) | async-done | bytes 16416 | tf_op jit(solution)/shard_map/all_to_all | solution.py:539
  63.9 0.7 %subtract_convert_fusion = bf16[4,4,64]{2,1,0:T(4,128)(2,1)} fusion(f32[4,4,64]{2,1,0:T(4,128)S(1)} %slice_add_fusion.2, f32[4,4,64]{2,1,0:T(4,128)S(1)} %bitcast.57, f32[4,64]{1,0:T(4,128)S(1)} %slice_add_fusion.5, f32[4]{0:T(128)S(1)} %sqrt_multiply_fusion), kind=kLoop, calls=%fused_computation.46 | loop fusion | flops 4096 | bytes 11280 | tf_op jit(solution)/shard_map/convert_element_type | solution.py:550
  (32 shorter events, 1.6 us)
Async XLA Ops:
  0.0 1.5 %collective-permute-start = (bf16[4,16,64]{2,1,0:T(8,128)(2,1)}, bf16[4,16,64]{2,1,0:T(8,128)(2,1)S(1)}, u32[]{:S(2)}, u32[]{:S(2)}) collective-permute-start(bf16[4,16,64]{2,1,0:T(8,128)(2,1)} %own_hbm.1), channel_id=1, source_target_pairs={{0,4},{1,5},{2,6},{3,7},{4,0},{5,1},{6,2},{7,3},{8,12},{9,13},{10,... | collective-permute-start | bytes 24584 | tf_op jit(solution)/shard_map/ppermute | solution.py:488
  1.5 12.8 %copy-start.1 = (bf16[64,1000]{1,0:T(8,128)(2,1)S(1)}, bf16[64,1000]{1,0:T(8,128)(2,1)}, u32[]{:S(2)}) copy-start(bf16[64,1000]{1,0:T(8,128)(2,1)} %param.18) | copy-start | bytes 384004
  7.2 19.5 %all-to-all-start = ((bf16[32,10,4,128]{3,2,1,0:T(4,128)(2,1)}), bf16[32,10,4,128]{3,2,1,0:T(4,128)(2,1)S(1)}, u32[]{:S(2)}, u32[]{:S(2)}) async-start(bf16[32,10,4,128]{3,2,1,0:T(4,128)(2,1)} %get-tuple-element.14), calls=%async_computation | async-start | bytes 655360 | tf_op jit(solution)/shard_map/all_to_all | solution.py:494
  14.4 1.4 %collective-permute-start.1 = (bf16[64,1000]{1,0:T(8,128)(2,1)S(1)}, bf16[64,1000]{1,0:T(8,128)(2,1)S(1)}, u32[]{:S(2)}, u32[]{:S(2)}) collective-permute-start(bf16[64,1000]{1,0:T(8,128)(2,1)S(1)} %copy-done.1), channel_id=1, source_target_pairs={{0,4},{1,5},{2,6},{3,7},{4,0},{5,1},{6,2},{7,3},{8,12},{9,13},{10,... | collective-permute-start | bytes 384008 | tf_op jit(solution)/shard_map/ppermute | solution.py:484
  15.8 43.4 %copy-start = (bf16[64,2048]{1,0:T(8,128)(2,1)S(1)}, bf16[64,2048]{1,0:T(8,128)(2,1)}, u32[]{:S(2)}) copy-start(bf16[64,2048]{1,0:T(8,128)(2,1)} %embed_hbm.1) | copy-start | bytes 786436
  27.9 11.0 %all-to-all-start.1 = ((bf16[32,4,512]{2,1,0:T(4,128)(2,1)}), bf16[32,4,512]{2,1,0:T(4,128)(2,1)S(1)}, u32[]{:S(2)}, u32[]{:S(2)}) async-start(bf16[32,4,512]{2,1,0:T(4,128)(2,1)} %broadcast_in_dim.7), calls=%async_computation.1 | async-start | bytes 262144 | tf_op jit(solution)/shard_map/all_to_all | solution.py:502
  30.7 0.6 copy-start.2
  41.9 10.1 %all-to-all-start.2 = ((bf16[32,2,4,128]{3,2,1,0:T(4,128)(2,1)}), bf16[32,2,4,128]{3,2,1,0:T(4,128)(2,1)S(1)}, u32[]{:S(2)}, u32[]{:S(2)}) async-start(bf16[32,2,4,128]{3,2,1,0:T(4,128)(2,1)} %pad_maximum_fusion.1), calls=%async_computation.2 | async-start | bytes 131072 | tf_op jit(solution)/shard_map/all_to_all | solution.py:530
  55.8 8.0 %all-to-all-start.3 = ((bf16[8,2,4,128]{3,2,1,0:T(4,128)(2,1)}), bf16[8,2,4,128]{3,2,1,0:T(4,128)(2,1)S(1)}, u32[]{:S(2)}, u32[]{:S(2)}) async-start(bf16[8,2,4,128]{3,2,1,0:T(4,128)(2,1)} %get-tuple-element.21), calls=%async_computation.3 | async-start | bytes 32768 | tf_op jit(solution)/shard_map/all_to_all | solution.py:539

commit v7 on v6

--- a/solution.py
+++ b/solution.py
@@ -465,6 +465,38 @@
     )(second, slope, joint, keep, *in_hbm(down))
 
 
+def pool_gradient_kernel(dpool_ref, embed_hbm, out_ref, embed_ref, sem):
+    copy = pltpu.make_async_copy(embed_hbm, embed_ref, sem)
+    copy.start()
+    copy.wait()
+    total = lax.dot_general(
+        dpool_ref[...],
+        embed_ref[...],
+        (((1,), (1,)), ((), ())),
+        preferred_element_type=jnp.float32,
+    )
+    half = total.shape[0] // 2
+    out_ref[...] = total[:half] + total[half:]
+
+
+def pool_gradient(dpool, embed_w):
+    vmem_spec = pl.BlockSpec(memory_space=pltpu.VMEM)
+    return pl.pallas_call(
+        pool_gradient_kernel,
+        out_shape=jax.ShapeDtypeStruct((dpool.shape[0] // 2, embed_w.shape[0]), jnp.float32),
+        in_specs=[vmem_spec, pl.BlockSpec(memory_space=pl.ANY)],
+        out_specs=vmem_spec,
+        scratch_shapes=[pltpu.VMEM(embed_w.shape, jnp.bfloat16), pltpu.SemaphoreType.DMA],
+        compiler_params=pltpu.CompilerParams(vmem_limit_bytes=32 << 20),
+        cost_estimate=pl.CostEstimate(
+            flops=2 * dpool.size * embed_w.shape[0],
+            bytes_accessed=2 * embed_w.size,
+            transcendentals=0,
+        ),
+        name="pool_gradient",
+    )(dpool, *in_hbm(embed_w))
+
+
 def per_device_fast(qkv, positions, w_proj, latents, embed_w, up_w, down_w, head_w, labels, timesteps):
     both = ("seq", "tp")
     n_seq, n_tp = (lax.axis_size("seq"), lax.axis_size("tp"))
@@ -498,7 +530,6 @@
     terms = jnp.pad(split_dot(pooled, head_pair), ((0, 0), (0, padded - classes)))
     terms = lax.dynamic_slice_in_dim(terms, half * (padded // 2), padded // 2, 1)
     terms = jnp.broadcast_to(terms.astype(jnp.bfloat16)[None], (count,) + terms.shape)
-    terms, moved = lax.optimization_barrier((terms, moved))
     terms = lax.all_to_all(terms, both, 0, 0, tiled=True)
 
     views = moved[:, 1:].reshape(count, 3, heads_dev, tok_dev, HEAD_DIM)
@@ -540,10 +571,7 @@
     dx = jnp.sum(dx_terms.astype(jnp.float32), axis=0)
     dx = dx.reshape(samples // 2, tok_dev, 2, lat).transpose(0, 2, 1, 3)
     dx = dx.reshape(samples, tok_dev, lat)
-    dx_pool = lax.dot_general(
-        dpool, embed_w, (((1,), (1,)), ((), ())), preferred_element_type=jnp.float32
-    )
-    dx = dx + (dx_pool[:samples] + dx_pool[samples:])[:, None, :]
+    dx = dx + pool_gradient(dpool, embed_w)[:, None, :]
     phase = (timesteps.astype(jnp.float32) / 1000.0 + 0.008) / 1.008 * (jnp.pi / 2)
     abar = jnp.cos(phase) ** 2
     scale = GUIDANCE * jnp.sqrt(1.0 - abar)

time: 65 us -> 63.1 us (0.971)
  matrix products: 2.66 us -> 0.91 us
  other arithmetic: 3.62 us -> 2.3 us
  Pallas kernels: 9.5 us -> 10.7 us
    pallas_call x0 -> x1, Pallas kernels: none -> 1.15 us  [pool_gradient(): pl.pallas_call(pool_gradient_kernel, out_shape=jax.ShapeDtypeStruct((dpoo...]
    all_to_all x1, waiting for transfers between devices: 4.32 us -> 3.37 us  [per_device_fast(): lax.all_to_all(dx_terms, both, 0, 0, tiled=True, axis_index_groups=planes)]
    dot_general x2, matrix products: 1.2 us -> 0.3 us  [split_dot(): lax.dot_general(split_rows(values), weights, (((1,), (contract,)), ((), (...]
    all_to_all x1, waiting for transfers between devices: 6.25 us -> 7.11 us  [per_device_fast(): terms = lax.all_to_all(terms, both, 0, 0, tiled=True)]
    dot_general x1, matrix products: 1.07 us -> 0.39 us  [per_device_fast(): jnp.einsum('hqd,lhd->ql', attended, proj_mine.reshape(lat, heads_dev, HEA...]
    another operation x4, other arithmetic: 0.78 us -> 0.12 us
    mul x1, other arithmetic: 0.71 us -> 0.05 us  [per_device_fast(): scale = GUIDANCE * jnp.sqrt(1.0 - abar)]
  transfers between devices with their start and end apart: 6 -> 6, of which waited for: 6 -> 6; matrix products, arithmetic and copies ran while one was open for 4% -> 2% of each run, Pallas kernels for 0% -> 2%
where the time goes in v7:
time: 63.1 us; the launch traced here: 62.8 us
  waiting for transfers between devices  30.8 us (49%)
  starting transfers between devices  16.5 us (26%)
  Pallas kernels  10.7 us (17%)
  other arithmetic  2.3 us (4%)
  local copies, waits for them, and re-layouts  1.38 us (2%)
  matrix products  0.91 us (1%)
    all_to_all x1, waiting for transfers between devices, per_device_fast(): moved = lax.all_to_all(payload, both, 0, 0, tiled=True)  10.8 us
    all_to_all x1, waiting for transfers between devices, per_device_fast(): lax.all_to_all(jnp.concatenate([eps_terms, share], axis=1), both, 0, 0, t...  7.43 us
    all_to_all x1, starting transfers between devices, per_device_fast(): moved = lax.all_to_all(payload, both, 0, 0, tiled=True)  7.23 us
    all_to_all x1, waiting for transfers between devices, per_device_fast(): terms = lax.all_to_all(terms, both, 0, 0, tiled=True)  7.11 us
    pallas_call x1, Pallas kernels, forward(): pl.pallas_call(functools.partial(forward_kernel, (n_seq, n_tp, steps, tok...  5.66 us
    pallas_call x1, Pallas kernels, backward(): pl.pallas_call(functools.partial(backward_kernel, steps), out_shape=(jax....  3.85 us
    all_to_all x1, waiting for transfers between devices, per_device_fast(): lax.all_to_all(dx_terms, both, 0, 0, tiled=True, axis_index_groups=planes)  3.37 us
    all_to_all x1, starting transfers between devices, per_device_fast(): lax.all_to_all(dx_terms, both, 0, 0, tiled=True, axis_index_groups=planes)  3.34 us
  transfers between devices with their start and end apart: 6, of which 6 were waited for; matrix products, arithmetic and copies ran while one was open for 2% of the time, Pallas kernels for 2%

profile of v7, /device:TPU:0, one launch (start us, length us, event | category | flops | bytes accessed | tf_op | source)
XLA Modules:
  0.0 62.8 jit_solution(7472315931142475530)
XLA Ops:
  0.0 0.5 collective-permute-start
  0.5 1.0 %collective-permute-done.other_hbm = bf16[4,16,64]{2,1,0:T(8,128)(2,1)S(1)} collective-permute-done((bf16[4,16,64]{2,1,0:T(8,128)(2,1)}, bf16[4,16,64]{2,1,0:T(8,128)(2,1)S(1)}, u32[]{:S(2)}, u32[]{:S(2)}) %collective-permute-start) | collective-permute-done | bytes 8224 | tf_op jit(solution)/shard_map/ppermute | solution.py:520
  1.6 5.7 %forward.1 = (bf16[32,10,4,128]{3,2,1,0:T(4,128)(2,1)}, bf16[128,1024]{1,0:T(8,128)(2,1)S(1)}, bf16[128,1024]{1,0:T(8,128)(2,1)S(1)}, bf16[512,2048]{1,0:T(8,128)(2,1)S(1)}, bf16[64,384]{1,0:T(8,128)(2,1)S(1)}) custom-call(s32[3,4,4]{2,1,0:T(4,128)} %pos_hbm.1, f32[8,128]{1,0:T(8,128)} %constant.48.clone.table_hbm, bf16[3,4,4,3072]{3,2,1,0:T(4,128)(2,1)} %qkv_hbm.1, ...), custom_call_target="tpu_custom_call" | custom-call | flops 536870912 | bytes 8388608 | tf_op jit(solution)/shard_map/forward/pallas_call | solution.py:359
  7.2 7.2 %all-to-all-start = ((bf16[32,10,4,128]{3,2,1,0:T(4,128)(2,1)}), bf16[32,10,4,128]{3,2,1,0:T(4,128)(2,1)S(1)}, u32[]{:S(2)}, u32[]{:S(2)}) async-start(bf16[32,10,4,128]{3,2,1,0:T(4,128)(2,1)} %get-tuple-element.12), calls=%async_computation | async-start | bytes 655360 | tf_op jit(solution)/shard_map/all_to_all | solution.py:526
  14.5 0.3 collective-permute-start.1
  14.8 1.1 %collective-permute-done.1 = bf16[64,1000]{1,0:T(8,128)(2,1)S(1)} collective-permute-done((bf16[64,1000]{1,0:T(8,128)(2,1)S(1)}, bf16[64,1000]{1,0:T(8,128)(2,1)S(1)}, u32[]{:S(2)}, u32[]{:S(2)}) %collective-permute-start.1) | collective-permute-done | bytes 128032 | tf_op jit(solution)/shard_map/ppermute | solution.py:516
  15.9 10.8 %all-to-all-done = bf16[32,10,4,128]{3,2,1,0:T(4,128)(2,1)S(1)} async-done(((bf16[32,10,4,128]{3,2,1,0:T(4,128)(2,1)}), bf16[32,10,4,128]{3,2,1,0:T(4,128)(2,1)S(1)}, u32[]{:S(2)}, u32[]{:S(2)}) %all-to-all-start) | async-done | bytes 327712 | tf_op jit(solution)/shard_map/all_to_all | solution.py:526
  26.8 0.1 fusion.22
  27.0 0.7 %broadcast_in_dim.7 = bf16[32,4,512]{2,1,0:T(4,128)(2,1)} broadcast(bf16[4,512]{1,0:T(4,128)(2,1)S(1)} %fusion.21), dimensions={1,2} | broadcast | bytes 135168 | tf_op jit(solution)/shard_map/broadcast_in_dim | solution.py:532
  27.6 2.6 %all-to-all-start.1 = ((bf16[32,4,512]{2,1,0:T(4,128)(2,1)}), bf16[32,4,512]{2,1,0:T(4,128)(2,1)S(1)}, u32[]{:S(2)}, u32[]{:S(2)}) async-start(bf16[32,4,512]{2,1,0:T(4,128)(2,1)} %broadcast_in_dim.7), calls=%async_computation.1 | async-start | bytes 262144 | tf_op jit(solution)/shard_map/all_to_all | solution.py:533
  30.6 0.2 fusion.34
  30.8 0.4 reduce-precision_convert_fusion
  31.5 7.1 %all-to-all-done.1 = bf16[32,4,512]{2,1,0:T(4,128)(2,1)S(1)} async-done(((bf16[32,4,512]{2,1,0:T(4,128)(2,1)}), bf16[32,4,512]{2,1,0:T(4,128)(2,1)S(1)}, u32[]{:S(2)}, u32[]{:S(2)}) %all-to-all-start.1) | async-done | bytes 131104 | tf_op jit(solution)/shard_map/all_to_all | solution.py:533
  38.7 0.1 slice_reduce_fusion
  38.8 0.2 fusion.20
  39.1 0.1 fusion.13
  39.4 0.7 %pad_maximum_fusion.1 = bf16[32,2,4,128]{3,2,1,0:T(4,128)(2,1)} fusion(bf16[32,1,4,128]{3,2,1,0:T(4,128)(2,1)S(1)} %broadcast_in_dim.8, bf16[32,1,4,64]{3,2,1,0:T(4,128)(2,1)S(1)} %bitcast.52, bf16[32,1,4,64]{3,2,1,0:T(4,128)(2,1)S(1)} %bitcast.51), kind=kLoop, calls=%fused_computation.15 | loop fusion | flops 196608 | bytes 131072 | tf_op jit(solution)/shard_map/concatenate | solution.py:562
  40.1 2.6 %all-to-all-start.2 = ((bf16[32,2,4,128]{3,2,1,0:T(4,128)(2,1)}), bf16[32,2,4,128]{3,2,1,0:T(4,128)(2,1)S(1)}, u32[]{:S(2)}, u32[]{:S(2)}) async-start(bf16[32,2,4,128]{3,2,1,0:T(4,128)(2,1)} %pad_maximum_fusion.1), calls=%async_computation.2 | async-start | bytes 131072 | tf_op jit(solution)/shard_map/all_to_all | solution.py:561
  42.7 7.4 %all-to-all-done.2.second_ref = bf16[32,2,4,128]{3,2,1,0:T(4,128)(2,1)S(1)} async-done(((bf16[32,2,4,128]{3,2,1,0:T(4,128)(2,1)}), bf16[32,2,4,128]{3,2,1,0:T(4,128)(2,1)S(1)}, u32[]{:S(2)}, u32[]{:S(2)}) %all-to-all-start.2) | async-done | bytes 65568 | tf_op jit(solution)/shard_map/all_to_all | solution.py:561
  50.1 3.8 %backward.1 = (bf16[8,2,4,128]{3,2,1,0:T(4,128)(2,1)}, bf16[8,2048]{1,0:T(8,128)(2,1)S(1)}) custom-call(bf16[32,2,4,128]{3,2,1,0:T(4,128)(2,1)S(1)} %all-to-all-done.2.second_ref, bf16[128,1024]{1,0:T(8,128)(2,1)S(1)} %get-tuple-element.14.slope_ref, bf16[128,1024]{1,0:T(8,128)(2,1)S(1)} %get-tuple-element.15.joint_ref, ...), custom_call_target="tpu_custom_call" | custom-call | tf_op jit(solution)/shard_map/backward/pallas_call | solution.py:451
  54.0 3.3 %all-to-all-start.3 = ((bf16[8,2,4,128]{3,2,1,0:T(4,128)(2,1)}), bf16[8,2,4,128]{3,2,1,0:T(4,128)(2,1)S(1)}, u32[]{:S(2)}, u32[]{:S(2)}) async-start(bf16[8,2,4,128]{3,2,1,0:T(4,128)(2,1)} %get-tuple-element.17), calls=%async_computation.3 | async-start | bytes 32768 | tf_op jit(solution)/shard_map/all_to_all | solution.py:570
  57.5 1.1 %pool_gradient.1 = f32[4,64]{1,0:T(4,128)S(1)} custom-call(bf16[8,2048]{1,0:T(8,128)(2,1)S(1)} %get-tuple-element.18.dpool_ref, bf16[64,2048]{1,0:T(8,128)(2,1)} %embed_hbm.3), custom_call_target="tpu_custom_call" | custom-call | flops 2097152 | bytes 262144 | tf_op jit(solution)/shard_map/pool_gradient/pallas_call | solution.py:484
  58.6 3.4 %all-to-all-done.3 = bf16[8,2,4,128]{3,2,1,0:T(4,128)(2,1)S(1)} async-done(((bf16[8,2,4,128]{3,2,1,0:T(4,128)(2,1)}), bf16[8,2,4,128]{3,2,1,0:T(4,128)(2,1)S(1)}, u32[]{:S(2)}, u32[]{:S(2)}) %all-to-all-start.3) | async-done | bytes 16416 | tf_op jit(solution)/shard_map/all_to_all | solution.py:570
  62.1 0.7 %subtract_convert_fusion = bf16[4,4,64]{2,1,0:T(4,128)(2,1)} fusion(f32[4,4,64]{2,1,0:T(4,128)S(1)} %slice_add_fusion.2, f32[4,4,64]{2,1,0:T(4,128)S(1)} %bitcast.55, f32[4,64]{1,0:T(4,128)S(1)} %pool_gradient.1, f32[4]{0:T(128)S(1)} %sqrt_multiply_fusion), kind=kLoop, calls=%fused_computation.46 | loop fusion | flops 4096 | bytes 11280 | tf_op jit(solution)/shard_map/convert_element_type | solution.py:578
  (31 shorter events, 1.3 us)
Async XLA Ops:
  0.0 1.5 %collective-permute-start = (bf16[4,16,64]{2,1,0:T(8,128)(2,1)}, bf16[4,16,64]{2,1,0:T(8,128)(2,1)S(1)}, u32[]{:S(2)}, u32[]{:S(2)}) collective-permute-start(bf16[4,16,64]{2,1,0:T(8,128)(2,1)} %own_hbm.1), channel_id=1, source_target_pairs={{0,4},{1,5},{2,6},{3,7},{4,0},{5,1},{6,2},{7,3},{8,12},{9,13},{10,... | collective-permute-start | bytes 24584 | tf_op jit(solution)/shard_map/ppermute | solution.py:520
  1.5 12.9 %copy-start = (bf16[64,1000]{1,0:T(8,128)(2,1)S(1)}, bf16[64,1000]{1,0:T(8,128)(2,1)}, u32[]{:S(2)}) copy-start(bf16[64,1000]{1,0:T(8,128)(2,1)} %param.18) | copy-start | bytes 384004
  1.5 37.4 %copy-start.1 = (s32[4]{0:T(128)S(1)}, s32[4]{0:T(128)}, u32[]{:S(2)}) copy-start(s32[4]{0:T(128)} %param.19) | copy-start | bytes 52
  1.5 41.1 %copy-start.2 = (s32[4]{0:T(128)S(1)}, s32[4]{0:T(128)}, u32[]{:S(2)}) copy-start(s32[4]{0:T(128)} %param.20) | copy-start | bytes 52
  7.2 19.5 %all-to-all-start = ((bf16[32,10,4,128]{3,2,1,0:T(4,128)(2,1)}), bf16[32,10,4,128]{3,2,1,0:T(4,128)(2,1)S(1)}, u32[]{:S(2)}, u32[]{:S(2)}) async-start(bf16[32,10,4,128]{3,2,1,0:T(4,128)(2,1)} %get-tuple-element.12), calls=%async_computation | async-start | bytes 655360 | tf_op jit(solution)/shard_map/all_to_all | solution.py:526
  14.5 1.4 %collective-permute-start.1 = (bf16[64,1000]{1,0:T(8,128)(2,1)S(1)}, bf16[64,1000]{1,0:T(8,128)(2,1)S(1)}, u32[]{:S(2)}, u32[]{:S(2)}) collective-permute-start(bf16[64,1000]{1,0:T(8,128)(2,1)S(1)} %copy-done), channel_id=1, source_target_pairs={{0,4},{1,5},{2,6},{3,7},{4,0},{5,1},{6,2},{7,3},{8,12},{9,13},{10,... | collective-permute-start | bytes 384008 | tf_op jit(solution)/shard_map/ppermute | solution.py:516
  27.6 10.9 %all-to-all-start.1 = ((bf16[32,4,512]{2,1,0:T(4,128)(2,1)}), bf16[32,4,512]{2,1,0:T(4,128)(2,1)S(1)}, u32[]{:S(2)}, u32[]{:S(2)}) async-start(bf16[32,4,512]{2,1,0:T(4,128)(2,1)} %broadcast_in_dim.7), calls=%async_computation.1 | async-start | bytes 262144 | tf_op jit(solution)/shard_map/all_to_all | solution.py:533
  40.1 10.1 %all-to-all-start.2 = ((bf16[32,2,4,128]{3,2,1,0:T(4,128)(2,1)}), bf16[32,2,4,128]{3,2,1,0:T(4,128)(2,1)S(1)}, u32[]{:S(2)}, u32[]{:S(2)}) async-start(bf16[32,2,4,128]{3,2,1,0:T(4,128)(2,1)} %pad_maximum_fusion.1), calls=%async_computation.2 | async-start | bytes 131072 | tf_op jit(solution)/shard_map/all_to_all | solution.py:561
  54.0 8.0 %all-to-all-start.3 = ((bf16[8,2,4,128]{3,2,1,0:T(4,128)(2,1)}), bf16[8,2,4,128]{3,2,1,0:T(4,128)(2,1)S(1)}, u32[]{:S(2)}, u32[]{:S(2)}) async-start(bf16[8,2,4,128]{3,2,1,0:T(4,128)(2,1)} %get-tuple-element.17), calls=%async_computation.3 | async-start | bytes 32768 | tf_op jit(solution)/shard_map/all_to_all | solution.py:570

commit v8 on v7

--- a/solution.py
+++ b/solution.py
@@ -270,8 +270,7 @@
     sine = jnp.sin(angles)
     sine = jnp.where(lane < HEAD_DIM // 2, -sine, sine)
 
-    qkv_copy.wait()
-    for sample in range(samples):
+    def pack(sample):
         cos_rows = cosine[sample * tok_dev : (sample + 1) * tok_dev]
         sin_rows = sine[sample * tok_dev : (sample + 1) * tok_dev]
         for head in range(width // HEAD_DIM):
@@ -285,6 +284,7 @@
                     values = values * cos_rows + pltpu.roll(values, HEAD_DIM // 2, 1) * sin_rows
                 pay_ref[target, group] = values.astype(jnp.bfloat16)
 
+    qkv_copy.wait()
     own_copy.wait()
     other_copy.wait()
     tok_pair = 2 * tok_seq
@@ -304,30 +304,37 @@
     total = jnp.dot(
         jnp.concatenate([lat_high, lat_low], axis=0), embed, preferred_element_type=jnp.float32
     )
-    parts = []
+
+    def activate(first, last):
+        span = slice(first * part, last * part)
+        hidden = jnp.dot(lat_rows, joint_ref[:, span], preferred_element_type=jnp.float32)
+        cdf = 0.5 * (1.0 + lax.erf(hidden * 0.7071067811865476))
+        pdf = jnp.exp(-0.5 * hidden * hidden) * 0.3989422804014327
+        slope_ref[:, span] = (cdf + hidden * pdf).astype(jnp.bfloat16)
+        act_sum = jnp.sum((hidden * cdf).reshape(samples, tok_pair, (last - first) * part), axis=1)
+        high = act_sum.astype(jnp.bfloat16)
+        low = (act_sum - high.astype(jnp.float32)).astype(jnp.bfloat16)
+        return jnp.concatenate([high, low], axis=0)
+
+    packed = 0
     for step in range(steps):
         up_copy(step).wait()
         joint = jnp.dot(embed, up_ref[step], preferred_element_type=jnp.float32)
+        while packed * steps < samples * (step + 1):
+            pack(packed)
+            packed += 1
+        if step == kept:
+            acts = activate(0, kept)
         high = joint.astype(jnp.bfloat16)
         low = (joint - high.astype(jnp.float32)).astype(jnp.bfloat16)
-        joint = jnp.concatenate([high, low], axis=0)
-        span = slice(step * part, (step + 1) * part)
-        joint_ref[:, span] = joint
-        hidden = jnp.dot(lat_rows, joint, preferred_element_type=jnp.float32)
-        cdf = 0.5 * (1.0 + lax.erf(hidden * 0.7071067811865476))
-        pdf = jnp.exp(-0.5 * hidden * hidden) * 0.3989422804014327
-        slope_ref[:, span] = (cdf + hidden * pdf).astype(jnp.bfloat16)
-        act_sum = jnp.sum((hidden * cdf).reshape(samples, tok_pair, part), axis=1)
-        high = act_sum.astype(jnp.bfloat16)
-        low = (act_sum - high.astype(jnp.float32)).astype(jnp.bfloat16)
-        parts.append(jnp.concatenate([high, low], axis=0))
-    for step in range(steps):
+        joint_ref[:, step * part : (step + 1) * part] = jnp.concatenate([high, low], axis=0)
+    for step in range(kept):
         down_copy(step).wait()
-        total = total + jnp.dot(
-            parts[step],
-            down_at(step)[...],
-            preferred_element_type=jnp.float32,
-        )
+    total = total + jnp.dot(acts, keep_ref[...], preferred_element_type=jnp.float32)
+    acts = activate(kept, steps)
+    for step in range(kept, steps):
+        down_copy(step).wait()
+    total = total + jnp.dot(acts, down_ref[...], preferred_element_type=jnp.float32)
     proj_copy.wait()
     pool = (total[:samples] + total[samples:]) * (1.0 / seq_len)
     side = lax.broadcasted_iota(jnp.int32, (samples, LANES), 1) < LANES // 2
@@ -418,20 +425,19 @@
         dpool_ref[:, pair * LANES : (pair + 1) * LANES] = jnp.concatenate([high, low], axis=0)
     dpool = dpool_ref[...]
     across = (((1,), (1,)), ((), ()))
-    dx = None
-    for step in range(steps):
-        if step < kept:
-            weights = keep_ref[step * part : (step + 1) * part]
-        else:
-            down_copy(step).wait()
-            weights = down_ref[(step - kept) * part : (step - kept + 1) * part]
+
+    def dx_part(weights, span):
         dact = lax.dot_general(dpool, weights, across, preferred_element_type=jnp.float32)
         dact = dact[:samples] + dact[samples:]
-        span = slice(step * part, (step + 1) * part)
-        slope = slope_ref[:, span].astype(jnp.float32).reshape(samples, rows, part)
-        dh1 = (slope * dact[:, None, :]).reshape(samples * rows, part).astype(jnp.bfloat16)
-        term = lax.dot_general(dh1, joint_ref[:, span], across, preferred_element_type=jnp.float32)
-        dx = term if dx is None else dx + term
+        size = span.stop - span.start
+        slope = slope_ref[:, span].astype(jnp.float32).reshape(samples, rows, size)
+        dh1 = (slope * dact[:, None, :]).reshape(samples * rows, size).astype(jnp.bfloat16)
+        return lax.dot_general(dh1, joint_ref[:, span], across, preferred_element_type=jnp.float32)
+
+    dx = dx_part(keep_ref[...], slice(0, kept * part))
+    for step in range(kept, steps):
+        down_copy(step).wait()
+    dx = dx + dx_part(down_ref[...], slice(kept * part, steps * part))
     dx = dx + pltpu.roll(dx, LANES // 2, 1)
     side = lax.broadcasted_iota(jnp.int32, (rows, LANES), 1) < LANES // 2
     tok_dev = out_ref.shape[2]

time: 63.1 us -> 62.6 us (level)
  no operation moved by 1% of the time
where the time goes in v8:
time: 62.6 us; the launch traced here: 62.2 us
  waiting for transfers between devices  30.8 us (49%)
  starting transfers between devices  16.5 us (26%)
  Pallas kernels  10.1 us (16%)
  other arithmetic  2.3 us (4%)
  local copies, waits for them, and re-layouts  1.38 us (2%)
  matrix products  0.91 us (1%)
    all_to_all x1, waiting for transfers between devices, per_device_fast(): moved = lax.all_to_all(payload, both, 0, 0, tiled=True)  10.8 us
    all_to_all x1, waiting for transfers between devices, per_device_fast(): lax.all_to_all(jnp.concatenate([eps_terms, share], axis=1), both, 0, 0, t...  7.43 us
    all_to_all x1, starting transfers between devices, per_device_fast(): moved = lax.all_to_all(payload, both, 0, 0, tiled=True)  7.23 us
    all_to_all x1, waiting for transfers between devices, per_device_fast(): terms = lax.all_to_all(terms, both, 0, 0, tiled=True)  7.11 us
    pallas_call x1, Pallas kernels, forward(): pl.pallas_call(functools.partial(forward_kernel, (n_seq, n_tp, steps, tok...  5.15 us
    pallas_call x1, Pallas kernels, backward(): pl.pallas_call(functools.partial(backward_kernel, steps), out_shape=(jax....  3.76 us
    all_to_all x1, waiting for transfers between devices, per_device_fast(): lax.all_to_all(dx_terms, both, 0, 0, tiled=True, axis_index_groups=planes)  3.37 us
    all_to_all x1, starting transfers between devices, per_device_fast(): lax.all_to_all(dx_terms, both, 0, 0, tiled=True, axis_index_groups=planes)  3.34 us
  transfers between devices with their start and end apart: 6, of which 6 were waited for; matrix products, arithmetic and copies ran while one was open for 2% of the time, Pallas kernels for 2%

profile of v8, /device:TPU:0, one launch (start us, length us, event | category | flops | bytes accessed | tf_op | source)
XLA Modules:
  0.0 62.2 jit_solution(18183680804428504591)
XLA Ops:
  0.0 0.5 collective-permute-start
  0.5 1.0 %collective-permute-done.other_hbm = bf16[4,16,64]{2,1,0:T(8,128)(2,1)S(1)} collective-permute-done((bf16[4,16,64]{2,1,0:T(8,128)(2,1)}, bf16[4,16,64]{2,1,0:T(8,128)(2,1)S(1)}, u32[]{:S(2)}, u32[]{:S(2)}) %collective-permute-start) | collective-permute-done | bytes 8224 | tf_op jit(solution)/shard_map/ppermute | solution.py:526
  1.6 5.1 %forward.1 = (bf16[32,10,4,128]{3,2,1,0:T(4,128)(2,1)}, bf16[128,1024]{1,0:T(8,128)(2,1)S(1)}, bf16[128,1024]{1,0:T(8,128)(2,1)S(1)}, bf16[512,2048]{1,0:T(8,128)(2,1)S(1)}, bf16[64,384]{1,0:T(8,128)(2,1)S(1)}) custom-call(s32[3,4,4]{2,1,0:T(4,128)} %pos_hbm.1, f32[8,128]{1,0:T(8,128)} %constant.48.clone.table_hbm, bf16[3,4,4,3072]{3,2,1,0:T(4,128)(2,1)} %qkv_hbm.1, ...), custom_call_target="tpu_custom_call" | custom-call | flops 536870912 | bytes 8388608 | tf_op jit(solution)/shard_map/forward/pallas_call | solution.py:366
  6.7 7.2 %all-to-all-start = ((bf16[32,10,4,128]{3,2,1,0:T(4,128)(2,1)}), bf16[32,10,4,128]{3,2,1,0:T(4,128)(2,1)S(1)}, u32[]{:S(2)}, u32[]{:S(2)}) async-start(bf16[32,10,4,128]{3,2,1,0:T(4,128)(2,1)} %get-tuple-element.12), calls=%async_computation | async-start | bytes 655360 | tf_op jit(solution)/shard_map/all_to_all | solution.py:532
  14.0 0.3 collective-permute-start.1
  14.3 1.1 %collective-permute-done.1 = bf16[64,1000]{1,0:T(8,128)(2,1)S(1)} collective-permute-done((bf16[64,1000]{1,0:T(8,128)(2,1)S(1)}, bf16[64,1000]{1,0:T(8,128)(2,1)S(1)}, u32[]{:S(2)}, u32[]{:S(2)}) %collective-permute-start.1) | collective-permute-done | bytes 128032 | tf_op jit(solution)/shard_map/ppermute | solution.py:522
  15.4 10.8 %all-to-all-done = bf16[32,10,4,128]{3,2,1,0:T(4,128)(2,1)S(1)} async-done(((bf16[32,10,4,128]{3,2,1,0:T(4,128)(2,1)}), bf16[32,10,4,128]{3,2,1,0:T(4,128)(2,1)S(1)}, u32[]{:S(2)}, u32[]{:S(2)}) %all-to-all-start) | async-done | bytes 327712 | tf_op jit(solution)/shard_map/all_to_all | solution.py:532
  26.3 0.1 fusion.22
  26.5 0.7 %broadcast_in_dim.7 = bf16[32,4,512]{2,1,0:T(4,128)(2,1)} broadcast(bf16[4,512]{1,0:T(4,128)(2,1)S(1)} %fusion.21), dimensions={1,2} | broadcast | bytes 135168 | tf_op jit(solution)/shard_map/broadcast_in_dim | solution.py:538
  27.1 2.6 %all-to-all-start.1 = ((bf16[32,4,512]{2,1,0:T(4,128)(2,1)}), bf16[32,4,512]{2,1,0:T(4,128)(2,1)S(1)}, u32[]{:S(2)}, u32[]{:S(2)}) async-start(bf16[32,4,512]{2,1,0:T(4,128)(2,1)} %broadcast_in_dim.7), calls=%async_computation.1 | async-start | bytes 262144 | tf_op jit(solution)/shard_map/all_to_all | solution.py:539
  30.1 0.2 fusion.34
  30.3 0.4 reduce-precision_convert_fusion
  31.0 7.1 %all-to-all-done.1 = bf16[32,4,512]{2,1,0:T(4,128)(2,1)S(1)} async-done(((bf16[32,4,512]{2,1,0:T(4,128)(2,1)}), bf16[32,4,512]{2,1,0:T(4,128)(2,1)S(1)}, u32[]{:S(2)}, u32[]{:S(2)}) %all-to-all-start.1) | async-done | bytes 131104 | tf_op jit(solution)/shard_map/all_to_all | solution.py:539
  38.2 0.1 slice_reduce_fusion
  38.3 0.2 fusion.20
  38.6 0.1 fusion.13
  38.9 0.7 %pad_maximum_fusion.1 = bf16[32,2,4,128]{3,2,1,0:T(4,128)(2,1)} fusion(bf16[32,1,4,128]{3,2,1,0:T(4,128)(2,1)S(1)} %broadcast_in_dim.8, bf16[32,1,4,64]{3,2,1,0:T(4,128)(2,1)S(1)} %bitcast.52, bf16[32,1,4,64]{3,2,1,0:T(4,128)(2,1)S(1)} %bitcast.51), kind=kLoop, calls=%fused_computation.15 | loop fusion | flops 196608 | bytes 131072 | tf_op jit(solution)/shard_map/concatenate | solution.py:568
  39.6 2.6 %all-to-all-start.2 = ((bf16[32,2,4,128]{3,2,1,0:T(4,128)(2,1)}), bf16[32,2,4,128]{3,2,1,0:T(4,128)(2,1)S(1)}, u32[]{:S(2)}, u32[]{:S(2)}) async-start(bf16[32,2,4,128]{3,2,1,0:T(4,128)(2,1)} %pad_maximum_fusion.1), calls=%async_computation.2 | async-start | bytes 131072 | tf_op jit(solution)/shard_map/all_to_all | solution.py:567
  42.2 7.4 %all-to-all-done.2.second_ref = bf16[32,2,4,128]{3,2,1,0:T(4,128)(2,1)S(1)} async-done(((bf16[32,2,4,128]{3,2,1,0:T(4,128)(2,1)}), bf16[32,2,4,128]{3,2,1,0:T(4,128)(2,1)S(1)}, u32[]{:S(2)}, u32[]{:S(2)}) %all-to-all-start.2) | async-done | bytes 65568 | tf_op jit(solution)/shard_map/all_to_all | solution.py:567
  49.6 3.8 %backward.1 = (bf16[8,2,4,128]{3,2,1,0:T(4,128)(2,1)}, bf16[8,2048]{1,0:T(8,128)(2,1)S(1)}) custom-call(bf16[32,2,4,128]{3,2,1,0:T(4,128)(2,1)S(1)} %all-to-all-done.2.second_ref, bf16[128,1024]{1,0:T(8,128)(2,1)S(1)} %get-tuple-element.14.slope_ref, bf16[128,1024]{1,0:T(8,128)(2,1)S(1)} %get-tuple-element.15.joint_ref, ...), custom_call_target="tpu_custom_call" | custom-call | tf_op jit(solution)/shard_map/backward/pallas_call | solution.py:457
  53.4 3.3 %all-to-all-start.3 = ((bf16[8,2,4,128]{3,2,1,0:T(4,128)(2,1)}), bf16[8,2,4,128]{3,2,1,0:T(4,128)(2,1)S(1)}, u32[]{:S(2)}, u32[]{:S(2)}) async-start(bf16[8,2,4,128]{3,2,1,0:T(4,128)(2,1)} %get-tuple-element.17), calls=%async_computation.3 | async-start | bytes 32768 | tf_op jit(solution)/shard_map/all_to_all | solution.py:576
  56.9 1.1 %pool_gradient.1 = f32[4,64]{1,0:T(4,128)S(1)} custom-call(bf16[8,2048]{1,0:T(8,128)(2,1)S(1)} %get-tuple-element.18.dpool_ref, bf16[64,2048]{1,0:T(8,128)(2,1)} %embed_hbm.3), custom_call_target="tpu_custom_call" | custom-call | flops 2097152 | bytes 262144 | tf_op jit(solution)/shard_map/pool_gradient/pallas_call | solution.py:490
  58.0 3.4 %all-to-all-done.3 = bf16[8,2,4,128]{3,2,1,0:T(4,128)(2,1)S(1)} async-done(((bf16[8,2,4,128]{3,2,1,0:T(4,128)(2,1)}), bf16[8,2,4,128]{3,2,1,0:T(4,128)(2,1)S(1)}, u32[]{:S(2)}, u32[]{:S(2)}) %all-to-all-start.3) | async-done | bytes 16416 | tf_op jit(solution)/shard_map/all_to_all | solution.py:576
  61.5 0.7 %subtract_convert_fusion = bf16[4,4,64]{2,1,0:T(4,128)(2,1)} fusion(f32[4,4,64]{2,1,0:T(4,128)S(1)} %slice_add_fusion.2, f32[4,4,64]{2,1,0:T(4,128)S(1)} %bitcast.55, f32[4,64]{1,0:T(4,128)S(1)} %pool_gradient.1, f32[4]{0:T(128)S(1)} %sqrt_multiply_fusion), kind=kLoop, calls=%fused_computation.46 | loop fusion | flops 4096 | bytes 11280 | tf_op jit(solution)/shard_map/convert_element_type | solution.py:584
  (31 shorter events, 1.3 us)
Async XLA Ops:
  0.0 1.5 %collective-permute-start = (bf16[4,16,64]{2,1,0:T(8,128)(2,1)}, bf16[4,16,64]{2,1,0:T(8,128)(2,1)S(1)}, u32[]{:S(2)}, u32[]{:S(2)}) collective-permute-start(bf16[4,16,64]{2,1,0:T(8,128)(2,1)} %own_hbm.1), channel_id=1, source_target_pairs={{0,4},{1,5},{2,6},{3,7},{4,0},{5,1},{6,2},{7,3},{8,12},{9,13},{10,... | collective-permute-start | bytes 24584 | tf_op jit(solution)/shard_map/ppermute | solution.py:526
  1.5 12.4 %copy-start = (bf16[64,1000]{1,0:T(8,128)(2,1)S(1)}, bf16[64,1000]{1,0:T(8,128)(2,1)}, u32[]{:S(2)}) copy-start(bf16[64,1000]{1,0:T(8,128)(2,1)} %param.18) | copy-start | bytes 384004
  1.5 36.9 %copy-start.1 = (s32[4]{0:T(128)S(1)}, s32[4]{0:T(128)}, u32[]{:S(2)}) copy-start(s32[4]{0:T(128)} %param.19) | copy-start | bytes 52
  1.5 40.6 %copy-start.2 = (s32[4]{0:T(128)S(1)}, s32[4]{0:T(128)}, u32[]{:S(2)}) copy-start(s32[4]{0:T(128)} %param.20) | copy-start | bytes 52
  6.7 19.5 %all-to-all-start = ((bf16[32,10,4,128]{3,2,1,0:T(4,128)(2,1)}), bf16[32,10,4,128]{3,2,1,0:T(4,128)(2,1)S(1)}, u32[]{:S(2)}, u32[]{:S(2)}) async-start(bf16[32,10,4,128]{3,2,1,0:T(4,128)(2,1)} %get-tuple-element.12), calls=%async_computation | async-start | bytes 655360 | tf_op jit(solution)/shard_map/all_to_all | solution.py:532
  14.0 1.4 %collective-permute-start.1 = (bf16[64,1000]{1,0:T(8,128)(2,1)S(1)}, bf16[64,1000]{1,0:T(8,128)(2,1)S(1)}, u32[]{:S(2)}, u32[]{:S(2)}) collective-permute-start(bf16[64,1000]{1,0:T(8,128)(2,1)S(1)} %copy-done), channel_id=1, source_target_pairs={{0,4},{1,5},{2,6},{3,7},{4,0},{5,1},{6,2},{7,3},{8,12},{9,13},{10,... | collective-permute-start | bytes 384008 | tf_op jit(solution)/shard_map/ppermute | solution.py:522
  27.1 10.9 %all-to-all-start.1 = ((bf16[32,4,512]{2,1,0:T(4,128)(2,1)}), bf16[32,4,512]{2,1,0:T(4,128)(2,1)S(1)}, u32[]{:S(2)}, u32[]{:S(2)}) async-start(bf16[32,4,512]{2,1,0:T(4,128)(2,1)} %broadcast_in_dim.7), calls=%async_computation.1 | async-start | bytes 262144 | tf_op jit(solution)/shard_map/all_to_all | solution.py:539
  39.6 10.1 %all-to-all-start.2 = ((bf16[32,2,4,128]{3,2,1,0:T(4,128)(2,1)}), bf16[32,2,4,128]{3,2,1,0:T(4,128)(2,1)S(1)}, u32[]{:S(2)}, u32[]{:S(2)}) async-start(bf16[32,2,4,128]{3,2,1,0:T(4,128)(2,1)} %pad_maximum_fusion.1), calls=%async_computation.2 | async-start | bytes 131072 | tf_op jit(solution)/shard_map/all_to_all | solution.py:567
  53.4 8.0 %all-to-all-start.3 = ((bf16[8,2,4,128]{3,2,1,0:T(4,128)(2,1)}), bf16[8,2,4,128]{3,2,1,0:T(4,128)(2,1)S(1)}, u32[]{:S(2)}, u32[]{:S(2)}) async-start(bf16[8,2,4,128]{3,2,1,0:T(4,128)(2,1)} %get-tuple-element.17), calls=%async_computation.3 | async-start | bytes 32768 | tf_op jit(solution)/shard_map/all_to_all | solution.py:576

commit v9 on v8

--- a/solution.py
+++ b/solution.py
@@ -396,7 +396,7 @@
 def backward_kernel(
     steps, second_ref, slope_ref, joint_ref, keep_ref, down_hbm, out_ref, dpool_ref, down_ref, sems
 ):
-    count, groups, samples, _ = second_ref.shape
+    count, samples, _ = second_ref.shape
     units = slope_ref.shape[1]
     part = units // steps
     kept = keep_ref.shape[0] // part
@@ -415,20 +415,15 @@
     rows = slope_ref.shape[0] // samples
     side = lax.broadcasted_iota(jnp.int32, (samples, LANES), 1) < LANES // 2
     for pair in range(count // 2):
-        first = second_ref[2 * pair, groups - 1].astype(jnp.float32)
-        second = second_ref[2 * pair + 1, groups - 1].astype(jnp.float32)
-        first = first + pltpu.roll(first, LANES // 2, 1)
-        second = second + pltpu.roll(second, LANES // 2, 1)
-        block = jnp.where(side, first, second)
-        high = block.astype(jnp.bfloat16)
-        low = (block - high.astype(jnp.float32)).astype(jnp.bfloat16)
-        dpool_ref[:, pair * LANES : (pair + 1) * LANES] = jnp.concatenate([high, low], axis=0)
+        first = second_ref[2 * pair].astype(jnp.float32)
+        second = second_ref[2 * pair + 1].astype(jnp.float32)
+        block = jnp.where(side, pltpu.roll(first, LANES // 2, 1), second)
+        dpool_ref[:, pair * LANES : (pair + 1) * LANES] = block.astype(jnp.bfloat16)
     dpool = dpool_ref[...]
     across = (((1,), (1,)), ((), ()))
 
     def dx_part(weights, span):
         dact = lax.dot_general(dpool, weights, across, preferred_element_type=jnp.float32)
-        dact = dact[:samples] + dact[samples:]
         size = span.stop - span.start
         slope = slope_ref[:, span].astype(jnp.float32).reshape(samples, rows, size)
         dh1 = (slope * dact[:, None, :]).reshape(samples * rows, size).astype(jnp.bfloat16)
@@ -450,7 +445,7 @@
 
 
 def backward(second, slope, joint, keep, down, tok_dev):
-    samples = second.shape[2]
+    samples = second.shape[1]
     targets = slope.shape[0] // samples // tok_dev
     units, steps = (slope.shape[1], slope.shape[1] // 256)
     vmem_spec = pl.BlockSpec(memory_space=pltpu.VMEM)
@@ -458,7 +453,7 @@
         functools.partial(backward_kernel, steps),
         out_shape=(
             jax.ShapeDtypeStruct((targets, samples // 2, tok_dev, LANES), jnp.bfloat16),
-            jax.ShapeDtypeStruct((2 * samples, down.shape[1]), jnp.bfloat16),
+            jax.ShapeDtypeStruct((samples, down.shape[1]), jnp.bfloat16),
         ),
         in_specs=[vmem_spec] * 4 + [pl.BlockSpec(memory_space=pl.ANY)],
         out_specs=(vmem_spec,) * 2,
@@ -475,21 +470,19 @@
     copy = pltpu.make_async_copy(embed_hbm, embed_ref, sem)
     copy.start()
     copy.wait()
-    total = lax.dot_general(
+    out_ref[...] = lax.dot_general(
         dpool_ref[...],
         embed_ref[...],
         (((1,), (1,)), ((), ())),
         preferred_element_type=jnp.float32,
     )
-    half = total.shape[0] // 2
-    out_ref[...] = total[:half] + total[half:]
 
 
 def pool_gradient(dpool, embed_w):
     vmem_spec = pl.BlockSpec(memory_space=pltpu.VMEM)
     return pl.pallas_call(
         pool_gradient_kernel,
-        out_shape=jax.ShapeDtypeStruct((dpool.shape[0] // 2, embed_w.shape[0]), jnp.float32),
+        out_shape=jax.ShapeDtypeStruct((dpool.shape[0], embed_w.shape[0]), jnp.float32),
         in_specs=[vmem_spec, pl.BlockSpec(memory_space=pl.ANY)],
         out_specs=vmem_spec,
         scratch_shapes=[pltpu.VMEM(embed_w.shape, jnp.bfloat16), pltpu.SemaphoreType.DMA],
@@ -555,21 +548,19 @@
         proj_mine.reshape(lat, heads_dev, HEAD_DIM),
         preferred_element_type=jnp.float32,
     )
-    eps_terms = split_two(eps_terms, 1).reshape(count, 1, tok_dev, 2 * lat)
+    eps_terms = eps_terms.reshape(count, tok_dev, lat)
 
     terms = terms.astype(jnp.float32).reshape(n_seq // 2, 2, n_tp, samples, padded // 2)
     logits = jnp.sum(terms, axis=(0, 2))
     logits = logits.transpose(1, 0, 2).reshape(samples, padded)[:, :classes]
     probs = jax.nn.softmax(logits, axis=-1)
     onehot = (labels[:, None] == jnp.arange(classes, dtype=jnp.int32)[None, :]).astype(jnp.float32)
-    share = split_two(split_dot(onehot - probs, head_w, 1), 1)
-    share = jnp.broadcast_to(share[None, None], (count, 1) + share.shape)
-    second = lax.all_to_all(
-        jnp.concatenate([eps_terms, share], axis=1), both, 0, 0, tiled=True
-    )
-    eps = second[:, 0].astype(jnp.float32).reshape(samples, per_sample, tok_dev, 2 * lat)
+    share = split_dot(onehot - probs, head_w, 1)
+    share = jnp.broadcast_to(share[None], (count,) + share.shape)
+    second = jnp.concatenate([eps_terms, share], axis=2).astype(jnp.bfloat16)
+    second = lax.all_to_all(second, both, 0, 0, tiled=True)
+    eps = second[..., :lat].astype(jnp.float32).reshape(samples, per_sample, tok_dev, lat)
     eps = jnp.sum(eps, axis=1)
-    eps = eps[..., :lat] + eps[..., lat:]
     eps = lax.optimization_barrier(eps)
     dx_terms, dpool = backward(second, slope, joint, keep, down_w, tok_dev)
     planes = [[first + k for k in range(2 * n_tp)] for first in range(0, count, 2 * n_tp)]

time: 62.6 us -> 62.2 us (level)
  no operation moved by 1% of the time
where the time goes in v9:
time: 62.2 us; the launch traced here: 61.9 us
  waiting for transfers between devices  30.9 us (50%)
  starting transfers between devices  16.5 us (27%)
  Pallas kernels  10 us (16%)
  other arithmetic  2.14 us (3%)
  local copies, waits for them, and re-layouts  1.13 us (2%)
  matrix products  0.93 us (1%)
    all_to_all x1, waiting for transfers between devices, per_device_fast(): moved = lax.all_to_all(payload, both, 0, 0, tiled=True)  10.8 us
    all_to_all x1, waiting for transfers between devices, per_device_fast(): terms = lax.all_to_all(terms, both, 0, 0, tiled=True)  7.29 us
    all_to_all x1, waiting for transfers between devices, per_device_fast(): second = lax.all_to_all(second, both, 0, 0, tiled=True)  7.24 us
    all_to_all x1, starting transfers between devices, per_device_fast(): moved = lax.all_to_all(payload, both, 0, 0, tiled=True)  7.23 us
    pallas_call x1, Pallas kernels, forward(): pl.pallas_call(functools.partial(forward_kernel, (n_seq, n_tp, steps, tok...  5.15 us
    pallas_call x1, Pallas kernels, backward(): pl.pallas_call(functools.partial(backward_kernel, steps), out_shape=(jax....  3.75 us
    all_to_all x1, waiting for transfers between devices, per_device_fast(): lax.all_to_all(dx_terms, both, 0, 0, tiled=True, axis_index_groups=planes)  3.46 us
    all_to_all x1, starting transfers between devices, per_device_fast(): lax.all_to_all(dx_terms, both, 0, 0, tiled=True, axis_index_groups=planes)  3.35 us
  transfers between devices with their start and end apart: 6, of which 6 were waited for; matrix products, arithmetic and copies ran while one was open for 2% of the time, Pallas kernels for 2%

profile of v9, /device:TPU:0, one launch (start us, length us, event | category | flops | bytes accessed | tf_op | source)
XLA Modules:
  0.0 61.9 jit_solution(6864162246999807458)
XLA Ops:
  0.0 0.5 collective-permute-start
  0.5 1.0 %collective-permute-done.other_hbm = bf16[4,16,64]{2,1,0:T(8,128)(2,1)S(1)} collective-permute-done((bf16[4,16,64]{2,1,0:T(8,128)(2,1)}, bf16[4,16,64]{2,1,0:T(8,128)(2,1)S(1)}, u32[]{:S(2)}, u32[]{:S(2)}) %collective-permute-start) | collective-permute-done | bytes 8224 | tf_op jit(solution)/shard_map/ppermute | solution.py:519
  1.6 5.1 %forward.1 = (bf16[32,10,4,128]{3,2,1,0:T(4,128)(2,1)}, bf16[128,1024]{1,0:T(8,128)(2,1)S(1)}, bf16[128,1024]{1,0:T(8,128)(2,1)S(1)}, bf16[512,2048]{1,0:T(8,128)(2,1)S(1)}, bf16[64,384]{1,0:T(8,128)(2,1)S(1)}) custom-call(s32[3,4,4]{2,1,0:T(4,128)} %pos_hbm.1, f32[8,128]{1,0:T(8,128)} %constant.48.clone.table_hbm, bf16[3,4,4,3072]{3,2,1,0:T(4,128)(2,1)} %qkv_hbm.1, ...), custom_call_target="tpu_custom_call" | custom-call | flops 536870912 | bytes 8388608 | tf_op jit(solution)/shard_map/forward/pallas_call | solution.py:366
  6.7 7.2 %all-to-all-start = ((bf16[32,10,4,128]{3,2,1,0:T(4,128)(2,1)}), bf16[32,10,4,128]{3,2,1,0:T(4,128)(2,1)S(1)}, u32[]{:S(2)}, u32[]{:S(2)}) async-start(bf16[32,10,4,128]{3,2,1,0:T(4,128)(2,1)} %get-tuple-element.12), calls=%async_computation | async-start | bytes 655360 | tf_op jit(solution)/shard_map/all_to_all | solution.py:525
  14.0 0.3 collective-permute-start.1
  14.3 1.1 %collective-permute-done.1 = bf16[64,1000]{1,0:T(8,128)(2,1)S(1)} collective-permute-done((bf16[64,1000]{1,0:T(8,128)(2,1)S(1)}, bf16[64,1000]{1,0:T(8,128)(2,1)S(1)}, u32[]{:S(2)}, u32[]{:S(2)}) %collective-permute-start.1) | collective-permute-done | bytes 128032 | tf_op jit(solution)/shard_map/ppermute | solution.py:515
  15.4 10.8 %all-to-all-done = bf16[32,10,4,128]{3,2,1,0:T(4,128)(2,1)S(1)} async-done(((bf16[32,10,4,128]{3,2,1,0:T(4,128)(2,1)}), bf16[32,10,4,128]{3,2,1,0:T(4,128)(2,1)S(1)}, u32[]{:S(2)}, u32[]{:S(2)}) %all-to-all-start) | async-done | bytes 327712 | tf_op jit(solution)/shard_map/all_to_all | solution.py:525
  26.3 0.1 fusion.17
  26.5 0.7 %broadcast_in_dim.7 = bf16[32,4,512]{2,1,0:T(4,128)(2,1)} broadcast(bf16[4,512]{1,0:T(4,128)(2,1)S(1)} %fusion.16), dimensions={1,2} | broadcast | bytes 135168 | tf_op jit(solution)/shard_map/broadcast_in_dim | solution.py:531
  27.1 2.6 %all-to-all-start.1 = ((bf16[32,4,512]{2,1,0:T(4,128)(2,1)}), bf16[32,4,512]{2,1,0:T(4,128)(2,1)S(1)}, u32[]{:S(2)}, u32[]{:S(2)}) async-start(bf16[32,4,512]{2,1,0:T(4,128)(2,1)} %broadcast_in_dim.7), calls=%async_computation.1 | async-start | bytes 262144 | tf_op jit(solution)/shard_map/all_to_all | solution.py:532
  30.1 0.2 fusion.29
  30.3 0.2 fusion.1
  30.6 0.2 convolution_bitcast_fusion.1
  30.8 7.3 %all-to-all-done.1 = bf16[32,4,512]{2,1,0:T(4,128)(2,1)S(1)} async-done(((bf16[32,4,512]{2,1,0:T(4,128)(2,1)}), bf16[32,4,512]{2,1,0:T(4,128)(2,1)S(1)}, u32[]{:S(2)}, u32[]{:S(2)}) %all-to-all-start.1) | async-done | bytes 131104 | tf_op jit(solution)/shard_map/all_to_all | solution.py:532
  38.3 0.2 fusion.15
  38.6 0.1 fusion.8
  38.8 0.7 %pad_maximum_fusion.1 = bf16[32,4,128]{2,1,0:T(4,128)(2,1)} fusion(bf16[32,4,64]{2,1,0:T(4,128)(2,1)S(1)} %broadcast_in_dim.8, bf16[32,4,64]{2,1,0:T(4,128)(2,1)S(1)} %copy.43), kind=kLoop, calls=%fused_computation.25 | loop fusion | flops 65536 | bytes 65536 | tf_op jit(solution)/shard_map/concatenate | solution.py:560
  39.5 2.6 %all-to-all-start.2 = ((bf16[32,4,128]{2,1,0:T(4,128)(2,1)}), bf16[32,4,128]{2,1,0:T(4,128)(2,1)S(1)}, u32[]{:S(2)}, u32[]{:S(2)}) async-start(bf16[32,4,128]{2,1,0:T(4,128)(2,1)} %pad_maximum_fusion.1), calls=%async_computation.2 | async-start | bytes 65536 | tf_op jit(solution)/shard_map/all_to_all | solution.py:561
  42.1 7.2 %all-to-all-done.2.second_ref = bf16[32,4,128]{2,1,0:T(4,128)(2,1)S(1)} async-done(((bf16[32,4,128]{2,1,0:T(4,128)(2,1)}), bf16[32,4,128]{2,1,0:T(4,128)(2,1)S(1)}, u32[]{:S(2)}, u32[]{:S(2)}) %all-to-all-start.2) | async-done | bytes 32800 | tf_op jit(solution)/shard_map/all_to_all | solution.py:561
  49.3 3.7 %backward.1 = (bf16[8,2,4,128]{3,2,1,0:T(4,128)(2,1)}, bf16[4,2048]{1,0:T(4,128)(2,1)S(1)}) custom-call(bf16[32,4,128]{2,1,0:T(4,128)(2,1)S(1)} %all-to-all-done.2.second_ref, bf16[128,1024]{1,0:T(8,128)(2,1)S(1)} %get-tuple-element.14.slope_ref, bf16[128,1024]{1,0:T(8,128)(2,1)S(1)} %get-tuple-element.15.joint_ref, ...), custom_call_target="tpu_custom_call" | custom-call | tf_op jit(solution)/shard_map/backward/pallas_call | solution.py:452
  53.1 3.3 %all-to-all-start.3 = ((bf16[8,2,4,128]{3,2,1,0:T(4,128)(2,1)}), bf16[8,2,4,128]{3,2,1,0:T(4,128)(2,1)S(1)}, u32[]{:S(2)}, u32[]{:S(2)}) async-start(bf16[8,2,4,128]{3,2,1,0:T(4,128)(2,1)} %get-tuple-element.17), calls=%async_computation.3 | async-start | bytes 32768 | tf_op jit(solution)/shard_map/all_to_all | solution.py:567
  56.5 1.1 %pool_gradient.1 = f32[4,64]{1,0:T(4,128)S(1)} custom-call(bf16[4,2048]{1,0:T(4,128)(2,1)S(1)} %get-tuple-element.18.dpool_ref, bf16[64,2048]{1,0:T(8,128)(2,1)} %embed_hbm.3), custom_call_target="tpu_custom_call" | custom-call | flops 1048576 | bytes 262144 | tf_op jit(solution)/shard_map/pool_gradient/pallas_call | solution.py:483
  57.6 3.5 %all-to-all-done.3 = bf16[8,2,4,128]{3,2,1,0:T(4,128)(2,1)S(1)} async-done(((bf16[8,2,4,128]{3,2,1,0:T(4,128)(2,1)}), bf16[8,2,4,128]{3,2,1,0:T(4,128)(2,1)S(1)}, u32[]{:S(2)}, u32[]{:S(2)}) %all-to-all-start.3) | async-done | bytes 16416 | tf_op jit(solution)/shard_map/all_to_all | solution.py:567
  61.2 0.7 %subtract_convert_fusion = bf16[4,4,64]{2,1,0:T(4,128)(2,1)} fusion(f32[4,4,64]{2,1,0:T(4,128)S(1)} %convert_reduce_fusion.1, f32[4,4,64]{2,1,0:T(4,128)S(1)} %bitcast.57, f32[4,64]{1,0:T(4,128)S(1)} %pool_gradient.1, f32[4]{0:T(128)S(1)} %sqrt_multiply_fusion), kind=kLoop, calls=%fused_computation.42 | loop fusion | flops 4096 | bytes 11280 | tf_op jit(solution)/shard_map/convert_element_type | solution.py:575
  (30 shorter events, 1.0 us)
Async XLA Ops:
  0.0 1.5 %collective-permute-start = (bf16[4,16,64]{2,1,0:T(8,128)(2,1)}, bf16[4,16,64]{2,1,0:T(8,128)(2,1)S(1)}, u32[]{:S(2)}, u32[]{:S(2)}) collective-permute-start(bf16[4,16,64]{2,1,0:T(8,128)(2,1)} %own_hbm.1), channel_id=1, source_target_pairs={{0,4},{1,5},{2,6},{3,7},{4,0},{5,1},{6,2},{7,3},{8,12},{9,13},{10,... | collective-permute-start | bytes 24584 | tf_op jit(solution)/shard_map/ppermute | solution.py:519
  1.5 12.4 %copy-start = (bf16[64,1000]{1,0:T(8,128)(2,1)S(1)}, bf16[64,1000]{1,0:T(8,128)(2,1)}, u32[]{:S(2)}) copy-start(bf16[64,1000]{1,0:T(8,128)(2,1)} %param.18) | copy-start | bytes 384004
  1.5 36.9 %copy-start.1 = (s32[4]{0:T(128)S(1)}, s32[4]{0:T(128)}, u32[]{:S(2)}) copy-start(s32[4]{0:T(128)} %param.19) | copy-start | bytes 52
  1.5 40.5 %copy-start.2 = (s32[4]{0:T(128)S(1)}, s32[4]{0:T(128)}, u32[]{:S(2)}) copy-start(s32[4]{0:T(128)} %param.20) | copy-start | bytes 52
  6.7 19.5 %all-to-all-start = ((bf16[32,10,4,128]{3,2,1,0:T(4,128)(2,1)}), bf16[32,10,4,128]{3,2,1,0:T(4,128)(2,1)S(1)}, u32[]{:S(2)}, u32[]{:S(2)}) async-start(bf16[32,10,4,128]{3,2,1,0:T(4,128)(2,1)} %get-tuple-element.12), calls=%async_computation | async-start | bytes 655360 | tf_op jit(solution)/shard_map/all_to_all | solution.py:525
  14.0 1.4 %collective-permute-start.1 = (bf16[64,1000]{1,0:T(8,128)(2,1)S(1)}, bf16[64,1000]{1,0:T(8,128)(2,1)S(1)}, u32[]{:S(2)}, u32[]{:S(2)}) collective-permute-start(bf16[64,1000]{1,0:T(8,128)(2,1)S(1)} %copy-done), channel_id=1, source_target_pairs={{0,4},{1,5},{2,6},{3,7},{4,0},{5,1},{6,2},{7,3},{8,12},{9,13},{10,... | collective-permute-start | bytes 384008 | tf_op jit(solution)/shard_map/ppermute | solution.py:515
  27.1 11.0 %all-to-all-start.1 = ((bf16[32,4,512]{2,1,0:T(4,128)(2,1)}), bf16[32,4,512]{2,1,0:T(4,128)(2,1)S(1)}, u32[]{:S(2)}, u32[]{:S(2)}) async-start(bf16[32,4,512]{2,1,0:T(4,128)(2,1)} %broadcast_in_dim.7), calls=%async_computation.1 | async-start | bytes 262144 | tf_op jit(solution)/shard_map/all_to_all | solution.py:532
  39.5 9.9 %all-to-all-start.2 = ((bf16[32,4,128]{2,1,0:T(4,128)(2,1)}), bf16[32,4,128]{2,1,0:T(4,128)(2,1)S(1)}, u32[]{:S(2)}, u32[]{:S(2)}) async-start(bf16[32,4,128]{2,1,0:T(4,128)(2,1)} %pad_maximum_fusion.1), calls=%async_computation.2 | async-start | bytes 65536 | tf_op jit(solution)/shard_map/all_to_all | solution.py:561
  53.1 8.0 %all-to-all-start.3 = ((bf16[8,2,4,128]{3,2,1,0:T(4,128)(2,1)}), bf16[8,2,4,128]{3,2,1,0:T(4,128)(2,1)S(1)}, u32[]{:S(2)}, u32[]{:S(2)}) async-start(bf16[8,2,4,128]{3,2,1,0:T(4,128)(2,1)} %get-tuple-element.17), calls=%async_computation.3 | async-start | bytes 32768 | tf_op jit(solution)/shard_map/all_to_all | solution.py:567

commit v10 on v9

--- a/solution.py
+++ b/solution.py
@@ -132,9 +132,7 @@
 
 def split_rows(values):
     high = rounded(values)
-    middle = rounded(values - high)
-    low = values - high - middle
-    return jnp.concatenate([high, middle, low], axis=0).astype(jnp.bfloat16)
+    return jnp.concatenate([high, values - high], axis=0).astype(jnp.bfloat16)
 
 
 def split_dot(values, weights, contract=0):
@@ -145,7 +143,7 @@
         (((1,), (contract,)), ((), ())),
         preferred_element_type=jnp.float32,
     )
-    return product[:rows] + product[rows : 2 * rows] + product[2 * rows :]
+    return product[:rows] + product[rows:]
 
 
 def split_two(values, axis):

time: 62.2 us -> 62.2 us (level)
  no operation moved by 1% of the time
where the time goes in v10:
time: 62.2 us; the launch traced here: 61.9 us
  waiting for transfers between devices  30.9 us (50%)
  starting transfers between devices  16.5 us (27%)
  Pallas kernels  10 us (16%)
  other arithmetic  2.13 us (3%)
  local copies, waits for them, and re-layouts  1.13 us (2%)
  matrix products  0.91 us (1%)
    all_to_all x1, waiting for transfers between devices, per_device_fast(): moved = lax.all_to_all(payload, both, 0, 0, tiled=True)  10.8 us
    all_to_all x1, waiting for transfers between devices, per_device_fast(): terms = lax.all_to_all(terms, both, 0, 0, tiled=True)  7.3 us
    all_to_all x1, waiting for transfers between devices, per_device_fast(): second = lax.all_to_all(second, both, 0, 0, tiled=True)  7.24 us
    all_to_all x1, starting transfers between devices, per_device_fast(): moved = lax.all_to_all(payload, both, 0, 0, tiled=True)  7.23 us
    pallas_call x1, Pallas kernels, forward(): pl.pallas_call(functools.partial(forward_kernel, (n_seq, n_tp, steps, tok...  5.15 us
    pallas_call x1, Pallas kernels, backward(): pl.pallas_call(functools.partial(backward_kernel, steps), out_shape=(jax....  3.75 us
    all_to_all x1, waiting for transfers between devices, per_device_fast(): lax.all_to_all(dx_terms, both, 0, 0, tiled=True, axis_index_groups=planes)  3.46 us
    all_to_all x1, starting transfers between devices, per_device_fast(): lax.all_to_all(dx_terms, both, 0, 0, tiled=True, axis_index_groups=planes)  3.35 us
  transfers between devices with their start and end apart: 6, of which 6 were waited for; matrix products, arithmetic and copies ran while one was open for 2% of the time, Pallas kernels for 2%

profile of v10, /device:TPU:0, one launch (start us, length us, event | category | flops | bytes accessed | tf_op | source)
XLA Modules:
  0.0 61.9 jit_solution(1151267777459769730)
XLA Ops:
  0.0 0.5 collective-permute-start
  0.5 1.0 %collective-permute-done.other_hbm = bf16[4,16,64]{2,1,0:T(8,128)(2,1)S(1)} collective-permute-done((bf16[4,16,64]{2,1,0:T(8,128)(2,1)}, bf16[4,16,64]{2,1,0:T(8,128)(2,1)S(1)}, u32[]{:S(2)}, u32[]{:S(2)}) %collective-permute-start) | collective-permute-done | bytes 8224 | tf_op jit(solution)/shard_map/ppermute | solution.py:517
  1.6 5.1 %forward.1 = (bf16[32,10,4,128]{3,2,1,0:T(4,128)(2,1)}, bf16[128,1024]{1,0:T(8,128)(2,1)S(1)}, bf16[128,1024]{1,0:T(8,128)(2,1)S(1)}, bf16[512,2048]{1,0:T(8,128)(2,1)S(1)}, bf16[64,384]{1,0:T(8,128)(2,1)S(1)}) custom-call(s32[3,4,4]{2,1,0:T(4,128)} %pos_hbm.1, f32[8,128]{1,0:T(8,128)} %constant.48.clone.table_hbm, bf16[3,4,4,3072]{3,2,1,0:T(4,128)(2,1)} %qkv_hbm.1, ...), custom_call_target="tpu_custom_call" | custom-call | flops 536870912 | bytes 8388608 | tf_op jit(solution)/shard_map/forward/pallas_call | solution.py:364
  6.7 7.2 %all-to-all-start = ((bf16[32,10,4,128]{3,2,1,0:T(4,128)(2,1)}), bf16[32,10,4,128]{3,2,1,0:T(4,128)(2,1)S(1)}, u32[]{:S(2)}, u32[]{:S(2)}) async-start(bf16[32,10,4,128]{3,2,1,0:T(4,128)(2,1)} %get-tuple-element.12), calls=%async_computation | async-start | bytes 655360 | tf_op jit(solution)/shard_map/all_to_all | solution.py:523
  14.0 0.3 collective-permute-start.1
  14.3 1.1 %collective-permute-done.1 = bf16[64,1000]{1,0:T(8,128)(2,1)S(1)} collective-permute-done((bf16[64,1000]{1,0:T(8,128)(2,1)S(1)}, bf16[64,1000]{1,0:T(8,128)(2,1)S(1)}, u32[]{:S(2)}, u32[]{:S(2)}) %collective-permute-start.1) | collective-permute-done | bytes 128032 | tf_op jit(solution)/shard_map/ppermute | solution.py:513
  15.4 10.8 %all-to-all-done = bf16[32,10,4,128]{3,2,1,0:T(4,128)(2,1)S(1)} async-done(((bf16[32,10,4,128]{3,2,1,0:T(4,128)(2,1)}), bf16[32,10,4,128]{3,2,1,0:T(4,128)(2,1)S(1)}, u32[]{:S(2)}, u32[]{:S(2)}) %all-to-all-start) | async-done | bytes 327712 | tf_op jit(solution)/shard_map/all_to_all | solution.py:523
  26.3 0.1 fusion.16
  26.4 0.7 %broadcast_in_dim.7 = bf16[32,4,512]{2,1,0:T(4,128)(2,1)} broadcast(bf16[4,512]{1,0:T(4,128)(2,1)S(1)} %fusion.14), dimensions={1,2} | broadcast | bytes 135168 | tf_op jit(solution)/shard_map/broadcast_in_dim | solution.py:529
  27.1 2.6 %all-to-all-start.1 = ((bf16[32,4,512]{2,1,0:T(4,128)(2,1)}), bf16[32,4,512]{2,1,0:T(4,128)(2,1)S(1)}, u32[]{:S(2)}, u32[]{:S(2)}) async-start(bf16[32,4,512]{2,1,0:T(4,128)(2,1)} %broadcast_in_dim.7), calls=%async_computation.1 | async-start | bytes 262144 | tf_op jit(solution)/shard_map/all_to_all | solution.py:530
  30.1 0.2 fusion.24
  30.3 0.2 fusion.1
  30.6 0.2 convolution_bitcast_fusion.1
  30.8 7.3 %all-to-all-done.1 = bf16[32,4,512]{2,1,0:T(4,128)(2,1)S(1)} async-done(((bf16[32,4,512]{2,1,0:T(4,128)(2,1)}), bf16[32,4,512]{2,1,0:T(4,128)(2,1)S(1)}, u32[]{:S(2)}, u32[]{:S(2)}) %all-to-all-start.1) | async-done | bytes 131104 | tf_op jit(solution)/shard_map/all_to_all | solution.py:530
  38.3 0.2 fusion.13
  38.6 0.1 fusion.9
  38.8 0.7 %pad_maximum_fusion.1 = bf16[32,4,128]{2,1,0:T(4,128)(2,1)} fusion(bf16[32,4,64]{2,1,0:T(4,128)(2,1)S(1)} %broadcast_in_dim.8, bf16[32,4,64]{2,1,0:T(4,128)(2,1)S(1)} %copy.43), kind=kLoop, calls=%fused_computation.19 | loop fusion | flops 65536 | bytes 65536 | tf_op jit(solution)/shard_map/concatenate | solution.py:558
  39.4 2.6 %all-to-all-start.2 = ((bf16[32,4,128]{2,1,0:T(4,128)(2,1)}), bf16[32,4,128]{2,1,0:T(4,128)(2,1)S(1)}, u32[]{:S(2)}, u32[]{:S(2)}) async-start(bf16[32,4,128]{2,1,0:T(4,128)(2,1)} %pad_maximum_fusion.1), calls=%async_computation.2 | async-start | bytes 65536 | tf_op jit(solution)/shard_map/all_to_all | solution.py:559
  42.1 7.2 %all-to-all-done.2.second_ref = bf16[32,4,128]{2,1,0:T(4,128)(2,1)S(1)} async-done(((bf16[32,4,128]{2,1,0:T(4,128)(2,1)}), bf16[32,4,128]{2,1,0:T(4,128)(2,1)S(1)}, u32[]{:S(2)}, u32[]{:S(2)}) %all-to-all-start.2) | async-done | bytes 32800 | tf_op jit(solution)/shard_map/all_to_all | solution.py:559
  49.3 3.7 %backward.1 = (bf16[8,2,4,128]{3,2,1,0:T(4,128)(2,1)}, bf16[4,2048]{1,0:T(4,128)(2,1)S(1)}) custom-call(bf16[32,4,128]{2,1,0:T(4,128)(2,1)S(1)} %all-to-all-done.2.second_ref, bf16[128,1024]{1,0:T(8,128)(2,1)S(1)} %get-tuple-element.14.slope_ref, bf16[128,1024]{1,0:T(8,128)(2,1)S(1)} %get-tuple-element.15.joint_ref, ...), custom_call_target="tpu_custom_call" | custom-call | tf_op jit(solution)/shard_map/backward/pallas_call | solution.py:450
  53.1 3.3 %all-to-all-start.3 = ((bf16[8,2,4,128]{3,2,1,0:T(4,128)(2,1)}), bf16[8,2,4,128]{3,2,1,0:T(4,128)(2,1)S(1)}, u32[]{:S(2)}, u32[]{:S(2)}) async-start(bf16[8,2,4,128]{3,2,1,0:T(4,128)(2,1)} %get-tuple-element.17), calls=%async_computation.3 | async-start | bytes 32768 | tf_op jit(solution)/shard_map/all_to_all | solution.py:565
  56.5 1.1 %pool_gradient.1 = f32[4,64]{1,0:T(4,128)S(1)} custom-call(bf16[4,2048]{1,0:T(4,128)(2,1)S(1)} %get-tuple-element.18.dpool_ref, bf16[64,2048]{1,0:T(8,128)(2,1)} %embed_hbm.3), custom_call_target="tpu_custom_call" | custom-call | flops 1048576 | bytes 262144 | tf_op jit(solution)/shard_map/pool_gradient/pallas_call | solution.py:481
  57.6 3.5 %all-to-all-done.3 = bf16[8,2,4,128]{3,2,1,0:T(4,128)(2,1)S(1)} async-done(((bf16[8,2,4,128]{3,2,1,0:T(4,128)(2,1)}), bf16[8,2,4,128]{3,2,1,0:T(4,128)(2,1)S(1)}, u32[]{:S(2)}, u32[]{:S(2)}) %all-to-all-start.3) | async-done | bytes 16416 | tf_op jit(solution)/shard_map/all_to_all | solution.py:565
  61.2 0.7 %subtract_convert_fusion = bf16[4,4,64]{2,1,0:T(4,128)(2,1)} fusion(f32[4,4,64]{2,1,0:T(4,128)S(1)} %convert_reduce_fusion.1, f32[4,4,64]{2,1,0:T(4,128)S(1)} %bitcast.57, f32[4,64]{1,0:T(4,128)S(1)} %pool_gradient.1, f32[4]{0:T(128)S(1)} %sqrt_multiply_fusion), kind=kLoop, calls=%fused_computation.37 | loop fusion | flops 4096 | bytes 11280 | tf_op jit(solution)/shard_map/convert_element_type | solution.py:573
  (30 shorter events, 1.0 us)
Async XLA Ops:
  0.0 1.5 %collective-permute-start = (bf16[4,16,64]{2,1,0:T(8,128)(2,1)}, bf16[4,16,64]{2,1,0:T(8,128)(2,1)S(1)}, u32[]{:S(2)}, u32[]{:S(2)}) collective-permute-start(bf16[4,16,64]{2,1,0:T(8,128)(2,1)} %own_hbm.1), channel_id=1, source_target_pairs={{0,4},{1,5},{2,6},{3,7},{4,0},{5,1},{6,2},{7,3},{8,12},{9,13},{10,... | collective-permute-start | bytes 24584 | tf_op jit(solution)/shard_map/ppermute | solution.py:517
  1.5 12.4 %copy-start = (bf16[64,1000]{1,0:T(8,128)(2,1)S(1)}, bf16[64,1000]{1,0:T(8,128)(2,1)}, u32[]{:S(2)}) copy-start(bf16[64,1000]{1,0:T(8,128)(2,1)} %param.18) | copy-start | bytes 384004
  1.5 36.9 %copy-start.1 = (s32[4]{0:T(128)S(1)}, s32[4]{0:T(128)}, u32[]{:S(2)}) copy-start(s32[4]{0:T(128)} %param.19) | copy-start | bytes 52
  1.5 40.5 %copy-start.2 = (s32[4]{0:T(128)S(1)}, s32[4]{0:T(128)}, u32[]{:S(2)}) copy-start(s32[4]{0:T(128)} %param.20) | copy-start | bytes 52
  6.7 19.5 %all-to-all-start = ((bf16[32,10,4,128]{3,2,1,0:T(4,128)(2,1)}), bf16[32,10,4,128]{3,2,1,0:T(4,128)(2,1)S(1)}, u32[]{:S(2)}, u32[]{:S(2)}) async-start(bf16[32,10,4,128]{3,2,1,0:T(4,128)(2,1)} %get-tuple-element.12), calls=%async_computation | async-start | bytes 655360 | tf_op jit(solution)/shard_map/all_to_all | solution.py:523
  14.0 1.4 %collective-permute-start.1 = (bf16[64,1000]{1,0:T(8,128)(2,1)S(1)}, bf16[64,1000]{1,0:T(8,128)(2,1)S(1)}, u32[]{:S(2)}, u32[]{:S(2)}) collective-permute-start(bf16[64,1000]{1,0:T(8,128)(2,1)S(1)} %copy-done), channel_id=1, source_target_pairs={{0,4},{1,5},{2,6},{3,7},{4,0},{5,1},{6,2},{7,3},{8,12},{9,13},{10,... | collective-permute-start | bytes 384008 | tf_op jit(solution)/shard_map/ppermute | solution.py:513
  27.1 11.0 %all-to-all-start.1 = ((bf16[32,4,512]{2,1,0:T(4,128)(2,1)}), bf16[32,4,512]{2,1,0:T(4,128)(2,1)S(1)}, u32[]{:S(2)}, u32[]{:S(2)}) async-start(bf16[32,4,512]{2,1,0:T(4,128)(2,1)} %broadcast_in_dim.7), calls=%async_computation.1 | async-start | bytes 262144 | tf_op jit(solution)/shard_map/all_to_all | solution.py:530
  39.4 9.9 %all-to-all-start.2 = ((bf16[32,4,128]{2,1,0:T(4,128)(2,1)}), bf16[32,4,128]{2,1,0:T(4,128)(2,1)S(1)}, u32[]{:S(2)}, u32[]{:S(2)}) async-start(bf16[32,4,128]{2,1,0:T(4,128)(2,1)} %pad_maximum_fusion.1), calls=%async_computation.2 | async-start | bytes 65536 | tf_op jit(solution)/shard_map/all_to_all | solution.py:559
  53.1 8.0 %all-to-all-start.3 = ((bf16[8,2,4,128]{3,2,1,0:T(4,128)(2,1)}), bf16[8,2,4,128]{3,2,1,0:T(4,128)(2,1)S(1)}, u32[]{:S(2)}, u32[]{:S(2)}) async-start(bf16[8,2,4,128]{3,2,1,0:T(4,128)(2,1)} %get-tuple-element.17), calls=%async_computation.3 | async-start | bytes 32768 | tf_op jit(solution)/shard_map/all_to_all | solution.py:565

commit v11 on v10

--- a/solution.py
+++ b/solution.py
@@ -242,9 +242,9 @@
     )
     pos_copy = pltpu.make_async_copy(pos_hbm, pos_ref, sems.at[4])
     table_copy = pltpu.make_async_copy(table_hbm, table_ref, sems.at[5])
-    for copy in (pos_copy, table_copy, own_copy, other_copy, qkv_copy, embed_copy):
+    for copy in (pos_copy, table_copy, own_copy, other_copy, embed_copy, up_copy(0), qkv_copy):
         copy.start()
-    for step in range(steps):
+    for step in range(1, steps):
         up_copy(step).start()
     for step in range(steps):
         down_copy(step).start()
@@ -282,7 +282,6 @@
                     values = values * cos_rows + pltpu.roll(values, HEAD_DIM // 2, 1) * sin_rows
                 pay_ref[target, group] = values.astype(jnp.bfloat16)
 
-    qkv_copy.wait()
     own_copy.wait()
     other_copy.wait()
     tok_pair = 2 * tok_seq
@@ -318,6 +317,8 @@
     for step in range(steps):
         up_copy(step).wait()
         joint = jnp.dot(embed, up_ref[step], preferred_element_type=jnp.float32)
+        if step == 0:
+            qkv_copy.wait()
         while packed * steps < samples * (step + 1):
             pack(packed)
             packed += 1

time: 62.2 us -> 62.2 us (level)
  no operation moved by 1% of the time
where the time goes in v11:
time: 62.2 us; the launch traced here: 61.9 us
  waiting for transfers between devices  30.9 us (50%)
  starting transfers between devices  16.5 us (27%)
  Pallas kernels  10.1 us (16%)
  other arithmetic  2.13 us (3%)
  local copies, waits for them, and re-layouts  1.13 us (2%)
  matrix products  0.91 us (1%)
    all_to_all x1, waiting for transfers between devices, per_device_fast(): moved = lax.all_to_all(payload, both, 0, 0, tiled=True)  10.8 us
    all_to_all x1, waiting for transfers between devices, per_device_fast(): terms = lax.all_to_all(terms, both, 0, 0, tiled=True)  7.3 us
    all_to_all x1, waiting for transfers between devices, per_device_fast(): second = lax.all_to_all(second, both, 0, 0, tiled=True)  7.24 us
    all_to_all x1, starting transfers between devices, per_device_fast(): moved = lax.all_to_all(payload, both, 0, 0, tiled=True)  7.22 us
    pallas_call x1, Pallas kernels, forward(): pl.pallas_call(functools.partial(forward_kernel, (n_seq, n_tp, steps, tok...  5.16 us
    pallas_call x1, Pallas kernels, backward(): pl.pallas_call(functools.partial(backward_kernel, steps), out_shape=(jax....  3.75 us
    all_to_all x1, waiting for transfers between devices, per_device_fast(): lax.all_to_all(dx_terms, both, 0, 0, tiled=True, axis_index_groups=planes)  3.46 us
    all_to_all x1, starting transfers between devices, per_device_fast(): lax.all_to_all(dx_terms, both, 0, 0, tiled=True, axis_index_groups=planes)  3.35 us
  transfers between devices with their start and end apart: 6, of which 6 were waited for; matrix products, arithmetic and copies ran while one was open for 2% of the time, Pallas kernels for 2%

profile of v11, /device:TPU:0, one launch (start us, length us, event | category | flops | bytes accessed | tf_op | source)
XLA Modules:
  0.0 61.9 jit_solution(15972966227455719193)
XLA Ops:
  0.0 0.5 collective-permute-start
  0.5 1.0 %collective-permute-done.other_hbm = bf16[4,16,64]{2,1,0:T(8,128)(2,1)S(1)} collective-permute-done((bf16[4,16,64]{2,1,0:T(8,128)(2,1)}, bf16[4,16,64]{2,1,0:T(8,128)(2,1)S(1)}, u32[]{:S(2)}, u32[]{:S(2)}) %collective-permute-start) | collective-permute-done | bytes 8224 | tf_op jit(solution)/shard_map/ppermute | solution.py:518
  1.6 5.2 %forward.1 = (bf16[32,10,4,128]{3,2,1,0:T(4,128)(2,1)}, bf16[128,1024]{1,0:T(8,128)(2,1)S(1)}, bf16[128,1024]{1,0:T(8,128)(2,1)S(1)}, bf16[512,2048]{1,0:T(8,128)(2,1)S(1)}, bf16[64,384]{1,0:T(8,128)(2,1)S(1)}) custom-call(s32[3,4,4]{2,1,0:T(4,128)} %pos_hbm.1, f32[8,128]{1,0:T(8,128)} %constant.48.clone.table_hbm, bf16[3,4,4,3072]{3,2,1,0:T(4,128)(2,1)} %qkv_hbm.1, ...), custom_call_target="tpu_custom_call" | custom-call | flops 536870912 | bytes 8388608 | tf_op jit(solution)/shard_map/forward/pallas_call | solution.py:365
  6.7 7.2 %all-to-all-start = ((bf16[32,10,4,128]{3,2,1,0:T(4,128)(2,1)}), bf16[32,10,4,128]{3,2,1,0:T(4,128)(2,1)S(1)}, u32[]{:S(2)}, u32[]{:S(2)}) async-start(bf16[32,10,4,128]{3,2,1,0:T(4,128)(2,1)} %get-tuple-element.12), calls=%async_computation | async-start | bytes 655360 | tf_op jit(solution)/shard_map/all_to_all | solution.py:524
  14.0 0.3 collective-permute-start.1
  14.3 1.1 %collective-permute-done.1 = bf16[64,1000]{1,0:T(8,128)(2,1)S(1)} collective-permute-done((bf16[64,1000]{1,0:T(8,128)(2,1)S(1)}, bf16[64,1000]{1,0:T(8,128)(2,1)S(1)}, u32[]{:S(2)}, u32[]{:S(2)}) %collective-permute-start.1) | collective-permute-done | bytes 128032 | tf_op jit(solution)/shard_map/ppermute | solution.py:514
  15.4 10.8 %all-to-all-done = bf16[32,10,4,128]{3,2,1,0:T(4,128)(2,1)S(1)} async-done(((bf16[32,10,4,128]{3,2,1,0:T(4,128)(2,1)}), bf16[32,10,4,128]{3,2,1,0:T(4,128)(2,1)S(1)}, u32[]{:S(2)}, u32[]{:S(2)}) %all-to-all-start) | async-done | bytes 327712 | tf_op jit(solution)/shard_map/all_to_all | solution.py:524
  26.3 0.1 fusion.16
  26.5 0.7 %broadcast_in_dim.7 = bf16[32,4,512]{2,1,0:T(4,128)(2,1)} broadcast(bf16[4,512]{1,0:T(4,128)(2,1)S(1)} %fusion.14), dimensions={1,2} | broadcast | bytes 135168 | tf_op jit(solution)/shard_map/broadcast_in_dim | solution.py:530
  27.1 2.6 %all-to-all-start.1 = ((bf16[32,4,512]{2,1,0:T(4,128)(2,1)}), bf16[32,4,512]{2,1,0:T(4,128)(2,1)S(1)}, u32[]{:S(2)}, u32[]{:S(2)}) async-start(bf16[32,4,512]{2,1,0:T(4,128)(2,1)} %broadcast_in_dim.7), calls=%async_computation.1 | async-start | bytes 262144 | tf_op jit(solution)/shard_map/all_to_all | solution.py:531
  30.1 0.2 fusion.24
  30.3 0.2 fusion.1
  30.6 0.2 convolution_bitcast_fusion.1
  30.8 7.3 %all-to-all-done.1 = bf16[32,4,512]{2,1,0:T(4,128)(2,1)S(1)} async-done(((bf16[32,4,512]{2,1,0:T(4,128)(2,1)}), bf16[32,4,512]{2,1,0:T(4,128)(2,1)S(1)}, u32[]{:S(2)}, u32[]{:S(2)}) %all-to-all-start.1) | async-done | bytes 131104 | tf_op jit(solution)/shard_map/all_to_all | solution.py:531
  38.3 0.2 fusion.13
  38.6 0.1 fusion.9
  38.8 0.7 %pad_maximum_fusion.1 = bf16[32,4,128]{2,1,0:T(4,128)(2,1)} fusion(bf16[32,4,64]{2,1,0:T(4,128)(2,1)S(1)} %broadcast_in_dim.8, bf16[32,4,64]{2,1,0:T(4,128)(2,1)S(1)} %copy.43), kind=kLoop, calls=%fused_computation.19 | loop fusion | flops 65536 | bytes 65536 | tf_op jit(solution)/shard_map/concatenate | solution.py:559
  39.5 2.6 %all-to-all-start.2 = ((bf16[32,4,128]{2,1,0:T(4,128)(2,1)}), bf16[32,4,128]{2,1,0:T(4,128)(2,1)S(1)}, u32[]{:S(2)}, u32[]{:S(2)}) async-start(bf16[32,4,128]{2,1,0:T(4,128)(2,1)} %pad_maximum_fusion.1), calls=%async_computation.2 | async-start | bytes 65536 | tf_op jit(solution)/shard_map/all_to_all | solution.py:560
  42.1 7.2 %all-to-all-done.2.second_ref = bf16[32,4,128]{2,1,0:T(4,128)(2,1)S(1)} async-done(((bf16[32,4,128]{2,1,0:T(4,128)(2,1)}), bf16[32,4,128]{2,1,0:T(4,128)(2,1)S(1)}, u32[]{:S(2)}, u32[]{:S(2)}) %all-to-all-start.2) | async-done | bytes 32800 | tf_op jit(solution)/shard_map/all_to_all | solution.py:560
  49.3 3.7 %backward.1 = (bf16[8,2,4,128]{3,2,1,0:T(4,128)(2,1)}, bf16[4,2048]{1,0:T(4,128)(2,1)S(1)}) custom-call(bf16[32,4,128]{2,1,0:T(4,128)(2,1)S(1)} %all-to-all-done.2.second_ref, bf16[128,1024]{1,0:T(8,128)(2,1)S(1)} %get-tuple-element.14.slope_ref, bf16[128,1024]{1,0:T(8,128)(2,1)S(1)} %get-tuple-element.15.joint_ref, ...), custom_call_target="tpu_custom_call" | custom-call | tf_op jit(solution)/shard_map/backward/pallas_call | solution.py:451
  53.1 3.3 %all-to-all-start.3 = ((bf16[8,2,4,128]{3,2,1,0:T(4,128)(2,1)}), bf16[8,2,4,128]{3,2,1,0:T(4,128)(2,1)S(1)}, u32[]{:S(2)}, u32[]{:S(2)}) async-start(bf16[8,2,4,128]{3,2,1,0:T(4,128)(2,1)} %get-tuple-element.17), calls=%async_computation.3 | async-start | bytes 32768 | tf_op jit(solution)/shard_map/all_to_all | solution.py:566
  56.5 1.1 %pool_gradient.1 = f32[4,64]{1,0:T(4,128)S(1)} custom-call(bf16[4,2048]{1,0:T(4,128)(2,1)S(1)} %get-tuple-element.18.dpool_ref, bf16[64,2048]{1,0:T(8,128)(2,1)} %embed_hbm.3), custom_call_target="tpu_custom_call" | custom-call | flops 1048576 | bytes 262144 | tf_op jit(solution)/shard_map/pool_gradient/pallas_call | solution.py:482
  57.6 3.5 %all-to-all-done.3 = bf16[8,2,4,128]{3,2,1,0:T(4,128)(2,1)S(1)} async-done(((bf16[8,2,4,128]{3,2,1,0:T(4,128)(2,1)}), bf16[8,2,4,128]{3,2,1,0:T(4,128)(2,1)S(1)}, u32[]{:S(2)}, u32[]{:S(2)}) %all-to-all-start.3) | async-done | bytes 16416 | tf_op jit(solution)/shard_map/all_to_all | solution.py:566
  61.2 0.7 %subtract_convert_fusion = bf16[4,4,64]{2,1,0:T(4,128)(2,1)} fusion(f32[4,4,64]{2,1,0:T(4,128)S(1)} %convert_reduce_fusion.1, f32[4,4,64]{2,1,0:T(4,128)S(1)} %bitcast.57, f32[4,64]{1,0:T(4,128)S(1)} %pool_gradient.1, f32[4]{0:T(128)S(1)} %sqrt_multiply_fusion), kind=kLoop, calls=%fused_computation.37 | loop fusion | flops 4096 | bytes 11280 | tf_op jit(solution)/shard_map/convert_element_type | solution.py:574
  (30 shorter events, 1.0 us)
Async XLA Ops:
  0.0 1.5 %collective-permute-start = (bf16[4,16,64]{2,1,0:T(8,128)(2,1)}, bf16[4,16,64]{2,1,0:T(8,128)(2,1)S(1)}, u32[]{:S(2)}, u32[]{:S(2)}) collective-permute-start(bf16[4,16,64]{2,1,0:T(8,128)(2,1)} %own_hbm.1), channel_id=1, source_target_pairs={{0,4},{1,5},{2,6},{3,7},{4,0},{5,1},{6,2},{7,3},{8,12},{9,13},{10,... | collective-permute-start | bytes 24584 | tf_op jit(solution)/shard_map/ppermute | solution.py:518
  1.5 12.4 %copy-start = (bf16[64,1000]{1,0:T(8,128)(2,1)S(1)}, bf16[64,1000]{1,0:T(8,128)(2,1)}, u32[]{:S(2)}) copy-start(bf16[64,1000]{1,0:T(8,128)(2,1)} %param.18) | copy-start | bytes 384004
  1.5 36.9 %copy-start.1 = (s32[4]{0:T(128)S(1)}, s32[4]{0:T(128)}, u32[]{:S(2)}) copy-start(s32[4]{0:T(128)} %param.19) | copy-start | bytes 52
  1.5 40.5 %copy-start.2 = (s32[4]{0:T(128)S(1)}, s32[4]{0:T(128)}, u32[]{:S(2)}) copy-start(s32[4]{0:T(128)} %param.20) | copy-start | bytes 52
  6.7 19.5 %all-to-all-start = ((bf16[32,10,4,128]{3,2,1,0:T(4,128)(2,1)}), bf16[32,10,4,128]{3,2,1,0:T(4,128)(2,1)S(1)}, u32[]{:S(2)}, u32[]{:S(2)}) async-start(bf16[32,10,4,128]{3,2,1,0:T(4,128)(2,1)} %get-tuple-element.12), calls=%async_computation | async-start | bytes 655360 | tf_op jit(solution)/shard_map/all_to_all | solution.py:524
  14.0 1.4 %collective-permute-start.1 = (bf16[64,1000]{1,0:T(8,128)(2,1)S(1)}, bf16[64,1000]{1,0:T(8,128)(2,1)S(1)}, u32[]{:S(2)}, u32[]{:S(2)}) collective-permute-start(bf16[64,1000]{1,0:T(8,128)(2,1)S(1)} %copy-done), channel_id=1, source_target_pairs={{0,4},{1,5},{2,6},{3,7},{4,0},{5,1},{6,2},{7,3},{8,12},{9,13},{10,... | collective-permute-start | bytes 384008 | tf_op jit(solution)/shard_map/ppermute | solution.py:514
  27.1 11.0 %all-to-all-start.1 = ((bf16[32,4,512]{2,1,0:T(4,128)(2,1)}), bf16[32,4,512]{2,1,0:T(4,128)(2,1)S(1)}, u32[]{:S(2)}, u32[]{:S(2)}) async-start(bf16[32,4,512]{2,1,0:T(4,128)(2,1)} %broadcast_in_dim.7), calls=%async_computation.1 | async-start | bytes 262144 | tf_op jit(solution)/shard_map/all_to_all | solution.py:531
  39.5 9.9 %all-to-all-start.2 = ((bf16[32,4,128]{2,1,0:T(4,128)(2,1)}), bf16[32,4,128]{2,1,0:T(4,128)(2,1)S(1)}, u32[]{:S(2)}, u32[]{:S(2)}) async-start(bf16[32,4,128]{2,1,0:T(4,128)(2,1)} %pad_maximum_fusion.1), calls=%async_computation.2 | async-start | bytes 65536 | tf_op jit(solution)/shard_map/all_to_all | solution.py:560
  53.1 8.0 %all-to-all-start.3 = ((bf16[8,2,4,128]{3,2,1,0:T(4,128)(2,1)}), bf16[8,2,4,128]{3,2,1,0:T(4,128)(2,1)S(1)}, u32[]{:S(2)}, u32[]{:S(2)}) async-start(bf16[8,2,4,128]{3,2,1,0:T(4,128)(2,1)} %get-tuple-element.17), calls=%async_computation.3 | async-start | bytes 32768 | tf_op jit(solution)/shard_map/all_to_all | solution.py:566
